TPU v7x, 128 devices: a whole 4x4x4 slice. The times are simulated.
128 devices in a mesh: grp: 2 (over z_lo), head: 64 (over y, z_hi, x, core).
Axes of the slice: x: 4, y: 4, z: 4 (z_hi: 2, z_lo: 2; z = z_hi * 2 + z_lo), core: 2. Of those that a mesh axis runs over, the one named last changes fastest.
Arguments:
- query: bfloat16 [72, 256, 8192], P('grp', 'head'), may hold values from -24 to 24
- out_grad: bfloat16 [72, 256, 8192], P('grp', 'head'), may hold values from -6 to 6
- forward_out: bfloat16 [72, 256, 8192], P('grp', 'head'), may hold values from -6 to 6
- key_codes: bfloat16 [4, 256, 8192], P('grp', 'head'), may hold values from -127 to 127, as said below
- key_scale: bfloat16 [4, 256, 64], P('grp', 'head'), may hold values from 0.0039 to 0.0402
- value_codes: bfloat16 [4, 256, 8192], P('grp', 'head'), may hold values from -127 to 127, as said below
- value_scale: bfloat16 [4, 256, 64], P('grp', 'head'), may hold values from 0.0039 to 0.0402
- pairing: int32 [72, 2], replicated, may hold values from 0 to 3, as said below
Outputs:
- grad_query: bfloat16 [72, 256, 8192], P('grp', 'head')
- grad_key: bfloat16 [4, 256, 8192], P('grp', 'head')
- grad_value: bfloat16 [4, 256, 8192], P('grp', 'head')
Inputs may be any that keep to these rules, and one draw needn't show every extreme that they name: `key_codes`: whole numbers. `value_codes`: whole numbers. `pairing`: the two entries of a row differ.
All inputs are finite; a program needn't handle non-finite values.
Results may differ from a plain program's by a relative error of at most 0.012.
The roundings to bfloat16 on the way count: a program that leaves them out, or rounds other values in their place, can miss the bound.
Values may be sent and summed in bfloat16 or wider, within the bound.
No kernel may reach another device: no remote copies, remote signals or barrier semaphores. Data moves between devices by JAX's collectives and lax.ppermute only.
A program may use at most 192 MiB of HBM per device.

v0:
```python
import jax
import jax.numpy as jnp
from jax import lax
from jax.sharding import PartitionSpec as P

HD = 128


def head_dots(first, second):
    head_count = first.shape[-1] // HD
    product = first.astype(jnp.float32) * second.astype(jnp.float32)
    return jnp.sum(product.reshape(first.shape[:-1] + (head_count, HD)), axis=-1)


def dequantize(codes, scales):
    count, length, width = codes.shape
    head_count = scales.shape[2]
    values = (
        codes.astype(jnp.float32).reshape(count, length, head_count, width // head_count)
        * scales.astype(jnp.float32)[..., None]
    )
    return values.reshape(count, length, width).astype(jnp.bfloat16)


def block_scores(query_rows, key_rows):
    return jnp.einsum(
        "rd,kd->rk", query_rows, key_rows, preferred_element_type=jnp.float32
    ) * HD ** (-0.5)


def backward_block(query_rows, grad_rows, dot_rows, key_rows, value_rows, probs):
    rounded = probs.astype(jnp.bfloat16)
    value_grad = jnp.einsum("rk,rd->kd", rounded, grad_rows, preferred_element_type=jnp.float32)
    prob_grad = jnp.einsum("rd,kd->rk", grad_rows, value_rows, preferred_element_type=jnp.float32)
    score_grad = (probs * (prob_grad - dot_rows[:, None]) * HD ** (-0.5)).astype(jnp.bfloat16)
    query_grad = jnp.dot(score_grad, key_rows, preferred_element_type=jnp.float32)
    key_grad = jnp.einsum("rk,rd->kd", score_grad, query_rows, preferred_element_type=jnp.float32)
    return (query_grad, key_grad, value_grad)


def paired_grads(query_block, grad_block, dot_block, key_set, value_set, highest=None, summed=None):
    length = query_block.shape[0]
    step_rows = min(512, length)
    query_parts, key_parts, value_parts = ([], [], [])
    window = slice(0, step_rows)
    scores = block_scores(query_block, key_set)
    row_high = jnp.max(scores, axis=1)
    weights = jnp.exp(scores - row_high[:, None])
    probs = weights / jnp.sum(weights, axis=1)[:, None]
    query_grad, key_grad, value_grad = backward_block(
        query_block, grad_block, dot_block[window, 0], key_set, value_set, probs
    )
    query_parts.append(query_grad)
    key_parts.append(key_grad)
    value_parts.append(value_grad)
    return (query_parts[0], key_parts[0], value_parts[0])


def kv_side(query_heads, grad_heads, dot_heads, key_own, value_own, pairing):
    key_all, value_all = (
        lax.all_gather(key_own, "grp", axis=0, tiled=True),
        lax.all_gather(value_own, "grp", axis=0, tiled=True),
    )
    group_index = lax.axis_index("grp")
    block_count, length, width = query_heads.shape
    key_acc = jnp.zeros(key_all.shape, jnp.float32)
    value_acc = jnp.zeros(value_all.shape, jnp.float32)
    query_out = []
    for block_pos in range(block_count):
        chosen = lax.dynamic_index_in_dim(
            pairing, group_index * block_count + block_pos, 0, keepdims=False
        )
        key_set = jnp.take(key_all, chosen, axis=0).reshape(2 * length, width)
        value_set = jnp.take(value_all, chosen, axis=0).reshape(2 * length, width)
        query_grad, key_grad, value_grad = paired_grads(
            query_heads[block_pos], grad_heads[block_pos], dot_heads[block_pos], key_set, value_set
        )
        query_out.append(query_grad)
        key_acc = key_acc.at[chosen].add(key_grad.reshape(2, length, width))
        value_acc = value_acc.at[chosen].add(value_grad.reshape(2, length, width))
    key_mine, value_mine = (
        lax.psum_scatter(
            key_acc.astype(jnp.bfloat16), "grp", scatter_dimension=0, tiled=True
        ).astype(jnp.float32),
        lax.psum_scatter(
            value_acc.astype(jnp.bfloat16), "grp", scatter_dimension=0, tiled=True
        ).astype(jnp.float32),
    )
    return (
        jnp.stack(query_out).astype(jnp.bfloat16),
        key_mine.astype(jnp.bfloat16),
        value_mine.astype(jnp.bfloat16),
    )


def on_device(
    query, out_grad, forward_out, key_codes, key_scale, value_codes, value_scale, pairing
):
    query_heads, grad_heads, output_heads = (
        lax.all_to_all(query, "head", split_axis=2, concat_axis=1, tiled=True),
        lax.all_to_all(out_grad, "head", split_axis=2, concat_axis=1, tiled=True),
        lax.all_to_all(forward_out, "head", split_axis=2, concat_axis=1, tiled=True),
    )
    dot_heads = head_dots(grad_heads, output_heads)
    key_heads, key_scales, value_heads, value_scales = (
        lax.all_to_all(key_codes, "head", split_axis=2, concat_axis=1, tiled=True),
        lax.all_to_all(key_scale, "head", split_axis=2, concat_axis=1, tiled=True),
        lax.all_to_all(value_codes, "head", split_axis=2, concat_axis=1, tiled=True),
        lax.all_to_all(value_scale, "head", split_axis=2, concat_axis=1, tiled=True),
    )
    key_own = dequantize(key_heads, key_scales)
    value_own = dequantize(value_heads, value_scales)
    query_grad, key_grad, value_grad = kv_side(
        query_heads, grad_heads, dot_heads, key_own, value_own, pairing
    )
    query_tokens = lax.all_to_all(query_grad, "head", split_axis=1, concat_axis=2, tiled=True)
    key_tokens, value_tokens = (
        lax.all_to_all(key_grad, "head", split_axis=1, concat_axis=2, tiled=True),
        lax.all_to_all(value_grad, "head", split_axis=1, concat_axis=2, tiled=True),
    )
    return (query_tokens, key_tokens, value_tokens)


def solution(mesh):
    placed = (
        P("grp", "head", None),
        P("grp", "head", None),
        P("grp", "head", None),
        P("grp", "head", None),
        P("grp", "head", None),
        P("grp", "head", None),
        P("grp", "head", None),
        P(),
    )
    return jax.shard_map(
        on_device,
        mesh=mesh,
        in_specs=placed,
        out_specs=(P("grp", "head", None), P("grp", "head", None), P("grp", "head", None)),
        check_vma=False,
    )
```

profile of v0, /device:TPU:1, one launch (start us, length us, event | category | flops | bytes accessed | tf_op | source)
XLA Modules:
  0.0 985.1 jit_solution(14958056979736004163)
XLA Ops:
  8.6 12.3 %all-to-all-start.1 = ((bf16[2,4,64]{1,0,2:T(2,128)(2,1)}), bf16[2,4,64]{1,0,2:T(2,128)(2,1)S(1)}, u32[]{:S(2)}, u32[]{:S(2)}) async-start(bf16[2,4,64]{1,0,2:T(2,128)(2,1)} %copy.63), calls=%async_computation.1 | async-start | bytes 65536 | tf_op jit(solution)/shard_map/all_to_all | solution.py:107
  71.0 9.5 reshape.3348
  81.2 9.6 copy.71
  90.8 23.3 %reshape.3350 = bf16[64,2,9216]{2,1,0:T(2,128)(2,1)} reshape(bf16[8192,4,36]{2,1,0:T(4,128)(2,1)} %bitcast.1075) | data formatting | bytes 4718592
  114.1 9.6 copy.73
  123.8 23.5 %reshape.3352 = bf16[64,2,9216]{2,1,0:T(2,128)(2,1)} reshape(bf16[8192,4,36]{2,1,0:T(4,128)(2,1)} %bitcast.1076) | data formatting | bytes 4718592
  147.2 9.6 copy.65
  156.9 23.2 %reshape.3356 = bf16[64,2,9216]{2,1,0:T(2,128)(2,1)} reshape(bf16[8192,4,36]{2,1,0:T(4,128)(2,1)} %bitcast.1077) | data formatting | bytes 4718592
  180.0 10.3 %all-to-all-start.4 = ((bf16[2,4,64]{1,0,2:T(2,128)(2,1)}), bf16[2,4,64]{1,0,2:T(2,128)(2,1)S(1)}, u32[]{:S(2)}, u32[]{:S(2)}) async-start(bf16[2,4,64]{1,0,2:T(2,128)(2,1)} %copy.69), calls=%async_computation.4 | async-start | bytes 65536 | tf_op jit(solution)/shard_map/all_to_all | solution.py:109
  204.6 10.0 %all-to-all-done = bf16[64,2,512]{2,1,0:T(2,128)(2,1)S(1)} async-done(((bf16[64,2,512]{2,1,0:T(2,128)(2,1)}), bf16[64,2,512]{2,1,0:T(2,128)(2,1)S(1)}, u32[]{:S(2)}, u32[]{:S(2)}) %all-to-all-start) | async-done | bytes 131104 | tf_op jit(solution)/shard_map/all_to_all | solution.py:106
  219.0 10.0 %reshape.3355 = bf16[8192,2,4]{2,1,0:T(2,128)(2,1)} reshape(bf16[64,2,512]{2,1,0:T(2,128)(2,1)S(1)} %all-to-all-done) | data formatting | bytes 262144
  242.9 11.9 %all-to-all-start.5 = ((bf16[64,2,9216]{2,1,0:T(2,128)(2,1)}), bf16[64,2,9216]{2,1,0:T(2,128)(2,1)S(1)}, u32[]{:S(2)}, u32[]{:S(2)}) async-start(bf16[64,2,9216]{2,1,0:T(2,128)(2,1)} %reshape.3350), calls=%async_computation.5 | async-start | bytes 4718592 | tf_op jit(solution)/shard_map/all_to_all | solution.py:101
  254.8 10.0 %reshape.3349 = bf16[8192,2,4]{2,1,0:T(2,128)(2,1)} reshape(bf16[64,2,512]{2,1,0:T(2,128)(2,1)S(1)} %all-to-all-done.3) | data formatting | bytes 262144
  273.5 11.4 %all_gather.7 = bf16[4,256,128]{2,1,0:T(8,128)(2,1)S(1)} all-gather(bf16[2,256,128]{2,1,0:T(8,128)(2,1)S(1)} %multiply_convert_fusion), channel_id=1, replica_groups=mesh['grp'=2,'head'=64] {'grp'}, dimensions={0}, use_global_device_ids=true | all-gather | bytes 393216 | tf_op jit(solution)/shard_map/all_gather | solution.py:62
  385.1 11.1 %all-to-all-start.6 = ((bf16[64,2,9216]{2,1,0:T(2,128)(2,1)}), bf16[64,2,9216]{2,1,0:T(2,128)(2,1)}, u32[]{:S(2)}, u32[]{:S(2)}) async-start(bf16[64,2,9216]{2,1,0:T(2,128)(2,1)} %reshape.3352), calls=%async_computation.6 | async-start | bytes 4718592 | tf_op jit(solution)/shard_map/all_to_all | solution.py:102
  409.2 20.6 %all-to-all-done.6 = bf16[64,2,9216]{2,1,0:T(2,128)(2,1)} async-done(((bf16[64,2,9216]{2,1,0:T(2,128)(2,1)}), bf16[64,2,9216]{2,1,0:T(2,128)(2,1)}, u32[]{:S(2)}, u32[]{:S(2)}) %all-to-all-start.6) | async-done | bytes 2359328 | tf_op jit(solution)/shard_map/all_to_all | solution.py:102
  446.7 25.0 %reshape.3351 = bf16[8192,4,36]{2,1,0:T(4,128)(2,1)} reshape(bf16[64,2,9216]{2,1,0:T(2,128)(2,1)S(1)} %all-to-all-done.5) | data formatting | bytes 4718592
  471.7 12.1 %copy.72 = bf16[36,4,64,128]{3,1,2,0:T(4,128)(2,1)S(1)} copy(bf16[36,4,64,128]{0,1,3,2:T(4,128)(2,1)} %bitcast.1072) | data formatting | bytes 4718592 | tf_op jit(solution)/shard_map/all_to_all | solution.py:101
  483.8 28.6 %reshape.3353 = bf16[8192,4,36]{2,1,0:T(4,128)(2,1)} reshape(bf16[64,2,9216]{2,1,0:T(2,128)(2,1)} %all-to-all-done.6) | data formatting | bytes 4718592
  512.4 13.7 %copy.74 = f32[36,4,64,128]{3,1,2,0:T(4,128)} copy(bf16[36,4,64,128]{0,1,3,2:T(4,128)(2,1)} %bitcast.1073) | data formatting | bytes 7077888 | tf_op jit(solution)/shard_map/convert_element_type | solution.py:11
  535.4 28.6 %reshape.3357 = bf16[8192,4,36]{2,1,0:T(4,128)(2,1)} reshape(bf16[64,2,9216]{2,1,0:T(2,128)(2,1)} %all-to-all-done.2) | data formatting | bytes 4718592
  564.0 12.4 %copy.66 = bf16[36,4,64,128]{3,1,2,0:T(4,128)(2,1)S(1)} copy(bf16[36,4,64,128]{0,1,3,2:T(4,128)(2,1)} %bitcast.1074) | data formatting | bytes 4718592 | tf_op jit(solution)/shard_map/all_to_all | solution.py:100
  893.8 10.7 %all-to-all-start.8 = ((bf16[2,256,128]{2,0,1:T(2,128)(2,1)}), bf16[2,256,128]{2,0,1:T(2,128)(2,1)S(1)}, u32[]{:S(2)}, u32[]{:S(2)}) async-start(bf16[2,256,128]{2,0,1:T(2,128)(2,1)} %copy.77), calls=%async_computation.9 | async-start | bytes 262144 | tf_op jit(solution)/shard_map/all_to_all | solution.py:118
  934.9 35.2 %all-to-all-done.7 = bf16[36,256,128]{2,0,1:T(8,128)(2,1)S(1)} async-done(((bf16[36,256,128]{2,0,1:T(8,128)(2,1)}), bf16[36,256,128]{2,0,1:T(8,128)(2,1)S(1)}, u32[]{:S(2)}, u32[]{:S(2)}) %all-to-all-start.7) | async-done | bytes 2359328 | tf_op jit(solution)/shard_map/all_to_all | solution.py:116
  (1301 shorter events, 583.9 us)
Async XLA Ops:
  8.6 171.5 %all-to-all-start.1 = ((bf16[2,4,64]{1,0,2:T(2,128)(2,1)}), bf16[2,4,64]{1,0,2:T(2,128)(2,1)S(1)}, u32[]{:S(2)}, u32[]{:S(2)}) async-start(bf16[2,4,64]{1,0,2:T(2,128)(2,1)} %copy.63), calls=%async_computation.1 | async-start | bytes 65536 | tf_op jit(solution)/shard_map/all_to_all | solution.py:107
  90.8 23.3 %copy-start.1 = (bf16[36,4,8192]{2,1,0:T(4,128)(2,1)S(1)}, bf16[36,4,8192]{2,1,0:T(4,128)(2,1)}, u32[]{:S(2)}) copy-start(bf16[36,4,8192]{2,1,0:T(4,128)(2,1)} %param.12) | copy-start | bytes 7077892
  123.8 23.5 %copy-start.2 = (bf16[36,4,8192]{2,1,0:T(4,128)(2,1)S(1)}, bf16[36,4,8192]{2,1,0:T(4,128)(2,1)}, u32[]{:S(2)}) copy-start(bf16[36,4,8192]{2,1,0:T(4,128)(2,1)} %param.10) | copy-start | bytes 7077892
  180.0 19.7 %all-to-all-start.4 = ((bf16[2,4,64]{1,0,2:T(2,128)(2,1)}), bf16[2,4,64]{1,0,2:T(2,128)(2,1)S(1)}, u32[]{:S(2)}, u32[]{:S(2)}) async-start(bf16[2,4,64]{1,0,2:T(2,128)(2,1)} %copy.69), calls=%async_computation.4 | async-start | bytes 65536 | tf_op jit(solution)/shard_map/all_to_all | solution.py:109
  199.7 14.8 %all-to-all-start = ((bf16[64,2,512]{2,1,0:T(2,128)(2,1)}), bf16[64,2,512]{2,1,0:T(2,128)(2,1)S(1)}, u32[]{:S(2)}, u32[]{:S(2)}) async-start(bf16[64,2,512]{2,1,0:T(2,128)(2,1)} %reshape.3354), calls=%async_computation | async-start | bytes 262144 | tf_op jit(solution)/shard_map/all_to_all | solution.py:106
  214.5 28.3 %all-to-all-start.3 = ((bf16[64,2,512]{2,1,0:T(2,128)(2,1)}), bf16[64,2,512]{2,1,0:T(2,128)(2,1)S(1)}, u32[]{:S(2)}, u32[]{:S(2)}) async-start(bf16[64,2,512]{2,1,0:T(2,128)(2,1)} %reshape.3348), calls=%async_computation.3 | async-start | bytes 262144 | tf_op jit(solution)/shard_map/all_to_all | solution.py:108
  242.9 142.2 %all-to-all-start.5 = ((bf16[64,2,9216]{2,1,0:T(2,128)(2,1)}), bf16[64,2,9216]{2,1,0:T(2,128)(2,1)S(1)}, u32[]{:S(2)}, u32[]{:S(2)}) async-start(bf16[64,2,9216]{2,1,0:T(2,128)(2,1)} %reshape.3350), calls=%async_computation.5 | async-start | bytes 4718592 | tf_op jit(solution)/shard_map/all_to_all | solution.py:101
  385.1 18.4 %copy-start.306 = (pred[2]{0:T(512)(128)(4,1)S(1)}, pred[2]{0:T(512)(128)(4,1)}, u32[]{:S(2)}) copy-start(pred[2]{0:T(512)(128)(4,1)} %get-tuple-element.337) | copy-start | bytes 10
  385.1 44.7 %all-to-all-start.6 = ((bf16[64,2,9216]{2,1,0:T(2,128)(2,1)}), bf16[64,2,9216]{2,1,0:T(2,128)(2,1)}, u32[]{:S(2)}, u32[]{:S(2)}) async-start(bf16[64,2,9216]{2,1,0:T(2,128)(2,1)} %reshape.3352), calls=%async_computation.6 | async-start | bytes 4718592 | tf_op jit(solution)/shard_map/all_to_all | solution.py:102
  429.8 105.6 %all-to-all-start.2 = ((bf16[64,2,9216]{2,1,0:T(2,128)(2,1)}), bf16[64,2,9216]{2,1,0:T(2,128)(2,1)}, u32[]{:S(2)}, u32[]{:S(2)}) async-start(bf16[64,2,9216]{2,1,0:T(2,128)(2,1)} %reshape.3356), calls=%async_computation.2 | async-start | bytes 4718592 | tf_op jit(solution)/shard_map/all_to_all | solution.py:100
  434.9 457.2 %reduce-scatter.3.cloned.1.call-start = ((), (), s32[]{:S(2)}) async-start(), calls=%async_computation.12 | async-start | bytes 393216 | tf_op jit(solution)/shard_map/reduce_scatter | solution.py:82
  534.1 46.2 %copy-start.227 = (bf16[1,64,4,128]{3,2,1,0:T(4,128)(2,1)}, bf16[1,64,4,128]{3,2,1,0:T(4,128)(2,1)S(1)}, u32[]{:S(2)}) copy-start(bf16[1,64,4,128]{3,2,1,0:T(4,128)(2,1)S(1)} %get-tuple-element.111) | copy-start | bytes 196612
  579.3 24.8 %copy-start.266 = (f32[1,64,4]{2,1,0:T(8,128)S(1)}, f32[1,64,4]{2,1,0:T(8,128)}, u32[]{:S(2)}) copy-start(f32[1,64,4]{2,1,0:T(8,128)} %get-tuple-element.130) | copy-start | bytes 3076
  579.3 25.4 %copy-start.265 = (f32[1,64,4]{2,1,0:T(8,128)S(1)}, f32[1,64,4]{2,1,0:T(8,128)}, u32[]{:S(2)}) copy-start(f32[1,64,4]{2,1,0:T(8,128)} %get-tuple-element.129) | copy-start | bytes 3076
  579.5 48.5 %copy-start.33 = (bf16[2,256,128]{2,1,0:T(8,128)(2,1)S(1)}, bf16[2,256,128]{2,1,0:T(8,128)(2,1)}, u32[]{:S(2)}) copy-start(bf16[2,256,128]{2,1,0:T(8,128)(2,1)} %get-tuple-element.216) | copy-start | bytes 393220
  580.5 49.5 %copy-start.32 = (bf16[2,256,128]{2,1,0:T(8,128)(2,1)S(1)}, bf16[2,256,128]{2,1,0:T(8,128)(2,1)}, u32[]{:S(2)}) copy-start(bf16[2,256,128]{2,1,0:T(8,128)(2,1)} %get-tuple-element.214) | copy-start | bytes 393220
  580.5 49.5 %copy-start.114 = (bf16[1,64,4,128]{3,2,1,0:T(4,128)(2,1)S(1)}, bf16[1,64,4,128]{3,2,1,0:T(4,128)(2,1)}, u32[]{:S(2)}) copy-start(bf16[1,64,4,128]{3,2,1,0:T(4,128)(2,1)} %get-tuple-element.92) | copy-start | bytes 196612
  605.4 25.8 %copy-start.31 = (bf16[2,256,128]{2,1,0:T(8,128)(2,1)S(1)}, bf16[2,256,128]{2,1,0:T(8,128)(2,1)}, u32[]{:S(2)}) copy-start(bf16[2,256,128]{2,1,0:T(8,128)(2,1)} %get-tuple-element.212) | copy-start | bytes 393220
  605.4 25.8 %copy-start.112 = (bf16[1,64,4,128]{3,2,1,0:T(4,128)(2,1)S(1)}, bf16[1,64,4,128]{3,2,1,0:T(4,128)(2,1)}, u32[]{:S(2)}) copy-start(bf16[1,64,4,128]{3,2,1,0:T(4,128)(2,1)} %get-tuple-element.91) | copy-start | bytes 196612
  785.5 119.4 %reduce-scatter.5.cloned.1.call-start = ((), (), s32[]{:S(2)}) async-start(), calls=%async_computation.13 | async-start | bytes 393216 | tf_op jit(solution)/shard_map/reduce_scatter | solution.py:85
  887.0 31.8 %copy-start.71 = (bf16[512,256]{1,0:T(8,128)(2,1)S(1)}, bf16[512,256]{1,0:T(8,128)(2,1)}, u32[]{:S(2)}) copy-start(bf16[512,256]{1,0:T(8,128)(2,1)} %copy-done.70) | copy-start | bytes 786436
  893.8 20.6 %all-to-all-start.8 = ((bf16[2,256,128]{2,0,1:T(2,128)(2,1)}), bf16[2,256,128]{2,0,1:T(2,128)(2,1)S(1)}, u32[]{:S(2)}, u32[]{:S(2)}) async-start(bf16[2,256,128]{2,0,1:T(2,128)(2,1)} %copy.77), calls=%async_computation.9 | async-start | bytes 262144 | tf_op jit(solution)/shard_map/all_to_all | solution.py:118
  914.4 14.6 %all-to-all-start.9 = ((bf16[2,256,128]{2,0,1:T(2,128)(2,1)}), bf16[2,256,128]{2,0,1:T(2,128)(2,1)S(1)}, u32[]{:S(2)}, u32[]{:S(2)}) async-start(bf16[2,256,128]{2,0,1:T(2,128)(2,1)} %copy.79), calls=%async_computation.11 | async-start | bytes 262144 | tf_op jit(solution)/shard_map/all_to_all | solution.py:119
  929.0 41.1 %all-to-all-start.7 = ((bf16[36,256,128]{2,0,1:T(8,128)(2,1)}), bf16[36,256,128]{2,0,1:T(8,128)(2,1)S(1)}, u32[]{:S(2)}, u32[]{:S(2)}) async-start(bf16[36,256,128]{2,0,1:T(8,128)(2,1)} %copy.75), calls=%async_computation.7 | async-start | bytes 5242880 | tf_op jit(solution)/shard_map/all_to_all | solution.py:116
  (332 other events, 1737.8 us)
Sparse Core Ops, SparseCore 0:
  785.7 15.2 reduce-scatter.2
  889.7 15.2 reduce-scatter.4
where the time goes:
time: 1000 us; the launch traced here: 985 us
  local copies, waits for them, and re-layouts  451 us (45%)
  other arithmetic  225 us (22%)
  matrix products  104 us (10%)
  waiting for transfers between devices  89.7 us (9%)
  starting transfers between devices  79.6 us (8%)
  between operations  19 us (2%)
  blocking collectives  16.6 us (2%)
    unnamed x705, local copies, waits for them, and re-layouts  240 us
    scatter-add x36, other arithmetic, kv_side(): value_acc = value_acc.at[chosen].add(value_grad.reshape(2, length, width))  61.8 us
    scatter-add x36, other arithmetic, kv_side(): key_acc = key_acc.at[chosen].add(key_grad.reshape(2, length, width))  60.1 us
    sub x36, local copies, waits for them, and re-layouts, backward_block(): prob_grad - dot_rows[:, None]  46.9 us
    gather x36, local copies, waits for them, and re-layouts, kv_side(): value_set = jnp.take(value_all, chosen, axis=0).reshape(2 * length, width)  42.3 us
    select_n x54, other arithmetic, kv_side(): key_set = jnp.take(key_all, chosen, axis=0).reshape(2 * length, width)  42.1 us
    gather x36, local copies, waits for them, and re-layouts, kv_side(): key_set = jnp.take(key_all, chosen, axis=0).reshape(2 * length, width)  39.7 us
    dot_general x36, matrix products, backward_block(): jnp.einsum('rk,rd->kd', rounded, grad_rows, preferred_element_type=jnp.fl...  37.8 us
  transfers between devices with their start and end apart: 12, of which 7 were waited for; matrix products, arithmetic and copies ran while one was open for 53% of the time, Pallas kernels for 0%

commit v1 on v0

v1 whole, which is shorter than its diff:
```python
import jax
import jax.numpy as jnp
from jax import lax
from jax.experimental import pallas as pl
from jax.experimental.pallas import tpu as pltpu
from jax.sharding import PartitionSpec as P

HD = 128
SCALE = HD ** (-0.5)
LOG2E = 1.4426950408889634
PIECE = 32


def params(mib=56):
    return pltpu.CompilerParams(vmem_limit_bytes=mib << 20)


def pack(query, out_grad, forward_out, first, count, step, kv=None):
    _, toks, width = query.shape
    heads = width // HD
    blocks = kv[0].shape[0] if kv else 0
    slots = 2 * count + 1 + 2 * blocks
    steps = count // step
    start = first // step

    def body(*refs):
        q_ref, g_ref, f_ref = refs[:3]
        kv_refs = refs[3 : 3 + (4 if kv else 0)]
        out_ref = refs[3 + len(kv_refs)]
        dots, dots_out = refs[4 + len(kv_refs) : 6 + len(kv_refs)]
        kv_out = refs[6 + len(kv_refs)] if kv else None
        sems = refs[-1]
        at = pl.program_id(0)

        @pl.when(at == 0)
        def _():
            dots[...] = jnp.zeros_like(dots)
            if kv:
                for which in range(2):
                    codes, scales = kv_refs[2 * which], kv_refs[2 * which + 1]
                    factor = scales[...].astype(jnp.float32)
                    for h in range(heads):
                        part = codes[:, :, h * HD : (h + 1) * HD].astype(jnp.float32)
                        rows = part * factor[:, :, h : h + 1]
                        kv_out[h, which * blocks : (which + 1) * blocks] = rows.astype(jnp.bfloat16)

        for h in range(heads):
            pltpu.make_async_copy(
                q_ref.at[:, :, pl.ds(h * HD, HD)], out_ref.at[h, pl.ds(at * step, step)], sems.at[0]
            ).start()
            pltpu.make_async_copy(
                g_ref.at[:, :, pl.ds(h * HD, HD)],
                out_ref.at[h, pl.ds(count + at * step, step)],
                sems.at[1],
            ).start()
        lane = lax.broadcasted_iota(jnp.int32, (step, toks, HD), 2)
        place = lax.broadcasted_iota(jnp.int32, (step, toks, HD), 0) + at * step
        chosen = lane == place
        for h in range(heads):
            cut = slice(h * HD, (h + 1) * HD)
            product = g_ref[:, :, cut].astype(jnp.float32) * f_ref[:, :, cut].astype(jnp.float32)
            total = jnp.sum(product, axis=-1, keepdims=True)
            dots[h] += jnp.sum(jnp.where(chosen, total, 0.0), axis=0)

        @pl.when(at == steps - 1)
        def _():
            for h in range(heads):
                value = dots[h]
                high = value.astype(jnp.bfloat16).astype(jnp.float32)
                middle = (value - high).astype(jnp.bfloat16).astype(jnp.float32)
                low = (value - high - middle).astype(jnp.bfloat16).astype(jnp.float32)
                spread = high + pltpu.roll(middle, PIECE, 1) + pltpu.roll(low, 2 * PIECE, 1)
                dots_out[h, 0] = spread.astype(jnp.bfloat16)
            copies = [
                pltpu.make_async_copy(dots_out, out_ref.at[:, pl.ds(2 * count, 1)], sems.at[2])
            ]
            if kv:
                copies.append(
                    pltpu.make_async_copy(
                        kv_out, out_ref.at[:, pl.ds(2 * count + 1, 2 * blocks)], sems.at[3]
                    )
                )
            for copy in copies:
                copy.start()
            for copy in copies:
                copy.wait()

        pltpu.make_async_copy(q_ref, q_ref, sems.at[0]).wait()
        pltpu.make_async_copy(g_ref, g_ref, sems.at[1]).wait()

    rows = pl.BlockSpec((step, toks, width), lambda i: (start + i, 0, 0))
    in_specs = [rows] * 3
    args = [query, out_grad, forward_out]
    scratch = [
        pltpu.VMEM((heads, toks, HD), jnp.float32),
        pltpu.VMEM((heads, 1, toks, HD), jnp.bfloat16),
    ]
    if kv:
        in_specs += [pl.BlockSpec(x.shape, lambda i: (0, 0, 0)) for x in kv]
        args += list(kv)
        scratch.append(pltpu.VMEM((heads, 2 * blocks, toks, HD), jnp.bfloat16))
    scratch.append(pltpu.SemaphoreType.DMA((4,)))
    return pl.pallas_call(
        body,
        name=f"pack{first}",
        grid=(steps,),
        in_specs=in_specs,
        out_specs=pl.BlockSpec(memory_space=pl.ANY),
        out_shape=jax.ShapeDtypeStruct((heads, slots, toks, HD), jnp.bfloat16),
        scratch_shapes=scratch,
        compiler_params=params(),
    )(*args)


def nt(a, b):
    return lax.dot_general(a, b, (((1,), (1,)), ((), ())), preferred_element_type=jnp.float32)


def nn(a, b):
    return jnp.dot(a, b, preferred_element_type=jnp.float32)


def attend(pairs, message, kv_own, kv_other, first, count, sums=None, extra=0):
    srcs, slots, toks, _ = message.shape
    length = srcs * toks
    blocks = kv_own.shape[1] // 2
    total = 2 * blocks
    last = sums is not None

    def body(pair_ref, m_ref, own_ref, other_ref, *refs):
        if last:
            sum_ref, out_ref, own_sum, other_sum = refs[:4]
            keys, keys_t, values, dots, key_acc, value_acc = refs[4:]
        else:
            out_ref, sum_out = refs[:2]
            keys, keys_t, values, dots = refs[2:]
            key_acc, value_acc = sum_out.at[0], sum_out.at[1]
        for b in range(total):
            source, at = (own_ref, b) if b < blocks else (other_ref, b - blocks)
            key = source[:, at].reshape(length, HD)
            keys[b] = key
            keys_t[b] = key.astype(jnp.float32).T.astype(jnp.bfloat16)
            values[b] = source[:, blocks + at].reshape(length, HD)
        row = lax.broadcasted_iota(jnp.int32, (PIECE, HD), 0)
        lane = lax.broadcasted_iota(jnp.int32, (PIECE, HD), 1)
        picks = jnp.where((lane % PIECE == row) & (lane < 3 * PIECE), 1.0, 0.0).astype(jnp.bfloat16)
        dots[...] = nt(picks, m_ref[:, 2 * count].reshape(length, HD))
        if last:
            key_acc[...] = sum_ref[0]
            value_acc[...] = sum_ref[1]
        else:
            sum_out[...] = jnp.zeros_like(sum_out)

        def block(c):
            query = m_ref[:, c].reshape(length, HD)
            grad = m_ref[:, count + c].reshape(length, HD)
            dot_row = dots[pl.ds(c, 1), :]
            places = [pair_ref[2 * (first + c)], pair_ref[2 * (first + c) + 1]]
            scores = [nt(keys[b], query) * (SCALE * LOG2E) for b in places]
            high = jnp.maximum(
                jnp.max(scores[0], axis=0, keepdims=True), jnp.max(scores[1], axis=0, keepdims=True)
            )
            weights = [jnp.exp2(s - high) for s in scores]
            norm = jnp.sum(weights[0], axis=0, keepdims=True) + jnp.sum(
                weights[1], axis=0, keepdims=True
            )
            inverse = 1.0 / norm
            query_t = None
            for b, weight in zip(places, weights):
                probs = weight * inverse
                value_acc[b] += nn(probs.astype(jnp.bfloat16), grad)
                prob_grad = nt(values[b], grad)
                score_grad = (probs * (prob_grad - dot_row) * SCALE).astype(jnp.bfloat16)
                key_acc[b] += nn(score_grad, query)
                part = nn(keys_t[b], score_grad)
                query_t = part if query_t is None else query_t + part
            out_ref[:, c] = query_t.T.astype(jnp.bfloat16).reshape(srcs, toks, HD)

        lax.fori_loop(0, count, lambda c, _: (block(c), 0)[1], 0)
        if last:
            own_sum[0] = key_acc[:blocks]
            own_sum[1] = value_acc[:blocks]
            other_sum[0] = key_acc[blocks:].astype(jnp.bfloat16)
            other_sum[1] = value_acc[blocks:].astype(jnp.bfloat16)

    def whole(shape):
        return pl.BlockSpec(shape, lambda i, p: (0,) * len(shape))

    dq = jax.ShapeDtypeStruct((srcs, count + extra, toks, HD), jnp.bfloat16)
    dq_spec = whole((srcs, count, toks, HD))
    acc = (2, total, length, HD)
    scratch = [
        pltpu.VMEM((total, length, HD), jnp.bfloat16),
        pltpu.VMEM((total, HD, length), jnp.bfloat16),
        pltpu.VMEM((total, length, HD), jnp.bfloat16),
        pltpu.VMEM((PIECE, length), jnp.float32),
    ]
    in_specs = [whole(message.shape), whole(kv_own.shape), whole(kv_other.shape)]
    args = [message, kv_own, kv_other]
    if last:
        part = (2, blocks, length, HD)
        out_shape = (
            dq,
            jax.ShapeDtypeStruct(part, jnp.float32),
            jax.ShapeDtypeStruct(part, jnp.bfloat16),
        )
        out_specs = [dq_spec, whole(part), whole(part)]
        scratch += [pltpu.VMEM((total, length, HD), jnp.float32)] * 2
        in_specs.append(whole(acc))
        args.append(sums)
    else:
        out_shape = (dq, jax.ShapeDtypeStruct(acc, jnp.float32))
        out_specs = [dq_spec, whole(acc)]
    flops = 2 * 5 * count * length * 2 * length * HD
    return pl.pallas_call(
        body,
        name=f"attend{first}",
        grid_spec=pltpu.PrefetchScalarGridSpec(
            num_scalar_prefetch=1,
            grid=(1,),
            in_specs=in_specs,
            out_specs=out_specs,
            scratch_shapes=scratch,
        ),
        out_shape=out_shape,
        compiler_params=params(),
        cost_estimate=pl.CostEstimate(
            flops=flops, transcendentals=2 * count * length * length, bytes_accessed=6 << 20
        ),
    )(pairs, *args)


def combine(message, own_sum, other_sum, count):
    srcs, _, toks, _ = message.shape
    blocks = own_sum.shape[1]

    def body(_, own_ref, other_ref, out_ref):
        for b in range(blocks):
            value = own_ref[0, b] + other_ref[0, b].astype(jnp.float32)
            out_ref[:, b] = value.astype(jnp.bfloat16).reshape(srcs, toks, HD)

    part = pl.BlockSpec((1,) + own_sum.shape[1:], lambda i: (i, 0, 0, 0))
    return pl.pallas_call(
        body,
        name="combine",
        grid=(2,),
        in_specs=[pl.BlockSpec(memory_space=pl.ANY), part, part],
        out_specs=pl.BlockSpec(
            (srcs, blocks, toks, HD), lambda i: (0, count // blocks + i, 0, 0)
        ),
        out_shape=jax.ShapeDtypeStruct(message.shape, message.dtype),
        input_output_aliases={0: 0},
        compiler_params=params(),
    )(message, own_sum, other_sum)


def unpack(message, total, first, count, step, into=None, blocks=0):
    heads, slots, toks, _ = message.shape
    width = heads * HD
    start = first // step

    def body(*refs):
        m_ref = refs[0]
        refs = refs[1:]
        if blocks:
            kv_refs, refs = refs[:2], refs[2:]
        if into is not None:
            refs = refs[1:]
        out_ref = refs[0]
        for h in range(heads):
            out_ref[:, :, h * HD : (h + 1) * HD] = m_ref[h]
        if blocks:

            @pl.when(pl.program_id(0) == 0)
            def _():
                for source, target in zip(kv_refs, refs[1:]):
                    for h in range(heads):
                        target[:, :, h * HD : (h + 1) * HD] = source[h]

    in_specs = [pl.BlockSpec((heads, step, toks, HD), lambda i: (0, i, 0, 0))]
    args = [message]
    out_shape = [jax.ShapeDtypeStruct((total, toks, width), message.dtype)]
    out_specs = [pl.BlockSpec((step, toks, width), lambda i: (start + i, 0, 0))]
    if blocks:
        behind = count // blocks
        in_specs += [
            pl.BlockSpec((heads, blocks, toks, HD), lambda i: (0, behind, 0, 0)),
            pl.BlockSpec((heads, blocks, toks, HD), lambda i: (0, behind + 1, 0, 0)),
        ]
        args += [message] * 2
        out_shape += [jax.ShapeDtypeStruct((blocks, toks, width), message.dtype)] * 2
        out_specs += [pl.BlockSpec((blocks, toks, width), lambda i: (0, 0, 0))] * 2
    aliases = {}
    if into is not None:
        in_specs.append(pl.BlockSpec(memory_space=pl.ANY))
        aliases = {len(args): 0}
        args.append(into)
    return pl.pallas_call(
        body,
        name=f"unpack{first}",
        grid=(count // step,),
        in_specs=in_specs,
        out_specs=out_specs,
        out_shape=out_shape,
        input_output_aliases=aliases,
        compiler_params=params(),
    )(*args)


def to_heads(message):
    return lax.all_to_all(message, "head", split_axis=0, concat_axis=0, tiled=True)


def on_device(
    query, out_grad, forward_out, key_codes, key_scale, value_codes, value_scale, pairing
):
    count = query.shape[0]
    blocks = key_codes.shape[0]
    half = count // 2
    swap = [(0, 1), (1, 0)]
    group = lax.axis_index("grp")
    mine = lax.dynamic_slice_in_dim(pairing, group * count, count, 0)
    pairs = ((mine + blocks * group) % (2 * blocks)).reshape(-1)

    send0 = pack(
        query, out_grad, forward_out, 0, half, 6, (key_codes, key_scale, value_codes, value_scale)
    )
    got0 = to_heads(send0)
    send1 = pack(query, out_grad, forward_out, half, half, 6)
    got1 = to_heads(send1)
    kv_own = got0[:, 2 * half + 1 :]
    kv_other = lax.ppermute(kv_own, "grp", swap)
    grad0, sums = attend(pairs, got0, kv_own, kv_other, 0, half)
    back0 = to_heads(grad0)
    grad1, own_sum, other_sum = attend(
        pairs, got1, kv_own, kv_other, half, half, sums, extra=2 * blocks
    )
    theirs = lax.ppermute(other_sum, "grp", swap)
    grad1 = combine(grad1, own_sum, theirs, half)
    back1 = to_heads(grad1)
    (rows,) = unpack(back0, count, 0, half, 6)
    rows, key_rows, value_rows = unpack(back1, count, half, half, 6, into=rows, blocks=blocks)
    return rows, key_rows, value_rows


def solution(mesh):
    spec = P("grp", "head", None)
    return jax.shard_map(
        on_device,
        mesh=mesh,
        in_specs=(spec,) * 7 + (P(),),
        out_specs=(spec,) * 3,
        check_vma=False,
    )
```

time: 1000 us -> 202 us (0.20); the launches traced: 985 us -> 201 us
  local copies, waits for them, and re-layouts: 451 us -> 3.39 us
  other arithmetic: 225 us -> 0.08 us
  matrix products: 104 us -> 0 us
  Pallas kernels: 0 us -> 65.1 us
  starting transfers between devices: 79.6 us -> 40.9 us
  between operations: 19 us -> 0.73 us
  blocking collectives: 16.6 us -> 0 us
    unnamed x705 -> x14, local copies, waits for them, and re-layouts: 240 us -> 2.57 us
    scatter-add x72 -> x0, other arithmetic: 122 us -> none  [the longest x36 61.8 us: kv_side(): value_acc = value_acc.at[chosen].add(value_grad.reshape(2, length, width))]
    dot_general x180 -> x0, matrix products: 104 us -> none  [the longest x36 37.8 us: backward_block(): jnp.einsum('rk,rd->kd', rounded, grad_rows, preferred_element_type=jnp.fl...]
    gather x72 -> x0, local copies, waits for them, and re-layouts: 82 us -> none  [the longest x36 42.3 us: kv_side(): value_set = jnp.take(value_all, chosen, axis=0).reshape(2 * length, width)]
    pallas_call x0 -> x7, Pallas kernels: none -> 65.1 us  [the longest x2 44.9 us: attend(): pl.pallas_call(body, name=f'attend{first}', grid_spec=pltpu.PrefetchScala...]
    select_n x72 -> x1, other arithmetic: 52.2 us -> 0.08 us  [on_device(): pairs = ((mine + blocks * group) % (2 * blocks)).reshape(-1)]
    sub x36 -> x0, local copies, waits for them, and re-layouts: 46.9 us -> none  [backward_block(): prob_grad - dot_rows[:, None]]
    all_to_all x10 -> x4, starting transfers between devices: 79.6 us -> 40.1 us  [to_heads(): lax.all_to_all(message, 'head', split_axis=0, concat_axis=0, tiled=True)]
  transfers between devices with their start and end apart: 12 -> 6, of which waited for: 7 -> 4; matrix products, arithmetic and copies ran while one was open for 53% -> 0% of each run, Pallas kernels for 0% -> 28%
where the time goes in v1:
time: 202 us; the launch traced here: 201 us
  waiting for transfers between devices  90.8 us (45%)
  Pallas kernels  65.1 us (32%)
  starting transfers between devices  40.9 us (20%)
  local copies, waits for them, and re-layouts  3.39 us (2%)
    all_to_all x4, waiting for transfers between devices, to_heads(): lax.all_to_all(message, 'head', split_axis=0, concat_axis=0, tiled=True)  52 us
    pallas_call x2, Pallas kernels, attend(): pl.pallas_call(body, name=f'attend{first}', grid_spec=pltpu.PrefetchScala...  44.9 us
    all_to_all x4, starting transfers between devices, to_heads(): lax.all_to_all(message, 'head', split_axis=0, concat_axis=0, tiled=True)  40.1 us
    ppermute x1, waiting for transfers between devices, on_device(): kv_other = lax.ppermute(kv_own, 'grp', swap)  31.2 us
    pallas_call x2, Pallas kernels, pack(): pl.pallas_call(body, name=f'pack{first}', grid=(steps,), in_specs=in_spec...  11.4 us
    ppermute x1, waiting for transfers between devices, on_device(): theirs = lax.ppermute(other_sum, 'grp', swap)  7.62 us
    pallas_call x2, Pallas kernels, unpack(): pl.pallas_call(body, name=f'unpack{first}', grid=(count // step,), in_spe...  6.94 us
  transfers between devices with their start and end apart: 6, of which 4 were waited for; matrix products, arithmetic and copies ran while one was open for 0% of the time, Pallas kernels for 28%

profile of v1, /device:TPU:1, one launch (start us, length us, event | category | flops | bytes accessed | tf_op | source)
XLA Modules:
  0.0 201.0 jit_solution(6057523269480536806)
XLA Ops:
  0.6 6.0 %pack0.1 = bf16[64,41,4,128]{3,2,1,0:T(4,128)(2,1)} custom-call(bf16[36,4,8192]{2,1,0:T(4,128)(2,1)} %refs_0_.3, bf16[36,4,8192]{2,1,0:T(4,128)(2,1)} %refs_1_.3, bf16[36,4,8192]{2,1,0:T(4,128)(2,1)} %refs_2_.3, bf16[2,4,8192]{2,1,0:T(4,128)(2,1)} %refs_3_.1, bf16[2,4,64]{2,1,0:T(4,128)(2,1)} %refs_4_.1, bf16[2,4,8192]{2,1,0:T(4,128)(2,1)} %refs_5_.1, ...), custom_call_target="tpu_custom_call" | custom-call | tf_op jit(solution)/shard_map/pack0/pallas_call | solution.py:103
  6.7 12.3 %all-to-all-start.1 = ((bf16[64,41,4,128]{3,2,1,0:T(4,128)(2,1)}), bf16[64,41,4,128]{3,2,1,0:T(4,128)(2,1)S(1)}, u32[]{:S(2)}, u32[]{:S(2)}) async-start(bf16[64,41,4,128]{3,2,1,0:T(4,128)(2,1)} %pack0.1), calls=%async_computation.1 | async-start | bytes 5373952 | tf_op jit(solution)/shard_map/all_to_all | solution.py:311
  19.0 5.4 %pack18.1 = bf16[64,37,4,128]{3,2,1,0:T(4,128)(2,1)} custom-call(bf16[36,4,8192]{2,1,0:T(4,128)(2,1)} %refs_0_.3, bf16[36,4,8192]{2,1,0:T(4,128)(2,1)} %refs_1_.3, bf16[36,4,8192]{2,1,0:T(4,128)(2,1)} %refs_2_.3), custom_call_target="tpu_custom_call" | custom-call | tf_op jit(solution)/shard_map/pack18/pallas_call | solution.py:103
  24.4 0.0 copy-start.5
  24.4 31.7 %all-to-all-done.1.m_ref = bf16[64,41,4,128]{3,2,1,0:T(4,128)(2,1)S(1)} async-done(((bf16[64,41,4,128]{3,2,1,0:T(4,128)(2,1)}), bf16[64,41,4,128]{3,2,1,0:T(4,128)(2,1)S(1)}, u32[]{:S(2)}, u32[]{:S(2)}) %all-to-all-start.1) | async-done | bytes 2687008 | tf_op jit(solution)/shard_map/all_to_all | solution.py:311
  56.2 5.1 %all-to-all-start = ((bf16[64,37,4,128]{3,2,1,0:T(4,128)(2,1)}), bf16[64,37,4,128]{3,2,1,0:T(4,128)(2,1)}, u32[]{:S(2)}, u32[]{:S(2)}) async-start(bf16[64,37,4,128]{3,2,1,0:T(4,128)(2,1)} %pack18.1), calls=%async_computation | async-start | bytes 4849664 | tf_op jit(solution)/shard_map/all_to_all | solution.py:311
  61.3 0.1 slice.4.own_ref
  61.4 0.8 collective-permute-start
  62.2 0.1 and_select_fusion
  62.3 0.1 copy.14
  62.4 0.6 reshape.9.pair_ref
  63.0 31.2 %collective-permute-done.other_ref = bf16[64,4,4,128]{3,2,1,0:T(4,128)(2,1)S(1)} collective-permute-done((bf16[64,4,4,128]{3,2,1,0:T(4,128)(2,1)S(1)}, bf16[64,4,4,128]{3,2,1,0:T(4,128)(2,1)S(1)}, u32[]{:S(2)}, u32[]{:S(2)}) %collective-permute-start) | collective-permute-done | bytes 262176 | tf_op jit(solution)/shard_map/ppermute | solution.py:332
  94.2 0.7 copy-done.6
  94.9 22.2 %attend0.1 = (bf16[64,18,4,128]{3,2,1,0:T(4,128)(2,1)}, f32[2,4,256,128]{3,2,1,0:T(8,128)}) custom-call(s32[72]{0:T(128)} %reshape.9.pair_ref, bf16[64,41,4,128]{3,2,1,0:T(4,128)(2,1)} %copy-done.2, bf16[64,4,4,128]{3,2,1,0:T(4,128)(2,1)} %copy-done.4, bf16[64,4,4,128]{3,2,1,0:T(4,128)(2,1)} %copy-done.6), custom_call_target="tpu_custom_call" | custom-call | flops 3019898880 | bytes 6291456 | tf_op jit(solution)/shard_map/attend0/pallas_call | solution.py:215
  117.1 11.4 %all-to-all-start.3 = ((bf16[64,18,4,128]{3,2,1,0:T(4,128)(2,1)}), bf16[64,18,4,128]{3,2,1,0:T(4,128)(2,1)S(1)}, u32[]{:S(2)}, u32[]{:S(2)}) async-start(bf16[64,18,4,128]{3,2,1,0:T(4,128)(2,1)} %get-tuple-element.12), calls=%async_computation.3 | async-start | bytes 2359296 | tf_op jit(solution)/shard_map/all_to_all | solution.py:311
  128.5 22.6 %attend18.1 = (bf16[64,22,4,128]{3,2,1,0:T(4,128)(2,1)}, f32[2,2,256,128]{3,2,1,0:T(8,128)}, bf16[2,2,256,128]{3,2,1,0:T(8,128)(2,1)}) custom-call(s32[72]{0:T(128)} %reshape.9.pair_ref, bf16[64,37,4,128]{3,2,1,0:T(4,128)(2,1)} %all-to-all-done.m_ref, bf16[64,4,4,128]{3,2,1,0:T(4,128)(2,1)} %copy-done.4, bf16[64,4,4,128]{3,2,1,0:T(4,128)(2,1)} %copy-done.6, ...), custom_call_target="tpu_custom_call" | custom-call | flops 3019898880 | bytes 6291456 | tf_op jit(solution)/shard_map/attend18/pallas_call | solution.py:215
  151.2 7.6 %collective-permute-done.1.other_ref = bf16[2,2,256,128]{3,2,1,0:T(8,128)(2,1)S(1)} collective-permute-done((bf16[2,2,256,128]{3,2,1,0:T(8,128)(2,1)}, bf16[2,2,256,128]{3,2,1,0:T(8,128)(2,1)S(1)}, u32[]{:S(2)}, u32[]{:S(2)}) %collective-permute-start.1) | collective-permute-done | bytes 262176 | tf_op jit(solution)/shard_map/ppermute | solution.py:338
  158.8 0.7 copy-done.3
  159.5 1.8 combine.1
  161.3 11.3 %all-to-all-start.2 = ((bf16[64,22,4,128]{3,2,1,0:T(4,128)(2,1)}), bf16[64,22,4,128]{3,2,1,0:T(4,128)(2,1)S(1)}, u32[]{:S(2)}, u32[]{:S(2)}) async-start(bf16[64,22,4,128]{3,2,1,0:T(4,128)(2,1)} %combine.1), calls=%async_computation.2 | async-start | bytes 2883584 | tf_op jit(solution)/shard_map/all_to_all | solution.py:311
  172.6 3.3 %unpack0.1.refs_3_ = bf16[36,4,8192]{2,1,0:T(4,128)(2,1)} custom-call(bf16[64,18,4,128]{3,2,1,0:T(4,128)(2,1)} %copy-done.1), custom_call_target="tpu_custom_call" | custom-call | tf_op jit(solution)/shard_map/unpack0/pallas_call | solution.py:298
  176.0 20.3 %all-to-all-done.2.refs_0_.refs_1_.refs_2_ = bf16[64,22,4,128]{3,2,1,0:T(4,128)(2,1)S(1)} async-done(((bf16[64,22,4,128]{3,2,1,0:T(4,128)(2,1)}), bf16[64,22,4,128]{3,2,1,0:T(4,128)(2,1)S(1)}, u32[]{:S(2)}, u32[]{:S(2)}) %all-to-all-start.2) | async-done | bytes 1441824 | tf_op jit(solution)/shard_map/all_to_all | solution.py:311
  196.2 1.1 copy-done
  197.4 3.6 %unpack18.1 = (bf16[36,4,8192]{2,1,0:T(4,128)(2,1)}, bf16[2,4,8192]{2,1,0:T(4,128)(2,1)}, bf16[2,4,8192]{2,1,0:T(4,128)(2,1)}) custom-call(bf16[64,22,4,128]{3,2,1,0:T(4,128)(2,1)} %copy-done, bf16[64,22,4,128]{3,2,1,0:T(4,128)(2,1)} %copy-done, bf16[64,22,4,128]{3,2,1,0:T(4,128)(2,1)} %copy-done, ...), custom_call_target="tpu_custom_call", output_to_operand_aliasing={{0}: (3, {})} | custom-call | tf_op jit(solution)/shard_map/unpack18/pallas_call | solution.py:298
  (13 shorter events, 0.0 us)
Async XLA Ops:
  6.7 49.5 %all-to-all-start.1 = ((bf16[64,41,4,128]{3,2,1,0:T(4,128)(2,1)}), bf16[64,41,4,128]{3,2,1,0:T(4,128)(2,1)S(1)}, u32[]{:S(2)}, u32[]{:S(2)}) async-start(bf16[64,41,4,128]{3,2,1,0:T(4,128)(2,1)} %pack0.1), calls=%async_computation.1 | async-start | bytes 5373952 | tf_op jit(solution)/shard_map/all_to_all | solution.py:311
  24.4 37.8 %copy-start.5 = (s32[72,2]{0,1:T(2,128)S(1)}, s32[72,2]{0,1:T(2,128)}, u32[]{:S(2)}) copy-start(s32[72,2]{0,1:T(2,128)} %param.15) | copy-start | bytes 1732
  56.2 5.1 %copy-start.2 = (bf16[64,41,4,128]{3,2,1,0:T(4,128)(2,1)}, bf16[64,41,4,128]{3,2,1,0:T(4,128)(2,1)S(1)}, u32[]{:S(2)}) copy-start(bf16[64,41,4,128]{3,2,1,0:T(4,128)(2,1)S(1)} %all-to-all-done.1.m_ref) | copy-start | bytes 8060932
  56.2 61.0 %all-to-all-start = ((bf16[64,37,4,128]{3,2,1,0:T(4,128)(2,1)}), bf16[64,37,4,128]{3,2,1,0:T(4,128)(2,1)}, u32[]{:S(2)}, u32[]{:S(2)}) async-start(bf16[64,37,4,128]{3,2,1,0:T(4,128)(2,1)} %pack18.1), calls=%async_computation | async-start | bytes 4849664 | tf_op jit(solution)/shard_map/all_to_all | solution.py:311
  61.4 32.8 %copy-start.4 = (bf16[64,4,4,128]{3,2,1,0:T(4,128)(2,1)}, bf16[64,4,4,128]{3,2,1,0:T(4,128)(2,1)S(1)}, u32[]{:S(2)}) copy-start(bf16[64,4,4,128]{3,2,1,0:T(4,128)(2,1)S(1)} %slice.4.own_ref) | copy-start | bytes 786436
  61.4 32.8 %collective-permute-start = (bf16[64,4,4,128]{3,2,1,0:T(4,128)(2,1)S(1)}, bf16[64,4,4,128]{3,2,1,0:T(4,128)(2,1)S(1)}, u32[]{:S(2)}, u32[]{:S(2)}) collective-permute-start(bf16[64,4,4,128]{3,2,1,0:T(4,128)(2,1)S(1)} %slice.4.own_ref), channel_id=1, source_target_pairs={{0,64},{64,0},{1,65},{65,1},{2,66},{66,2},{3,67},{67,3},{4,68},{68... | collective-permute-start | bytes 786440 | tf_op jit(solution)/shard_map/ppermute | solution.py:332
  94.2 0.7 copy-start.6
  117.1 44.2 %all-to-all-start.3 = ((bf16[64,18,4,128]{3,2,1,0:T(4,128)(2,1)}), bf16[64,18,4,128]{3,2,1,0:T(4,128)(2,1)S(1)}, u32[]{:S(2)}, u32[]{:S(2)}) async-start(bf16[64,18,4,128]{3,2,1,0:T(4,128)(2,1)} %get-tuple-element.12), calls=%async_computation.3 | async-start | bytes 2359296 | tf_op jit(solution)/shard_map/all_to_all | solution.py:311
  151.2 7.6 %collective-permute-start.1 = (bf16[2,2,256,128]{3,2,1,0:T(8,128)(2,1)}, bf16[2,2,256,128]{3,2,1,0:T(8,128)(2,1)S(1)}, u32[]{:S(2)}, u32[]{:S(2)}) collective-permute-start(bf16[2,2,256,128]{3,2,1,0:T(8,128)(2,1)} %get-tuple-element.11), channel_id=1, source_target_pairs={{0,64},{64,0},{1,65},{65,1},{2,66},{66,2},{3,67},{67,3},{4,68},{68... | collective-permute-start | bytes 786440 | tf_op jit(solution)/shard_map/ppermute | solution.py:338
  158.8 0.7 copy-start.3
  161.3 11.3 %copy-start.1 = (bf16[64,18,4,128]{3,2,1,0:T(4,128)(2,1)}, bf16[64,18,4,128]{3,2,1,0:T(4,128)(2,1)S(1)}, u32[]{:S(2)}) copy-start(bf16[64,18,4,128]{3,2,1,0:T(4,128)(2,1)S(1)} %all-to-all-done.3.refs_0_) | copy-start | bytes 3538948
  161.3 34.9 %all-to-all-start.2 = ((bf16[64,22,4,128]{3,2,1,0:T(4,128)(2,1)}), bf16[64,22,4,128]{3,2,1,0:T(4,128)(2,1)S(1)}, u32[]{:S(2)}, u32[]{:S(2)}) async-start(bf16[64,22,4,128]{3,2,1,0:T(4,128)(2,1)} %combine.1), calls=%async_computation.2 | async-start | bytes 2883584 | tf_op jit(solution)/shard_map/all_to_all | solution.py:311
  196.2 1.1 copy-start

commit v2 on v1

v2 whole, which is shorter than its diff:
```python
import jax
import jax.numpy as jnp
from jax import lax
from jax.experimental import pallas as pl
from jax.experimental.pallas import tpu as pltpu
from jax.sharding import PartitionSpec as P


HD = 128
SCALE = HD ** (-0.5)
LOG2E = 1.4426950408889634
EXP_SCALE = SCALE * LOG2E
SLOTS = 3
PIECE = 32


def params(mib=56):
    return pltpu.CompilerParams(vmem_limit_bytes=mib << 20)


def pack(query, out_grad, forward_out, first, count, step, kv=None):
    _, toks, width = query.shape
    heads = width // HD
    blocks = kv[0].shape[0] if kv else 0
    slots = 2 * count + 1 + 2 * blocks
    steps = count // step
    start = first // step

    def body(*refs):
        q_ref, g_ref, f_ref = refs[:3]
        kv_refs = refs[3 : 3 + (4 if kv else 0)]
        out_ref = refs[3 + len(kv_refs)]
        dots, dots_out = refs[4 + len(kv_refs) : 6 + len(kv_refs)]
        kv_out = refs[6 + len(kv_refs)] if kv else None
        sems = refs[-1]
        at = pl.program_id(0)

        @pl.when(at == 0)
        def _():
            dots[...] = jnp.zeros_like(dots)
            if kv:
                for which in range(2):
                    codes, scales = kv_refs[2 * which], kv_refs[2 * which + 1]
                    factor = scales[...].astype(jnp.float32)
                    for h in range(heads):
                        part = codes[:, :, h * HD : (h + 1) * HD].astype(jnp.float32)
                        rows = part * factor[:, :, h : h + 1]
                        kv_out[h, which * blocks : (which + 1) * blocks] = rows.astype(jnp.bfloat16)

        for h in range(heads):
            pltpu.make_async_copy(
                q_ref.at[:, :, pl.ds(h * HD, HD)], out_ref.at[h, pl.ds(at * step, step)], sems.at[0]
            ).start()
            pltpu.make_async_copy(
                g_ref.at[:, :, pl.ds(h * HD, HD)],
                out_ref.at[h, pl.ds(count + at * step, step)],
                sems.at[1],
            ).start()
        lane = lax.broadcasted_iota(jnp.int32, (step, toks, HD), 2)
        place = lax.broadcasted_iota(jnp.int32, (step, toks, HD), 0) + at * step
        chosen = lane == place
        for h in range(heads):
            cut = slice(h * HD, (h + 1) * HD)
            product = g_ref[:, :, cut].astype(jnp.float32) * f_ref[:, :, cut].astype(jnp.float32)
            total = jnp.sum(product, axis=-1, keepdims=True)
            dots[h] += jnp.sum(jnp.where(chosen, total, 0.0), axis=0)

        @pl.when(at == steps - 1)
        def _():
            for h in range(heads):
                value = dots[h]
                high = value.astype(jnp.bfloat16).astype(jnp.float32)
                middle = (value - high).astype(jnp.bfloat16).astype(jnp.float32)
                low = (value - high - middle).astype(jnp.bfloat16).astype(jnp.float32)
                spread = high + pltpu.roll(middle, PIECE, 1) + pltpu.roll(low, 2 * PIECE, 1)
                dots_out[h, 0] = spread.astype(jnp.bfloat16)
            copies = [
                pltpu.make_async_copy(dots_out, out_ref.at[:, pl.ds(2 * count, 1)], sems.at[2])
            ]
            if kv:
                copies.append(
                    pltpu.make_async_copy(
                        kv_out, out_ref.at[:, pl.ds(2 * count + 1, 2 * blocks)], sems.at[3]
                    )
                )
            for copy in copies:
                copy.start()
            for copy in copies:
                copy.wait()

        pltpu.make_async_copy(q_ref, q_ref, sems.at[0]).wait()
        pltpu.make_async_copy(g_ref, g_ref, sems.at[1]).wait()

    rows = pl.BlockSpec((step, toks, width), lambda i: (start + i, 0, 0))
    in_specs = [rows] * 3
    args = [query, out_grad, forward_out]
    scratch = [
        pltpu.VMEM((heads, toks, HD), jnp.float32),
        pltpu.VMEM((heads, 1, toks, HD), jnp.bfloat16),
    ]
    if kv:
        in_specs += [pl.BlockSpec(x.shape, lambda i: (0, 0, 0)) for x in kv]
        args += list(kv)
        scratch.append(pltpu.VMEM((heads, 2 * blocks, toks, HD), jnp.bfloat16))
    scratch.append(pltpu.SemaphoreType.DMA((4,)))
    return pl.pallas_call(
        body,
        grid=(steps,),
        in_specs=in_specs,
        out_specs=pl.BlockSpec(memory_space=pl.ANY),
        out_shape=jax.ShapeDtypeStruct((heads, slots, toks, HD), jnp.bfloat16),
        scratch_shapes=scratch,
        compiler_params=params(),
    )(*args)


def nt(a, b):
    return lax.dot_general(a, b, (((1,), (1,)), ((), ())), preferred_element_type=jnp.float32)


def nn(a, b):
    return jnp.dot(a, b, preferred_element_type=jnp.float32)


def attend(pairs, message, kv_own, kv_other, first, count, total_out, sums=None, into=None):
    srcs, _, toks, _ = message.shape
    length = srcs * toks
    blocks = kv_own.shape[1] // 2
    total = 2 * blocks
    last = sums is not None

    def body(pair_ref, m_ref, own_ref, other_ref, *refs):
        if last:
            sum_ref, _, target = refs[:3]
            refs, (key_acc, value_acc, out_ref, sems) = refs[3:-4], refs[-4:]
        else:
            out_ref, sum_out = refs[:2]
            refs = refs[2:]
            key_acc, value_acc = sum_out.at[0], sum_out.at[1]
        keys, keys_t, values, dots = refs[:4]
        scores, prob_grads, probs, score_grads, queries, grads = (
            refs[4 + SLOTS * at : 4 + SLOTS * (at + 1)] for at in range(6)
        )
        for b in range(total):
            source, at = (own_ref, b) if b < blocks else (other_ref, b - blocks)
            key = source[:, at].reshape(length, HD)
            keys[b] = key
            keys_t[b] = key.astype(jnp.float32).T.astype(jnp.bfloat16)
            values[b] = source[:, blocks + at].reshape(length, HD)
        row = lax.broadcasted_iota(jnp.int32, (PIECE, HD), 0)
        lane = lax.broadcasted_iota(jnp.int32, (PIECE, HD), 1)
        picks = jnp.where((lane % PIECE == row) & (lane < 3 * PIECE), 1.0, 0.0).astype(jnp.bfloat16)
        dots[...] = nt(picks, m_ref[:, 2 * count].reshape(length, HD))
        if last:
            key_acc[...] = sum_ref[0]
            value_acc[...] = sum_ref[1]
        else:
            sum_out[...] = jnp.zeros_like(sum_out)

        def place(c, j):
            return pair_ref[2 * (first + c) + j]

        def scores_of(c, slot):
            query = m_ref[:, c].reshape(length, HD)
            grad = m_ref[:, count + c].reshape(length, HD)
            queries[slot][...] = query
            grads[slot][...] = grad
            for j in range(2):
                scores[slot][j] = nt(keys[place(c, j)], query)
                prob_grads[slot][j] = nt(values[place(c, j)], grad)

        def probs_of(c, slot):
            score, prob_grad = scores[slot], prob_grads[slot]
            cuts = [(j, slice(r, r + 32)) for j in range(2) for r in range(0, length, 32)]
            high = None
            for j, rows in cuts:
                part = jnp.max(score[j, rows].reshape(32 // 8, 8, length), axis=0)
                high = part if high is None else jnp.maximum(high, part)
            high = jnp.max(high, axis=0, keepdims=True) * EXP_SCALE
            norm = None
            for j, rows in cuts:
                weight = jnp.exp2(score[j, rows] * EXP_SCALE - high)
                score[j, rows] = weight
                part = jnp.sum(weight.reshape(32 // 8, 8, length), axis=0)
                norm = part if norm is None else norm + part
            inverse = 1.0 / jnp.sum(norm, axis=0, keepdims=True)
            dot_row = dots[pl.ds(c, 1), :]
            for j, rows in cuts:
                prob = score[j, rows] * inverse
                probs[slot][j, rows] = prob.astype(jnp.bfloat16)
                score_grads[slot][j, rows] = (prob * (prob_grad[j, rows] - dot_row)).astype(
                    jnp.bfloat16
                )

        def grads_of(c, slot):
            query_t = None
            for j in range(2):
                b = place(c, j)
                value_acc[b] += nn(probs[slot][j], grads[slot][...])
                key_acc[b] += nn(score_grads[slot][j], queries[slot][...])
                part = nn(keys_t[b], score_grads[slot][j])
                query_t = part if query_t is None else query_t + part
            out_ref[:, c] = (query_t * SCALE).T.astype(jnp.bfloat16).reshape(srcs, toks, HD)

        for ref in (probs[-1], score_grads[-1], queries[-1], grads[-1]):
            ref[...] = jnp.zeros_like(ref)
        scores_of(0, 0)

        def several(i, _):
            for k in range(SLOTS):
                c = i * SLOTS + k
                grads_of(jnp.maximum(c - 1, 0), (k - 1) % SLOTS)
                scores_of(jnp.minimum(c + 1, count - 1), (k + 1) % SLOTS)
                probs_of(c, k)
            return 0

        lax.fori_loop(0, count // SLOTS, several, 0)
        grads_of(count - 1, SLOTS - 1)
        if last:
            for b in range(total):
                at = count + (b // blocks) * 2 * blocks + b % blocks
                key_rows = (key_acc[b] * SCALE).astype(jnp.bfloat16)
                out_ref[:, at] = key_rows.reshape(srcs, toks, HD)
                value_rows = value_acc[b].astype(jnp.bfloat16)
                out_ref[:, at + blocks] = value_rows.reshape(srcs, toks, HD)
            copy = pltpu.make_async_copy(
                out_ref, target.at[:, pl.ds(first, count + 2 * total)], sems.at[0]
            )
            copy.start()
            copy.wait()

    def whole(shape):
        return pl.BlockSpec(shape, lambda i, p: (0,) * len(shape))

    dq = jax.ShapeDtypeStruct((srcs, total_out, toks, HD), jnp.bfloat16)
    dq_spec = whole((srcs, count, toks, HD))
    acc = (2, total, length, HD)
    scratch = [
        pltpu.VMEM((total, length, HD), jnp.bfloat16),
        pltpu.VMEM((total, HD, length), jnp.bfloat16),
        pltpu.VMEM((total, length, HD), jnp.bfloat16),
        pltpu.VMEM((PIECE, length), jnp.float32),
    ]
    scratch += [pltpu.VMEM((2, length, length), jnp.float32)] * (2 * SLOTS)
    scratch += [pltpu.VMEM((2, length, length), jnp.bfloat16)] * (2 * SLOTS)
    scratch += [pltpu.VMEM((length, HD), jnp.bfloat16)] * (2 * SLOTS)
    in_specs = [whole(message.shape), whole(kv_own.shape), whole(kv_other.shape)]
    args = [message, kv_own, kv_other]
    aliases = {}
    if last:
        out_shape = dq
        out_specs = pl.BlockSpec(memory_space=pl.ANY)
        scratch += [pltpu.VMEM((total, length, HD), jnp.float32)] * 2
        scratch.append(pltpu.VMEM((srcs, count + 2 * total, toks, HD), jnp.bfloat16))
        scratch.append(pltpu.SemaphoreType.DMA((1,)))
        in_specs += [whole(acc), pl.BlockSpec(memory_space=pl.ANY)]
        args += [sums, into]
        aliases = {len(args): 0}
    else:
        out_shape = (dq, jax.ShapeDtypeStruct(acc, jnp.float32))
        out_specs = [dq_spec, whole(acc)]
    flops = 2 * 5 * count * length * 2 * length * HD
    return pl.pallas_call(
        body,
        grid_spec=pltpu.PrefetchScalarGridSpec(
            num_scalar_prefetch=1,
            grid=(1,),
            in_specs=in_specs,
            out_specs=out_specs,
            scratch_shapes=scratch,
        ),
        out_shape=out_shape,
        input_output_aliases=aliases,
        compiler_params=params(),
        cost_estimate=pl.CostEstimate(
            flops=flops, transcendentals=2 * count * length * length, bytes_accessed=6 << 20
        ),
    )(pairs, *args)


def unpack(message, count, step):
    heads, _, toks, _ = message.shape
    width = heads * HD

    def body(m_ref, out_ref):
        for h in range(heads):
            out_ref[:, :, h * HD : (h + 1) * HD] = m_ref[h]

    return pl.pallas_call(
        body,
        name="unpack",
        grid=(count // step,),
        in_specs=[pl.BlockSpec((heads, step, toks, HD), lambda i: (0, i, 0, 0))],
        out_specs=pl.BlockSpec((step, toks, width), lambda i: (i, 0, 0)),
        out_shape=jax.ShapeDtypeStruct((count, toks, width), message.dtype),
        compiler_params=params(),
    )(message)


def unpack_sums(message, theirs, first, blocks):
    heads, _, toks, _ = message.shape
    width = heads * HD
    behind = first // blocks

    def body(k_ref, v_ref, t_ref, key_out, value_out):
        for which, (mine, out) in enumerate(((k_ref, key_out), (v_ref, value_out))):
            for h in range(heads):
                other = t_ref[h, which * blocks : (which + 1) * blocks].astype(jnp.float32)
                total = mine[h].astype(jnp.float32) + other
                out[:, :, h * HD : (h + 1) * HD] = total.astype(jnp.bfloat16)

    rows = jax.ShapeDtypeStruct((blocks, toks, width), message.dtype)
    rows_spec = pl.BlockSpec((blocks, toks, width), lambda i: (0, 0, 0))
    return pl.pallas_call(
        body,
        name="unpack_sums",
        grid=(1,),
        in_specs=[
            pl.BlockSpec((heads, blocks, toks, HD), lambda i: (0, behind, 0, 0)),
            pl.BlockSpec((heads, blocks, toks, HD), lambda i: (0, behind + 1, 0, 0)),
            pl.BlockSpec(theirs.shape, lambda i: (0, 0, 0, 0)),
        ],
        out_specs=[rows_spec] * 2,
        out_shape=[rows] * 2,
        compiler_params=params(),
    )(message, message, theirs)


def to_heads(message):
    return lax.all_to_all(message, "head", split_axis=0, concat_axis=0, tiled=True)


def on_device(
    query, out_grad, forward_out, key_codes, key_scale, value_codes, value_scale, pairing
):
    count = query.shape[0]
    blocks = key_codes.shape[0]
    large = count * 2 // 3
    small = count - large
    swap = [(0, 1), (1, 0)]
    group = lax.axis_index("grp")
    mine = lax.dynamic_slice_in_dim(pairing, group * count, count, 0)
    pairs = ((mine + blocks * group) % (2 * blocks)).reshape(-1)
    codes = (key_codes, key_scale, value_codes, value_scale)
    send0 = pack(query, out_grad, forward_out, 0, large, 6, codes)
    got0 = to_heads(send0)
    send1 = pack(query, out_grad, forward_out, large, small, 6)
    got1 = to_heads(send1)
    kv_own = got0[:, 2 * large + 1 :]
    kv_other = lax.ppermute(kv_own, "grp", swap)
    slots = count + 4 * blocks
    grads, sums = attend(pairs, got0, kv_own, kv_other, 0, large, slots)
    grads = attend(pairs, got1, kv_own, kv_other, large, small, slots, sums, grads)
    back = to_heads(grads)
    theirs = lax.ppermute(back[:, count + 2 * blocks :], "grp", swap)
    rows = unpack(back, count, 6)
    key_rows, value_rows = unpack_sums(back, theirs, count, blocks)
    return rows, key_rows, value_rows


def solution(mesh):
    spec = P("grp", "head", None)
    return jax.shard_map(
        on_device,
        mesh=mesh,
        in_specs=(spec,) * 7 + (P(),),
        out_specs=(spec,) * 3,
        check_vma=False,
    )
```

time: 202 us -> 190 us (0.941)
  blocking collectives: 0 us -> 50.1 us
  waiting for transfers between devices: 90.8 us -> 64.9 us
  starting transfers between devices: 40.9 us -> 18 us
  Pallas kernels: 65.1 us -> 48 us
  local copies, waits for them, and re-layouts: 3.39 us -> 7.61 us
    all_to_all x0 -> x1, blocking collectives: none -> 50.1 us  [to_heads(): lax.all_to_all(message, 'head', split_axis=0, concat_axis=0, tiled=True)]
    all_to_all x4 -> x2, starting transfers between devices: 40.1 us -> 17.1 us  [to_heads(): lax.all_to_all(message, 'head', split_axis=0, concat_axis=0, tiled=True)]
    pallas_call x7 -> x6, Pallas kernels: 65.1 us -> 48 us  [the longest x2 29.4 us: attend(): pl.pallas_call(body, grid_spec=pltpu.PrefetchScalarGridSpec(num_scalar_pr...]
    all_to_all x4 -> x2, waiting for transfers between devices: 52 us -> 41.5 us  [to_heads(): lax.all_to_all(message, 'head', split_axis=0, concat_axis=0, tiled=True)]
    ppermute x1, waiting for transfers between devices: 31.2 us -> 22.5 us  [on_device(): kv_other = lax.ppermute(kv_own, 'grp', swap)]
    ppermute x1, waiting for transfers between devices: 7.62 us -> 0.82 us  [on_device(): theirs = lax.ppermute(back[:, count + 2 * blocks:], 'grp', swap)]
    unnamed x14, local copies, waits for them, and re-layouts: 2.57 us -> 5.73 us
  transfers between devices with their start and end apart: 6 -> 4, of which waited for: 4 -> 3; matrix products, arithmetic and copies ran while one was open for 0% -> 1% of each run, Pallas kernels for 28% -> 15%
where the time goes in v2:
time: 190 us; the launch traced here: 189 us
  waiting for transfers between devices  64.9 us (34%)
  blocking collectives  50.1 us (26%)
  Pallas kernels  48 us (25%)
  starting transfers between devices  18 us (9%)
  local copies, waits for them, and re-layouts  7.61 us (4%)
    all_to_all x1, blocking collectives, to_heads(): lax.all_to_all(message, 'head', split_axis=0, concat_axis=0, tiled=True)  50.1 us
    all_to_all x2, waiting for transfers between devices, to_heads(): lax.all_to_all(message, 'head', split_axis=0, concat_axis=0, tiled=True)  41.5 us
    pallas_call x2, Pallas kernels, attend(): pl.pallas_call(body, grid_spec=pltpu.PrefetchScalarGridSpec(num_scalar_pr...  29.4 us
    ppermute x1, waiting for transfers between devices, on_device(): kv_other = lax.ppermute(kv_own, 'grp', swap)  22.5 us
    all_to_all x2, starting transfers between devices, to_heads(): lax.all_to_all(message, 'head', split_axis=0, concat_axis=0, tiled=True)  17.1 us
    pallas_call x2, Pallas kernels, pack(): pl.pallas_call(body, grid=(steps,), in_specs=in_specs, out_specs=pl.Block...  11.4 us
    unnamed x14, local copies, waits for them, and re-layouts  5.73 us
    pallas_call x1, Pallas kernels, unpack(): pl.pallas_call(body, name='unpack', grid=(count // step,), in_specs=[pl.B...  5.24 us
  transfers between devices with their start and end apart: 4, of which 3 were waited for; matrix products, arithmetic and copies ran while one was open for 1% of the time, Pallas kernels for 15%

profile of v2, /device:TPU:1, one launch (start us, length us, event | category | flops | bytes accessed | tf_op | source)
XLA Modules:
  0.0 189.4 jit_solution(10951911211451678773)
XLA Ops:
  0.6 7.4 %shard_map.104 = bf16[64,53,4,128]{3,2,1,0:T(4,128)(2,1)} custom-call(bf16[36,4,8192]{2,1,0:T(4,128)(2,1)} %refs_0_.3, bf16[36,4,8192]{2,1,0:T(4,128)(2,1)} %refs_1_.3, bf16[36,4,8192]{2,1,0:T(4,128)(2,1)} %refs_2_.3, bf16[2,4,8192]{2,1,0:T(4,128)(2,1)} %refs_3_.1, bf16[2,4,64]{2,1,0:T(4,128)(2,1)} %refs_4_.1, bf16[2,4,8192]{2,1,0:T(4,128)(2,1)} %refs_5_.1, ...), custom_call_target="tpu_custom_call" | custom-call | tf_op jit(solution)/shard_map/pallas_call | solution.py:106
  8.0 12.3 %all-to-all-start.1 = ((bf16[64,53,4,128]{3,2,1,0:T(4,128)(2,1)}), bf16[64,53,4,128]{3,2,1,0:T(4,128)(2,1)S(1)}, u32[]{:S(2)}, u32[]{:S(2)}) async-start(bf16[64,53,4,128]{3,2,1,0:T(4,128)(2,1)} %shard_map.104), calls=%async_computation.1 | async-start | bytes 6946816 | tf_op jit(solution)/shard_map/all_to_all | solution.py:330
  20.3 4.0 %shard_map.103 = bf16[64,25,4,128]{3,2,1,0:T(4,128)(2,1)} custom-call(bf16[36,4,8192]{2,1,0:T(4,128)(2,1)} %refs_0_.3, bf16[36,4,8192]{2,1,0:T(4,128)(2,1)} %refs_1_.3, bf16[36,4,8192]{2,1,0:T(4,128)(2,1)} %refs_2_.3), custom_call_target="tpu_custom_call" | custom-call | tf_op jit(solution)/shard_map/pallas_call | solution.py:106
  24.4 41.5 %all-to-all-done.1.m_ref = bf16[64,53,4,128]{3,2,1,0:T(4,128)(2,1)S(1)} async-done(((bf16[64,53,4,128]{3,2,1,0:T(4,128)(2,1)}), bf16[64,53,4,128]{3,2,1,0:T(4,128)(2,1)S(1)}, u32[]{:S(2)}, u32[]{:S(2)}) %all-to-all-start.1) | async-done | bytes 3473440 | tf_op jit(solution)/shard_map/all_to_all | solution.py:330
  65.9 1.7 copy-done.2
  67.7 4.8 %all-to-all-start = ((bf16[64,25,4,128]{3,2,1,0:T(4,128)(2,1)}), bf16[64,25,4,128]{3,2,1,0:T(4,128)(2,1)S(1)}, u32[]{:S(2)}, u32[]{:S(2)}) async-start(bf16[64,25,4,128]{3,2,1,0:T(4,128)(2,1)} %shard_map.103), calls=%async_computation | async-start | bytes 3276800 | tf_op jit(solution)/shard_map/all_to_all | solution.py:330
  72.5 1.1 slice.8.own_ref
  73.5 0.8 collective-permute-start
  74.4 0.1 and_select_fusion
  74.4 0.1 copy.13
  74.5 0.6 reshape.9.pair_ref
  75.2 22.5 %collective-permute-done.other_ref = bf16[64,4,4,128]{3,2,1,0:T(4,128)(2,1)S(1)} collective-permute-done((bf16[64,4,4,128]{3,2,1,0:T(4,128)(2,1)S(1)}, bf16[64,4,4,128]{3,2,1,0:T(4,128)(2,1)S(1)}, u32[]{:S(2)}, u32[]{:S(2)}) %collective-permute-start) | collective-permute-done | bytes 262176 | tf_op jit(solution)/shard_map/ppermute | solution.py:350
  97.7 0.7 copy-done.4
  98.4 18.3 %shard_map.105 = (bf16[64,44,4,128]{3,2,1,0:T(4,128)(2,1)}, f32[2,4,256,128]{3,2,1,0:T(8,128)}) custom-call(s32[72]{0:T(128)} %reshape.9.pair_ref, bf16[64,53,4,128]{3,2,1,0:T(4,128)(2,1)} %copy-done.2, bf16[64,4,4,128]{3,2,1,0:T(4,128)(2,1)} %copy-done.3, bf16[64,4,4,128]{3,2,1,0:T(4,128)(2,1)} %copy-done.4), custom_call_target="tpu_custom_call" | custom-call | flops 4026531840 | bytes 6291456 | tf_op jit(solution)/shard_map/pallas_call | solution.py:263
  116.7 1.2 copy-done.1
  117.9 11.1 %shard_map.106 = bf16[64,44,4,128]{3,2,1,0:T(4,128)(2,1)} custom-call(s32[72]{0:T(128)} %reshape.9.pair_ref, bf16[64,25,4,128]{3,2,1,0:T(4,128)(2,1)} %copy-done.1, bf16[64,4,4,128]{3,2,1,0:T(4,128)(2,1)} %copy-done.3, bf16[64,4,4,128]{3,2,1,0:T(4,128)(2,1)} %copy-done.4, ...), custom_call_target="tpu_custom_call", output_to_operand_aliasing={{}: (5, {})} | custom-call | flops 2013265920 | bytes 6291456 | tf_op jit(solution)/shard_map/pallas_call | solution.py:263
  129.0 50.1 %all_to_all.15.m_ref.k_ref.v_ref = bf16[64,44,4,128]{3,2,1,0:T(4,128)(2,1)S(1)} all-to-all(bf16[64,44,4,128]{3,2,1,0:T(4,128)(2,1)} %shard_map.106), channel_id=1, replica_groups=mesh['grp'=2,'head'=64] {'head'}, dimensions={0} | all-to-all | bytes 5767168 | tf_op jit(solution)/shard_map/all_to_all | solution.py:330
  179.2 0.1 slice.9
  179.3 0.1 collective-permute-start.1
  179.4 1.4 copy-done
  180.8 5.2 %unpack.1 = bf16[36,4,8192]{2,1,0:T(4,128)(2,1)} custom-call(bf16[64,44,4,128]{3,2,1,0:T(4,128)(2,1)} %copy-done), custom_call_target="tpu_custom_call" | custom-call | tf_op jit(solution)/shard_map/unpack/pallas_call | solution.py:289
  186.0 0.8 collective-permute-done.1.t_ref
  186.8 0.7 copy-done.5
  187.5 1.9 unpack_sums.1
  (10 shorter events, 0.0 us)
Async XLA Ops:
  8.0 57.9 %all-to-all-start.1 = ((bf16[64,53,4,128]{3,2,1,0:T(4,128)(2,1)}), bf16[64,53,4,128]{3,2,1,0:T(4,128)(2,1)S(1)}, u32[]{:S(2)}, u32[]{:S(2)}) async-start(bf16[64,53,4,128]{3,2,1,0:T(4,128)(2,1)} %shard_map.104), calls=%async_computation.1 | async-start | bytes 6946816 | tf_op jit(solution)/shard_map/all_to_all | solution.py:330
  24.4 50.0 %copy-start.6 = (s32[72,2]{0,1:T(2,128)S(1)}, s32[72,2]{0,1:T(2,128)}, u32[]{:S(2)}) copy-start(s32[72,2]{0,1:T(2,128)} %param.15) | copy-start | bytes 1732
  65.9 1.7 copy-start.2
  67.7 49.1 %all-to-all-start = ((bf16[64,25,4,128]{3,2,1,0:T(4,128)(2,1)}), bf16[64,25,4,128]{3,2,1,0:T(4,128)(2,1)S(1)}, u32[]{:S(2)}, u32[]{:S(2)}) async-start(bf16[64,25,4,128]{3,2,1,0:T(4,128)(2,1)} %shard_map.103), calls=%async_computation | async-start | bytes 3276800 | tf_op jit(solution)/shard_map/all_to_all | solution.py:330
  73.5 24.2 %copy-start.3 = (bf16[64,4,4,128]{3,2,1,0:T(4,128)(2,1)}, bf16[64,4,4,128]{3,2,1,0:T(4,128)(2,1)S(1)}, u32[]{:S(2)}) copy-start(bf16[64,4,4,128]{3,2,1,0:T(4,128)(2,1)S(1)} %slice.8.own_ref) | copy-start | bytes 786436
  73.5 24.2 %collective-permute-start = (bf16[64,4,4,128]{3,2,1,0:T(4,128)(2,1)S(1)}, bf16[64,4,4,128]{3,2,1,0:T(4,128)(2,1)S(1)}, u32[]{:S(2)}, u32[]{:S(2)}) collective-permute-start(bf16[64,4,4,128]{3,2,1,0:T(4,128)(2,1)S(1)} %slice.8.own_ref), channel_id=1, source_target_pairs={{0,64},{64,0},{1,65},{65,1},{2,66},{66,2},{3,67},{67,3},{4,68},{68... | collective-permute-start | bytes 786440 | tf_op jit(solution)/shard_map/ppermute | solution.py:350
  97.7 0.7 copy-start.4
  116.7 1.2 copy-start.1
  179.2 1.6 copy-start
  179.3 7.6 %collective-permute-start.1 = (bf16[64,4,4,128]{3,2,1,0:T(4,128)(2,1)S(1)}, bf16[64,4,4,128]{3,2,1,0:T(4,128)(2,1)S(1)}, u32[]{:S(2)}, u32[]{:S(2)}) collective-permute-start(bf16[64,4,4,128]{3,2,1,0:T(4,128)(2,1)S(1)} %slice.9), channel_id=1, source_target_pairs={{0,64},{64,0},{1,65},{65,1},{2,66},{66,2},{3,67},{67,3},{4,68},{68... | collective-permute-start | bytes 786440 | tf_op jit(solution)/shard_map/ppermute | solution.py:355
  186.8 0.7 copy-start.5

commit v3 on v2

--- a/solution.py
+++ b/solution.py
@@ -12,6 +12,13 @@
 EXP_SCALE = SCALE * LOG2E
 SLOTS = 3
 PIECE = 32
+
+
+HELD = pl.BlockSpec(memory_space=pltpu.VMEM)
+
+
+def held(x):
+    return pltpu.with_memory_space_constraint(x, pltpu.VMEM)
 
 
 def params(mib=56):
@@ -56,14 +63,15 @@
                 out_ref.at[h, pl.ds(count + at * step, step)],
                 sems.at[1],
             ).start()
-        lane = lax.broadcasted_iota(jnp.int32, (step, toks, HD), 2)
-        place = lax.broadcasted_iota(jnp.int32, (step, toks, HD), 0) + at * step
+        lane = lax.broadcasted_iota(jnp.int32, (step * toks, HD), 1)
+        place = lax.broadcasted_iota(jnp.int32, (step * toks, HD), 0) // toks + at * step
         chosen = lane == place
         for h in range(heads):
             cut = slice(h * HD, (h + 1) * HD)
             product = g_ref[:, :, cut].astype(jnp.float32) * f_ref[:, :, cut].astype(jnp.float32)
-            total = jnp.sum(product, axis=-1, keepdims=True)
-            dots[h] += jnp.sum(jnp.where(chosen, total, 0.0), axis=0)
+            total = jnp.sum(product.reshape(step * toks, HD), axis=-1, keepdims=True)
+            rows_of = jnp.where(chosen, total, 0.0)
+            dots[h] += jnp.sum(rows_of.reshape(step, toks, HD), axis=0)
 
         @pl.when(at == steps - 1)
         def _():
@@ -244,8 +252,8 @@
     scratch += [pltpu.VMEM((2, length, length), jnp.float32)] * (2 * SLOTS)
     scratch += [pltpu.VMEM((2, length, length), jnp.bfloat16)] * (2 * SLOTS)
     scratch += [pltpu.VMEM((length, HD), jnp.bfloat16)] * (2 * SLOTS)
-    in_specs = [whole(message.shape), whole(kv_own.shape), whole(kv_other.shape)]
-    args = [message, kv_own, kv_other]
+    in_specs = [HELD if last else whole(message.shape), HELD, HELD]
+    args = [held(message) if last else message, held(kv_own), held(kv_other)]
     aliases = {}
     if last:
         out_shape = dq
@@ -253,12 +261,12 @@
         scratch += [pltpu.VMEM((total, length, HD), jnp.float32)] * 2
         scratch.append(pltpu.VMEM((srcs, count + 2 * total, toks, HD), jnp.bfloat16))
         scratch.append(pltpu.SemaphoreType.DMA((1,)))
-        in_specs += [whole(acc), pl.BlockSpec(memory_space=pl.ANY)]
-        args += [sums, into]
+        in_specs += [HELD, pl.BlockSpec(memory_space=pl.ANY)]
+        args += [held(sums), into]
         aliases = {len(args): 0}
     else:
-        out_shape = (dq, jax.ShapeDtypeStruct(acc, jnp.float32))
-        out_specs = [dq_spec, whole(acc)]
+        out_shape = (dq, pltpu.VMEM(acc, jnp.float32))
+        out_specs = [dq_spec, HELD]
     flops = 2 * 5 * count * length * 2 * length * HD
     return pl.pallas_call(
         body,
@@ -283,47 +291,43 @@
     width = heads * HD
 
     def body(m_ref, out_ref):
+        first = pl.program_id(0) * step
         for h in range(heads):
-            out_ref[:, :, h * HD : (h + 1) * HD] = m_ref[h]
+            out_ref[:, :, h * HD : (h + 1) * HD] = m_ref[h, pl.ds(first, step)]
 
     return pl.pallas_call(
         body,
         name="unpack",
         grid=(count // step,),
-        in_specs=[pl.BlockSpec((heads, step, toks, HD), lambda i: (0, i, 0, 0))],
+        in_specs=[HELD],
         out_specs=pl.BlockSpec((step, toks, width), lambda i: (i, 0, 0)),
         out_shape=jax.ShapeDtypeStruct((count, toks, width), message.dtype),
         compiler_params=params(),
-    )(message)
+    )(held(message))
 
 
 def unpack_sums(message, theirs, first, blocks):
     heads, _, toks, _ = message.shape
     width = heads * HD
-    behind = first // blocks
-
-    def body(k_ref, v_ref, t_ref, key_out, value_out):
-        for which, (mine, out) in enumerate(((k_ref, key_out), (v_ref, value_out))):
+
+    def body(m_ref, t_ref, *outs):
+        for which, out in enumerate(outs):
+            at = which * blocks
             for h in range(heads):
-                other = t_ref[h, which * blocks : (which + 1) * blocks].astype(jnp.float32)
-                total = mine[h].astype(jnp.float32) + other
+                total = m_ref[h, first + at : first + at + blocks].astype(jnp.float32)
+                total += t_ref[h, at : at + blocks].astype(jnp.float32)
                 out[:, :, h * HD : (h + 1) * HD] = total.astype(jnp.bfloat16)
 
     rows = jax.ShapeDtypeStruct((blocks, toks, width), message.dtype)
-    rows_spec = pl.BlockSpec((blocks, toks, width), lambda i: (0, 0, 0))
     return pl.pallas_call(
         body,
         name="unpack_sums",
         grid=(1,),
-        in_specs=[
-            pl.BlockSpec((heads, blocks, toks, HD), lambda i: (0, behind, 0, 0)),
-            pl.BlockSpec((heads, blocks, toks, HD), lambda i: (0, behind + 1, 0, 0)),
-            pl.BlockSpec(theirs.shape, lambda i: (0, 0, 0, 0)),
-        ],
-        out_specs=[rows_spec] * 2,
+        in_specs=[HELD] * 2,
+        out_specs=[pl.BlockSpec((blocks, toks, width), lambda i: (0, 0, 0))] * 2,
         out_shape=[rows] * 2,
         compiler_params=params(),
-    )(message, message, theirs)
+    )(held(message), held(theirs))
 
 
 def to_heads(message):
@@ -335,16 +339,16 @@
 ):
     count = query.shape[0]
     blocks = key_codes.shape[0]
-    large = count * 2 // 3
+    large = count * 3 // 4
     small = count - large
     swap = [(0, 1), (1, 0)]
     group = lax.axis_index("grp")
     mine = lax.dynamic_slice_in_dim(pairing, group * count, count, 0)
     pairs = ((mine + blocks * group) % (2 * blocks)).reshape(-1)
     codes = (key_codes, key_scale, value_codes, value_scale)
-    send0 = pack(query, out_grad, forward_out, 0, large, 6, codes)
+    send0 = pack(query, out_grad, forward_out, 0, large, large, codes)
     got0 = to_heads(send0)
-    send1 = pack(query, out_grad, forward_out, large, small, 6)
+    send1 = pack(query, out_grad, forward_out, large, small, small)
     got1 = to_heads(send1)
     kv_own = got0[:, 2 * large + 1 :]
     kv_other = lax.ppermute(kv_own, "grp", swap)

time: 190 us -> 181 us (0.953)
  Pallas kernels: 48 us -> 39.8 us
  local copies, waits for them, and re-layouts: 7.61 us -> 1.88 us
  waiting for transfers between devices: 64.9 us -> 69.9 us
    unnamed x14 -> x2, local copies, waits for them, and re-layouts: 5.73 us -> 0.01 us
    all_to_all x2, waiting for transfers between devices: 41.5 us -> 46.7 us  [to_heads(): lax.all_to_all(message, 'head', split_axis=0, concat_axis=0, tiled=True)]
    ppermute x1, waiting for transfers between devices: 22.5 us -> 18.5 us  [on_device(): kv_other = lax.ppermute(kv_own, 'grp', swap)]
    ppermute x1, waiting for transfers between devices: 0.82 us -> 4.64 us  [on_device(): theirs = lax.ppermute(back[:, count + 2 * blocks:], 'grp', swap)]
    pallas_call x2, Pallas kernels: 7.12 us -> 3.61 us  [the longest x1 2.81 us: unpack(): pl.pallas_call(body, name='unpack', grid=(count // step,), in_specs=[HELD...]
    pallas_call x2, Pallas kernels: 29.4 us -> 27.1 us  [attend(): pl.pallas_call(body, grid_spec=pltpu.PrefetchScalarGridSpec(num_scalar_pr...]
    pallas_call x2, Pallas kernels: 11.4 us -> 9.1 us  [pack(): pl.pallas_call(body, grid=(steps,), in_specs=in_specs, out_specs=pl.Block...]
  transfers between devices with their start and end apart: 4 -> 4, of which waited for: 3 -> 3; matrix products, arithmetic and copies ran while one was open for 1% -> 1% of each run, Pallas kernels for 15% -> 14%
where the time goes in v3:
time: 181 us
  waiting for transfers between devices  69.9 us (39%)
  blocking collectives  49.8 us (28%)
  Pallas kernels  39.8 us (22%)
  starting transfers between devices  18.5 us (10%)
  local copies, waits for them, and re-layouts  1.88 us (1%)
    all_to_all x1, blocking collectives, to_heads(): lax.all_to_all(message, 'head', split_axis=0, concat_axis=0, tiled=True)  49.8 us
    all_to_all x2, waiting for transfers between devices, to_heads(): lax.all_to_all(message, 'head', split_axis=0, concat_axis=0, tiled=True)  46.7 us
    pallas_call x2, Pallas kernels, attend(): pl.pallas_call(body, grid_spec=pltpu.PrefetchScalarGridSpec(num_scalar_pr...  27.1 us
    ppermute x1, waiting for transfers between devices, on_device(): kv_other = lax.ppermute(kv_own, 'grp', swap)  18.5 us
    all_to_all x2, starting transfers between devices, to_heads(): lax.all_to_all(message, 'head', split_axis=0, concat_axis=0, tiled=True)  17.6 us
    pallas_call x2, Pallas kernels, pack(): pl.pallas_call(body, grid=(steps,), in_specs=in_specs, out_specs=pl.Block...  9.1 us
    ppermute x1, waiting for transfers between devices, on_device(): theirs = lax.ppermute(back[:, count + 2 * blocks:], 'grp', swap)  4.64 us
  transfers between devices with their start and end apart: 4, of which 3 were waited for; matrix products, arithmetic and copies ran while one was open for 1% of the time, Pallas kernels for 14%

profile of v3, /device:TPU:1, one launch (start us, length us, event | category | flops | bytes accessed | tf_op | source)
XLA Modules:
  0.0 180.7 jit_solution(13194846528497089267)
XLA Ops:
  0.6 6.1 %shard_map.104 = bf16[64,59,4,128]{3,2,1,0:T(4,128)(2,1)} custom-call(bf16[36,4,8192]{2,1,0:T(4,128)(2,1)} %refs_0_.3, bf16[36,4,8192]{2,1,0:T(4,128)(2,1)} %refs_1_.3, bf16[36,4,8192]{2,1,0:T(4,128)(2,1)} %refs_2_.3, bf16[2,4,8192]{2,1,0:T(4,128)(2,1)} %refs_3_.1, bf16[2,4,64]{2,1,0:T(4,128)(2,1)} %refs_4_.1, bf16[2,4,8192]{2,1,0:T(4,128)(2,1)} %refs_5_.1, ...), custom_call_target="tpu_custom_call" | custom-call | tf_op jit(solution)/shard_map/pallas_call | solution.py:114
  6.7 12.5 %all-to-all-start.1 = ((bf16[64,59,4,128]{3,2,1,0:T(4,128)(2,1)}), bf16[64,59,4,128]{3,2,1,0:T(4,128)(2,1)}, u32[]{:S(2)}, u32[]{:S(2)}) async-start(bf16[64,59,4,128]{3,2,1,0:T(4,128)(2,1)} %shard_map.104), calls=%async_computation.1 | async-start | bytes 7733248 | tf_op jit(solution)/shard_map/all_to_all | solution.py:334
  19.2 3.0 %shard_map.103 = bf16[64,19,4,128]{3,2,1,0:T(4,128)(2,1)} custom-call(bf16[36,4,8192]{2,1,0:T(4,128)(2,1)} %refs_0_.3, bf16[36,4,8192]{2,1,0:T(4,128)(2,1)} %refs_1_.3, bf16[36,4,8192]{2,1,0:T(4,128)(2,1)} %refs_2_.3), custom_call_target="tpu_custom_call" | custom-call | tf_op jit(solution)/shard_map/pallas_call | solution.py:114
  22.2 0.0 copy-start
  22.2 46.7 %all-to-all-done.1.m_ref = bf16[64,59,4,128]{3,2,1,0:T(4,128)(2,1)} async-done(((bf16[64,59,4,128]{3,2,1,0:T(4,128)(2,1)}), bf16[64,59,4,128]{3,2,1,0:T(4,128)(2,1)}, u32[]{:S(2)}, u32[]{:S(2)}) %all-to-all-start.1) | async-done | bytes 3866656 | tf_op jit(solution)/shard_map/all_to_all | solution.py:334
  69.0 5.1 %all-to-all-start = ((bf16[64,19,4,128]{3,2,1,0:T(4,128)(2,1)}), bf16[64,19,4,128]{3,2,1,0:T(4,128)(2,1)S(1)}, u32[]{:S(2)}, u32[]{:S(2)}) async-start(bf16[64,19,4,128]{3,2,1,0:T(4,128)(2,1)} %shard_map.103), calls=%async_computation | async-start | bytes 2490368 | tf_op jit(solution)/shard_map/all_to_all | solution.py:334
  74.1 1.1 slice.8.own_ref
  75.2 0.8 collective-permute-start
  76.0 0.0 copy-done
  76.0 0.1 and_select_fusion
  76.1 0.1 copy.13
  76.2 0.6 reshape.9.pair_ref
  76.8 18.5 %collective-permute-done.other_ref = bf16[64,4,4,128]{3,2,1,0:T(4,128)(2,1)S(1)} collective-permute-done((bf16[64,4,4,128]{3,2,1,0:T(4,128)(2,1)S(1)}, bf16[64,4,4,128]{3,2,1,0:T(4,128)(2,1)S(1)}, u32[]{:S(2)}, u32[]{:S(2)}) %collective-permute-start) | collective-permute-done | bytes 262176 | tf_op jit(solution)/shard_map/ppermute | solution.py:354
  95.3 19.5 %shard_map.105 = (bf16[64,44,4,128]{3,2,1,0:T(4,128)(2,1)}, f32[2,4,256,128]{3,2,1,0:T(8,128)S(1)}) custom-call(s32[72]{0:T(128)} %reshape.9.pair_ref, bf16[64,59,4,128]{3,2,1,0:T(4,128)(2,1)} %all-to-all-done.1.m_ref, bf16[64,4,4,128]{3,2,1,0:T(4,128)(2,1)S(1)} %slice.8.own_ref, bf16[64,4,4,128]{3,2,1,0:T(4,128)(2,1)S(1)} %collective-permute-done.other_ref), custom_call_target="tpu_custom_call" | custom-call | flops 4529848320 | bytes 6291456 | tf_op jit(solution)/shard_map/pallas_call | solution.py:271
  114.9 0.0 all-to-all-done.m_ref
  114.9 7.5 %shard_map.106 = bf16[64,44,4,128]{3,2,1,0:T(4,128)(2,1)} custom-call(s32[72]{0:T(128)} %reshape.9.pair_ref, bf16[64,19,4,128]{3,2,1,0:T(4,128)(2,1)S(1)} %all-to-all-done.m_ref, bf16[64,4,4,128]{3,2,1,0:T(4,128)(2,1)S(1)} %slice.8.own_ref, bf16[64,4,4,128]{3,2,1,0:T(4,128)(2,1)S(1)} %collective-permute-done.other_ref, ...), custom_call_target="tpu_custom_call", output_to_operand_aliasing={{}: (5, {})} | custom-call | flops 1509949440 | bytes 6291456 | tf_op jit(solution)/shard_map/pallas_call | solution.py:271
  122.4 49.8 %all_to_all.15.m_ref = bf16[64,44,4,128]{3,2,1,0:T(4,128)(2,1)S(1)} all-to-all(bf16[64,44,4,128]{3,2,1,0:T(4,128)(2,1)} %shard_map.106), channel_id=1, replica_groups=mesh['grp'=2,'head'=64] {'head'}, dimensions={0} | all-to-all | bytes 5767168 | tf_op jit(solution)/shard_map/all_to_all | solution.py:334
  172.2 0.1 slice.9
  172.3 0.1 collective-permute-start.1
  172.4 2.8 %unpack.1 = bf16[36,4,8192]{2,1,0:T(4,128)(2,1)} custom-call(bf16[64,44,4,128]{3,2,1,0:T(4,128)(2,1)S(1)} %all_to_all.15.m_ref), custom_call_target="tpu_custom_call" | custom-call | tf_op jit(solution)/shard_map/unpack/pallas_call | solution.py:298
  175.2 4.6 %collective-permute-done.1.t_ref = bf16[64,4,4,128]{3,2,1,0:T(4,128)(2,1)S(1)} collective-permute-done((bf16[64,4,4,128]{3,2,1,0:T(4,128)(2,1)S(1)}, bf16[64,4,4,128]{3,2,1,0:T(4,128)(2,1)S(1)}, u32[]{:S(2)}, u32[]{:S(2)}) %collective-permute-start.1) | collective-permute-done | bytes 262176 | tf_op jit(solution)/shard_map/ppermute | solution.py:359
  179.9 0.8 unpack_sums.1
Async XLA Ops:
  6.7 62.2 %all-to-all-start.1 = ((bf16[64,59,4,128]{3,2,1,0:T(4,128)(2,1)}), bf16[64,59,4,128]{3,2,1,0:T(4,128)(2,1)}, u32[]{:S(2)}, u32[]{:S(2)}) async-start(bf16[64,59,4,128]{3,2,1,0:T(4,128)(2,1)} %shard_map.104), calls=%async_computation.1 | async-start | bytes 7733248 | tf_op jit(solution)/shard_map/all_to_all | solution.py:334
  22.2 53.8 %copy-start = (s32[72,2]{0,1:T(2,128)S(1)}, s32[72,2]{0,1:T(2,128)}, u32[]{:S(2)}) copy-start(s32[72,2]{0,1:T(2,128)} %param.15) | copy-start | bytes 1732
  69.0 45.9 %all-to-all-start = ((bf16[64,19,4,128]{3,2,1,0:T(4,128)(2,1)}), bf16[64,19,4,128]{3,2,1,0:T(4,128)(2,1)S(1)}, u32[]{:S(2)}, u32[]{:S(2)}) async-start(bf16[64,19,4,128]{3,2,1,0:T(4,128)(2,1)} %shard_map.103), calls=%async_computation | async-start | bytes 2490368 | tf_op jit(solution)/shard_map/all_to_all | solution.py:334
  75.2 20.2 %collective-permute-start = (bf16[64,4,4,128]{3,2,1,0:T(4,128)(2,1)S(1)}, bf16[64,4,4,128]{3,2,1,0:T(4,128)(2,1)S(1)}, u32[]{:S(2)}, u32[]{:S(2)}) collective-permute-start(bf16[64,4,4,128]{3,2,1,0:T(4,128)(2,1)S(1)} %slice.8.own_ref), channel_id=1, source_target_pairs={{0,64},{64,0},{1,65},{65,1},{2,66},{66,2},{3,67},{67,3},{4,68},{68... | collective-permute-start | bytes 786440 | tf_op jit(solution)/shard_map/ppermute | solution.py:354
  172.3 7.6 %collective-permute-start.1 = (bf16[64,4,4,128]{3,2,1,0:T(4,128)(2,1)S(1)}, bf16[64,4,4,128]{3,2,1,0:T(4,128)(2,1)S(1)}, u32[]{:S(2)}, u32[]{:S(2)}) collective-permute-start(bf16[64,4,4,128]{3,2,1,0:T(4,128)(2,1)S(1)} %slice.9), channel_id=1, source_target_pairs={{0,64},{64,0},{1,65},{65,1},{2,66},{66,2},{3,67},{67,3},{4,68},{68... | collective-permute-start | bytes 786440 | tf_op jit(solution)/shard_map/ppermute | solution.py:359

commit v4 on v3

--- a/solution.py
+++ b/solution.py
@@ -130,7 +130,7 @@
     return jnp.dot(a, b, preferred_element_type=jnp.float32)
 
 
-def attend(pairs, message, kv_own, kv_other, first, count, total_out, sums=None, into=None):
+def attend(pairs, message, kv_own, kv_other, first, count, sums=None, extra=0):
     srcs, _, toks, _ = message.shape
     length = srcs * toks
     blocks = kv_own.shape[1] // 2
@@ -139,8 +139,8 @@
 
     def body(pair_ref, m_ref, own_ref, other_ref, *refs):
         if last:
-            sum_ref, _, target = refs[:3]
-            refs, (key_acc, value_acc, out_ref, sems) = refs[3:-4], refs[-4:]
+            sum_ref, out_ref, own_sum, other_sum = refs[:4]
+            refs, (key_acc, value_acc) = refs[4:-2], refs[-2:]
         else:
             out_ref, sum_out = refs[:2]
             refs = refs[2:]
@@ -225,22 +225,15 @@
         lax.fori_loop(0, count // SLOTS, several, 0)
         grads_of(count - 1, SLOTS - 1)
         if last:
-            for b in range(total):
-                at = count + (b // blocks) * 2 * blocks + b % blocks
-                key_rows = (key_acc[b] * SCALE).astype(jnp.bfloat16)
-                out_ref[:, at] = key_rows.reshape(srcs, toks, HD)
-                value_rows = value_acc[b].astype(jnp.bfloat16)
-                out_ref[:, at + blocks] = value_rows.reshape(srcs, toks, HD)
-            copy = pltpu.make_async_copy(
-                out_ref, target.at[:, pl.ds(first, count + 2 * total)], sems.at[0]
-            )
-            copy.start()
-            copy.wait()
+            own_sum[0] = key_acc[:blocks] * SCALE
+            own_sum[1] = value_acc[:blocks]
+            other_sum[0] = (key_acc[blocks:] * SCALE).astype(jnp.bfloat16)
+            other_sum[1] = value_acc[blocks:].astype(jnp.bfloat16)
 
     def whole(shape):
         return pl.BlockSpec(shape, lambda i, p: (0,) * len(shape))
 
-    dq = jax.ShapeDtypeStruct((srcs, total_out, toks, HD), jnp.bfloat16)
+    dq = jax.ShapeDtypeStruct((srcs, count + extra, toks, HD), jnp.bfloat16)
     dq_spec = whole((srcs, count, toks, HD))
     acc = (2, total, length, HD)
     scratch = [
@@ -254,16 +247,13 @@
     scratch += [pltpu.VMEM((length, HD), jnp.bfloat16)] * (2 * SLOTS)
     in_specs = [HELD if last else whole(message.shape), HELD, HELD]
     args = [held(message) if last else message, held(kv_own), held(kv_other)]
-    aliases = {}
     if last:
-        out_shape = dq
-        out_specs = pl.BlockSpec(memory_space=pl.ANY)
+        part = (2, blocks, length, HD)
+        out_shape = (dq, pltpu.VMEM(part, jnp.float32), pltpu.VMEM(part, jnp.bfloat16))
+        out_specs = [dq_spec, HELD, HELD]
         scratch += [pltpu.VMEM((total, length, HD), jnp.float32)] * 2
-        scratch.append(pltpu.VMEM((srcs, count + 2 * total, toks, HD), jnp.bfloat16))
-        scratch.append(pltpu.SemaphoreType.DMA((1,)))
-        in_specs += [HELD, pl.BlockSpec(memory_space=pl.ANY)]
-        args += [held(sums), into]
-        aliases = {len(args): 0}
+        in_specs.append(HELD)
+        args.append(held(sums))
     else:
         out_shape = (dq, pltpu.VMEM(acc, jnp.float32))
         out_specs = [dq_spec, HELD]
@@ -278,7 +268,6 @@
             scratch_shapes=scratch,
         ),
         out_shape=out_shape,
-        input_output_aliases=aliases,
         compiler_params=params(),
         cost_estimate=pl.CostEstimate(
             flops=flops, transcendentals=2 * count * length * length, bytes_accessed=6 << 20
@@ -286,48 +275,64 @@
     )(pairs, *args)
 
 
-def unpack(message, count, step):
+def combine(message, own_sum, other_sum, count):
+    srcs, _, toks, _ = message.shape
+    blocks = own_sum.shape[1]
+
+    def body(_, own_ref, other_ref, out_ref):
+        which = pl.program_id(0)
+        for b in range(blocks):
+            value = own_ref[which, b] + other_ref[which, b].astype(jnp.float32)
+            out_ref[:, b] = value.astype(jnp.bfloat16).reshape(srcs, toks, HD)
+
+    return pl.pallas_call(
+        body,
+        name="combine",
+        grid=(2,),
+        in_specs=[pl.BlockSpec(memory_space=pl.ANY), HELD, HELD],
+        out_specs=pl.BlockSpec((srcs, blocks, toks, HD), lambda i: (0, count // blocks + i, 0, 0)),
+        out_shape=jax.ShapeDtypeStruct(message.shape, message.dtype),
+        input_output_aliases={0: 0},
+        compiler_params=params(),
+    )(message, held(own_sum), held(other_sum))
+
+
+def unpack(message, total, first, count, step, into=None, blocks=0):
     heads, _, toks, _ = message.shape
     width = heads * HD
-
-    def body(m_ref, out_ref):
-        first = pl.program_id(0) * step
+    start = first // step
+
+    def body(m_ref, *refs):
+        out_ref, *sums = refs if into is None else refs[1:]
+        at = pl.program_id(0) * step
         for h in range(heads):
-            out_ref[:, :, h * HD : (h + 1) * HD] = m_ref[h, pl.ds(first, step)]
-
+            out_ref[:, :, h * HD : (h + 1) * HD] = m_ref[h, pl.ds(at, step)]
+        for which, out in enumerate(sums):
+            behind = count + which * blocks
+            for h in range(heads):
+                out[:, :, h * HD : (h + 1) * HD] = m_ref[h, behind : behind + blocks]
+
+    in_specs = [HELD]
+    args = [held(message)]
+    out_shape = [jax.ShapeDtypeStruct((total, toks, width), message.dtype)]
+    out_specs = [pl.BlockSpec((step, toks, width), lambda i: (start + i, 0, 0))]
+    if blocks:
+        out_shape += [jax.ShapeDtypeStruct((blocks, toks, width), message.dtype)] * 2
+        out_specs += [pl.BlockSpec((blocks, toks, width), lambda i: (0, 0, 0))] * 2
+    aliases = {}
+    if into is not None:
+        in_specs.append(pl.BlockSpec(memory_space=pl.ANY))
+        args.append(into)
+        aliases = {1: 0}
     return pl.pallas_call(
         body,
-        name="unpack",
         grid=(count // step,),
-        in_specs=[HELD],
-        out_specs=pl.BlockSpec((step, toks, width), lambda i: (i, 0, 0)),
-        out_shape=jax.ShapeDtypeStruct((count, toks, width), message.dtype),
+        in_specs=in_specs,
+        out_specs=out_specs,
+        out_shape=out_shape,
+        input_output_aliases=aliases,
         compiler_params=params(),
-    )(held(message))
-
-
-def unpack_sums(message, theirs, first, blocks):
-    heads, _, toks, _ = message.shape
-    width = heads * HD
-
-    def body(m_ref, t_ref, *outs):
-        for which, out in enumerate(outs):
-            at = which * blocks
-            for h in range(heads):
-                total = m_ref[h, first + at : first + at + blocks].astype(jnp.float32)
-                total += t_ref[h, at : at + blocks].astype(jnp.float32)
-                out[:, :, h * HD : (h + 1) * HD] = total.astype(jnp.bfloat16)
-
-    rows = jax.ShapeDtypeStruct((blocks, toks, width), message.dtype)
-    return pl.pallas_call(
-        body,
-        name="unpack_sums",
-        grid=(1,),
-        in_specs=[HELD] * 2,
-        out_specs=[pl.BlockSpec((blocks, toks, width), lambda i: (0, 0, 0))] * 2,
-        out_shape=[rows] * 2,
-        compiler_params=params(),
-    )(held(message), held(theirs))
+    )(*args)
 
 
 def to_heads(message):
@@ -339,7 +344,7 @@
 ):
     count = query.shape[0]
     blocks = key_codes.shape[0]
-    large = count * 3 // 4
+    large = count * 2 // 3
     small = count - large
     swap = [(0, 1), (1, 0)]
     group = lax.axis_index("grp")
@@ -348,18 +353,21 @@
     codes = (key_codes, key_scale, value_codes, value_scale)
     send0 = pack(query, out_grad, forward_out, 0, large, large, codes)
     got0 = to_heads(send0)
-    send1 = pack(query, out_grad, forward_out, large, small, small)
+    later, pairs = lax.optimization_barrier((forward_out, pairs))
+    send1 = pack(query, out_grad, later, large, small, small)
     got1 = to_heads(send1)
     kv_own = got0[:, 2 * large + 1 :]
     kv_other = lax.ppermute(kv_own, "grp", swap)
-    slots = count + 4 * blocks
-    grads, sums = attend(pairs, got0, kv_own, kv_other, 0, large, slots)
-    grads = attend(pairs, got1, kv_own, kv_other, large, small, slots, sums, grads)
-    back = to_heads(grads)
-    theirs = lax.ppermute(back[:, count + 2 * blocks :], "grp", swap)
-    rows = unpack(back, count, 6)
-    key_rows, value_rows = unpack_sums(back, theirs, count, blocks)
-    return rows, key_rows, value_rows
+    grads0, sums = attend(pairs, got0, kv_own, kv_other, 0, large)
+    back0 = to_heads(grads0)
+    grads1, own_sum, other_sum = attend(
+        pairs, got1, kv_own, kv_other, large, small, sums, extra=2 * blocks
+    )
+    theirs = lax.ppermute(other_sum, "grp", swap)
+    grads1 = combine(grads1, own_sum, theirs, small)
+    back1 = to_heads(grads1)
+    (rows,) = unpack(back0, count, 0, large, 6)
+    return unpack(back1, count, large, small, small, into=rows, blocks=blocks)
 
 
 def solution(mesh):

time: 181 us -> 183 us (1.011)
  blocking collectives: 49.8 us -> 0 us
  waiting for transfers between devices: 69.9 us -> 96.1 us
  starting transfers between devices: 18.5 us -> 38.1 us
  local copies, waits for them, and re-layouts: 1.88 us -> 7.39 us
    all_to_all x1 -> x0, blocking collectives: 49.8 us -> none  [to_heads(): lax.all_to_all(message, 'head', split_axis=0, concat_axis=0, tiled=True)]
    all_to_all x2 -> x4, starting transfers between devices: 17.6 us -> 37.3 us  [to_heads(): lax.all_to_all(message, 'head', split_axis=0, concat_axis=0, tiled=True)]
    all_to_all x2 -> x4, waiting for transfers between devices: 46.7 us -> 59 us  [to_heads(): lax.all_to_all(message, 'head', split_axis=0, concat_axis=0, tiled=True)]
    ppermute x1, waiting for transfers between devices: 4.64 us -> 13.7 us  [on_device(): theirs = lax.ppermute(other_sum, 'grp', swap)]
    unnamed x2 -> x12, local copies, waits for them, and re-layouts: 0.01 us -> 5.61 us
    ppermute x1, waiting for transfers between devices: 18.5 us -> 23.4 us  [on_device(): kv_other = lax.ppermute(kv_own, 'grp', swap)]
    pallas_call x2 -> x3, Pallas kernels: 3.61 us -> 4.14 us  [the longest x2 3.35 us: unpack(): pl.pallas_call(body, grid=(count // step,), in_specs=in_specs, out_specs=...]
  transfers between devices with their start and end apart: 4 -> 6, of which waited for: 3 -> 4; matrix products, arithmetic and copies ran while one was open for 1% -> 1% of each run, Pallas kernels for 14% -> 18%
where the time goes in v4:
time: 183 us; the launch traced here: 182 us
  waiting for transfers between devices  96.1 us (53%)
  Pallas kernels  39.7 us (22%)
  starting transfers between devices  38.1 us (21%)
  local copies, waits for them, and re-layouts  7.39 us (4%)
    all_to_all x4, waiting for transfers between devices, to_heads(): lax.all_to_all(message, 'head', split_axis=0, concat_axis=0, tiled=True)  59 us
    all_to_all x4, starting transfers between devices, to_heads(): lax.all_to_all(message, 'head', split_axis=0, concat_axis=0, tiled=True)  37.3 us
    pallas_call x2, Pallas kernels, attend(): pl.pallas_call(body, grid_spec=pltpu.PrefetchScalarGridSpec(num_scalar_pr...  26.6 us
    ppermute x1, waiting for transfers between devices, on_device(): kv_other = lax.ppermute(kv_own, 'grp', swap)  23.4 us
    ppermute x1, waiting for transfers between devices, on_device(): theirs = lax.ppermute(other_sum, 'grp', swap)  13.7 us
    pallas_call x2, Pallas kernels, pack(): pl.pallas_call(body, grid=(steps,), in_specs=in_specs, out_specs=pl.Block...  8.96 us
    unnamed x12, local copies, waits for them, and re-layouts  5.61 us
  transfers between devices with their start and end apart: 6, of which 4 were waited for; matrix products, arithmetic and copies ran while one was open for 1% of the time, Pallas kernels for 18%

profile of v4, /device:TPU:1, one launch (start us, length us, event | category | flops | bytes accessed | tf_op | source)
XLA Modules:
  0.0 182.1 jit_solution(963296201469962739)
XLA Ops:
  0.6 5.6 %shard_map.104 = bf16[64,53,4,128]{3,2,1,0:T(4,128)(2,1)} custom-call(bf16[36,4,8192]{2,1,0:T(4,128)(2,1)} %refs_0_.3, bf16[36,4,8192]{2,1,0:T(4,128)(2,1)} %refs_1_.3, bf16[36,4,8192]{2,1,0:T(4,128)(2,1)} %refs_2_.2, bf16[2,4,8192]{2,1,0:T(4,128)(2,1)} %refs_3_.1, bf16[2,4,64]{2,1,0:T(4,128)(2,1)} %refs_4_.1, bf16[2,4,8192]{2,1,0:T(4,128)(2,1)} %refs_5_.1, ...), custom_call_target="tpu_custom_call" | custom-call | tf_op jit(solution)/shard_map/pallas_call | solution.py:114
  6.3 12.3 %all-to-all-start.1 = ((bf16[64,53,4,128]{3,2,1,0:T(4,128)(2,1)}), bf16[64,53,4,128]{3,2,1,0:T(4,128)(2,1)S(1)}, u32[]{:S(2)}, u32[]{:S(2)}) async-start(bf16[64,53,4,128]{3,2,1,0:T(4,128)(2,1)} %shard_map.104), calls=%async_computation.1 | async-start | bytes 6946816 | tf_op jit(solution)/shard_map/all_to_all | solution.py:339
  18.7 0.1 copy.14
  18.8 0.6 reshape.9.pair_ref
  19.4 3.3 %shard_map.103 = bf16[64,25,4,128]{3,2,1,0:T(4,128)(2,1)} custom-call(bf16[36,4,8192]{2,1,0:T(4,128)(2,1)} %refs_0_.3, bf16[36,4,8192]{2,1,0:T(4,128)(2,1)} %refs_1_.3, bf16[36,4,8192]{2,1,0:T(4,128)(2,1)} %refs_2_.2), custom_call_target="tpu_custom_call" | custom-call | tf_op jit(solution)/shard_map/pallas_call | solution.py:114
  22.8 41.4 %all-to-all-done.1.m_ref = bf16[64,53,4,128]{3,2,1,0:T(4,128)(2,1)S(1)} async-done(((bf16[64,53,4,128]{3,2,1,0:T(4,128)(2,1)}), bf16[64,53,4,128]{3,2,1,0:T(4,128)(2,1)S(1)}, u32[]{:S(2)}, u32[]{:S(2)}) %all-to-all-start.1) | async-done | bytes 3473440 | tf_op jit(solution)/shard_map/all_to_all | solution.py:339
  64.2 1.7 copy-done.4
  65.9 4.8 %all-to-all-start = ((bf16[64,25,4,128]{3,2,1,0:T(4,128)(2,1)}), bf16[64,25,4,128]{3,2,1,0:T(4,128)(2,1)S(1)}, u32[]{:S(2)}, u32[]{:S(2)}) async-start(bf16[64,25,4,128]{3,2,1,0:T(4,128)(2,1)} %shard_map.103), calls=%async_computation | async-start | bytes 3276800 | tf_op jit(solution)/shard_map/all_to_all | solution.py:339
  70.7 1.1 slice.4.own_ref
  71.8 0.8 collective-permute-start
  72.6 23.4 %collective-permute-done.other_ref = bf16[64,4,4,128]{3,2,1,0:T(4,128)(2,1)S(1)} collective-permute-done((bf16[64,4,4,128]{3,2,1,0:T(4,128)(2,1)S(1)}, bf16[64,4,4,128]{3,2,1,0:T(4,128)(2,1)S(1)}, u32[]{:S(2)}, u32[]{:S(2)}) %collective-permute-start) | collective-permute-done | bytes 262176 | tf_op jit(solution)/shard_map/ppermute | solution.py:360
  96.0 17.6 %shard_map.105 = (bf16[64,24,4,128]{3,2,1,0:T(4,128)(2,1)}, f32[2,4,256,128]{3,2,1,0:T(8,128)S(1)}) custom-call(s32[72]{0:T(128)} %reshape.9.pair_ref, bf16[64,53,4,128]{3,2,1,0:T(4,128)(2,1)} %copy-done.4, bf16[64,4,4,128]{3,2,1,0:T(4,128)(2,1)S(1)} %slice.4.own_ref, bf16[64,4,4,128]{3,2,1,0:T(4,128)(2,1)S(1)} %collective-permute-done.other_ref), custom_call_target="tpu_custom_call" | custom-call | flops 4026531840 | bytes 6291456 | tf_op jit(solution)/shard_map/pallas_call | solution.py:261
  113.6 0.7 copy-done
  114.3 1.0 copy-done.2
  115.3 10.8 %all-to-all-start.3 = ((bf16[64,24,4,128]{3,2,1,0:T(4,128)(2,1)}), bf16[64,24,4,128]{3,2,1,0:T(4,128)(2,1)S(1)}, u32[]{:S(2)}, u32[]{:S(2)}) async-start(bf16[64,24,4,128]{3,2,1,0:T(4,128)(2,1)} %get-tuple-element.16), calls=%async_computation.3 | async-start | bytes 3145728 | tf_op jit(solution)/shard_map/all_to_all | solution.py:339
  126.2 0.9 copy-done.1
  127.1 1.2 copy-done.3
  128.3 9.0 %shard_map.106 = (bf16[64,16,4,128]{3,2,1,0:T(4,128)(2,1)}, f32[2,2,256,128]{3,2,1,0:T(8,128)S(1)}, bf16[2,2,256,128]{3,2,1,0:T(8,128)(2,1)S(1)}) custom-call(s32[72]{0:T(128)} %reshape.9.pair_ref, bf16[64,25,4,128]{3,2,1,0:T(4,128)(2,1)S(1)} %all-to-all-done.m_ref, bf16[64,4,4,128]{3,2,1,0:T(4,128)(2,1)S(1)} %slice.4.own_ref, ...), custom_call_target="tpu_custom_call" | custom-call | flops 2013265920 | bytes 6291456 | tf_op jit(solution)/shard_map/pallas_call | solution.py:261
  137.3 13.7 %collective-permute-done.1.other_ref = bf16[2,2,256,128]{3,2,1,0:T(8,128)(2,1)S(1)} collective-permute-done((bf16[2,2,256,128]{3,2,1,0:T(8,128)(2,1)S(1)}, bf16[2,2,256,128]{3,2,1,0:T(8,128)(2,1)S(1)}, u32[]{:S(2)}, u32[]{:S(2)}) %collective-permute-start.1) | collective-permute-done | bytes 262176 | tf_op jit(solution)/shard_map/ppermute | solution.py:366
  151.0 0.8 combine.1
  151.8 9.3 %all-to-all-start.2 = ((bf16[64,16,4,128]{3,2,1,0:T(4,128)(2,1)}), bf16[64,16,4,128]{3,2,1,0:T(4,128)(2,1)S(1)}, u32[]{:S(2)}, u32[]{:S(2)}) async-start(bf16[64,16,4,128]{3,2,1,0:T(4,128)(2,1)} %combine.1), calls=%async_computation.2 | async-start | bytes 2097152 | tf_op jit(solution)/shard_map/all_to_all | solution.py:339
  161.1 1.9 %shard_map.107.refs_0_ = bf16[36,4,8192]{2,1,0:T(4,128)(2,1)} custom-call(bf16[64,24,4,128]{3,2,1,0:T(4,128)(2,1)S(1)} %all-to-all-done.3.m_ref), custom_call_target="tpu_custom_call" | custom-call | tf_op jit(solution)/shard_map/pallas_call | solution.py:327
  163.1 17.6 %all-to-all-done.2.m_ref = bf16[64,16,4,128]{3,2,1,0:T(4,128)(2,1)S(1)} async-done(((bf16[64,16,4,128]{3,2,1,0:T(4,128)(2,1)}), bf16[64,16,4,128]{3,2,1,0:T(4,128)(2,1)S(1)}, u32[]{:S(2)}, u32[]{:S(2)}) %all-to-all-start.2) | async-done | bytes 1048608 | tf_op jit(solution)/shard_map/all_to_all | solution.py:339
  180.7 1.4 shard_map.108
  (11 shorter events, 0.1 us)
Async XLA Ops:
  6.3 12.3 %copy-start.5 = (s32[72,2]{0,1:T(2,128)S(1)}, s32[72,2]{0,1:T(2,128)}, u32[]{:S(2)}) copy-start(s32[72,2]{0,1:T(2,128)} %param.15) | copy-start | bytes 1732
  6.3 57.9 %all-to-all-start.1 = ((bf16[64,53,4,128]{3,2,1,0:T(4,128)(2,1)}), bf16[64,53,4,128]{3,2,1,0:T(4,128)(2,1)S(1)}, u32[]{:S(2)}, u32[]{:S(2)}) async-start(bf16[64,53,4,128]{3,2,1,0:T(4,128)(2,1)} %shard_map.104), calls=%async_computation.1 | async-start | bytes 6946816 | tf_op jit(solution)/shard_map/all_to_all | solution.py:339
  64.2 1.7 copy-start.4
  65.9 49.4 %all-to-all-start = ((bf16[64,25,4,128]{3,2,1,0:T(4,128)(2,1)}), bf16[64,25,4,128]{3,2,1,0:T(4,128)(2,1)S(1)}, u32[]{:S(2)}, u32[]{:S(2)}) async-start(bf16[64,25,4,128]{3,2,1,0:T(4,128)(2,1)} %shard_map.103), calls=%async_computation | async-start | bytes 3276800 | tf_op jit(solution)/shard_map/all_to_all | solution.py:339
  71.8 24.2 %collective-permute-start = (bf16[64,4,4,128]{3,2,1,0:T(4,128)(2,1)S(1)}, bf16[64,4,4,128]{3,2,1,0:T(4,128)(2,1)S(1)}, u32[]{:S(2)}, u32[]{:S(2)}) collective-permute-start(bf16[64,4,4,128]{3,2,1,0:T(4,128)(2,1)S(1)} %slice.4.own_ref), channel_id=1, source_target_pairs={{0,64},{64,0},{1,65},{65,1},{2,66},{66,2},{3,67},{67,3},{4,68},{68... | collective-permute-start | bytes 786440 | tf_op jit(solution)/shard_map/ppermute | solution.py:360
  113.6 0.7 copy-start
  114.3 1.0 copy-start.2
  115.3 36.5 %all-to-all-start.3 = ((bf16[64,24,4,128]{3,2,1,0:T(4,128)(2,1)}), bf16[64,24,4,128]{3,2,1,0:T(4,128)(2,1)S(1)}, u32[]{:S(2)}, u32[]{:S(2)}) async-start(bf16[64,24,4,128]{3,2,1,0:T(4,128)(2,1)} %get-tuple-element.16), calls=%async_computation.3 | async-start | bytes 3145728 | tf_op jit(solution)/shard_map/all_to_all | solution.py:339
  126.2 1.0 copy-start.1
  127.1 1.2 copy-start.3
  137.3 13.7 %collective-permute-start.1 = (bf16[2,2,256,128]{3,2,1,0:T(8,128)(2,1)S(1)}, bf16[2,2,256,128]{3,2,1,0:T(8,128)(2,1)S(1)}, u32[]{:S(2)}, u32[]{:S(2)}) collective-permute-start(bf16[2,2,256,128]{3,2,1,0:T(8,128)(2,1)S(1)} %get-tuple-element.15), channel_id=1, source_target_pairs={{0,64},{64,0},{1,65},{65,1},{2,66},{66,2},{3,67},{67,3},{4,68},{68... | collective-permute-start | bytes 786440 | tf_op jit(solution)/shard_map/ppermute | solution.py:366
  151.8 28.9 %all-to-all-start.2 = ((bf16[64,16,4,128]{3,2,1,0:T(4,128)(2,1)}), bf16[64,16,4,128]{3,2,1,0:T(4,128)(2,1)S(1)}, u32[]{:S(2)}, u32[]{:S(2)}) async-start(bf16[64,16,4,128]{3,2,1,0:T(4,128)(2,1)} %combine.1), calls=%async_computation.2 | async-start | bytes 2097152 | tf_op jit(solution)/shard_map/all_to_all | solution.py:339

commit v5 on v4

--- a/solution.py
+++ b/solution.py
@@ -25,95 +25,102 @@
     return pltpu.CompilerParams(vmem_limit_bytes=mib << 20)
 
 
-def pack(query, out_grad, forward_out, first, count, step, kv=None):
+def pack(query, out_grad, forward_out, first, count, parts, kv=None):
     _, toks, width = query.shape
     heads = width // HD
     blocks = kv[0].shape[0] if kv else 0
     slots = 2 * count + 1 + 2 * blocks
-    steps = count // step
-    start = first // step
+    step = count // parts
 
     def body(*refs):
-        q_ref, g_ref, f_ref = refs[:3]
+        sources = refs[:3]
         kv_refs = refs[3 : 3 + (4 if kv else 0)]
         out_ref = refs[3 + len(kv_refs)]
-        dots, dots_out = refs[4 + len(kv_refs) : 6 + len(kv_refs)]
-        kv_out = refs[6 + len(kv_refs)] if kv else None
-        sems = refs[-1]
-        at = pl.program_id(0)
-
-        @pl.when(at == 0)
-        def _():
-            dots[...] = jnp.zeros_like(dots)
-            if kv:
-                for which in range(2):
-                    codes, scales = kv_refs[2 * which], kv_refs[2 * which + 1]
-                    factor = scales[...].astype(jnp.float32)
-                    for h in range(heads):
-                        part = codes[:, :, h * HD : (h + 1) * HD].astype(jnp.float32)
-                        rows = part * factor[:, :, h : h + 1]
-                        kv_out[h, which * blocks : (which + 1) * blocks] = rows.astype(jnp.bfloat16)
-
+        *refs, in_sems, out_sems = refs[4 + len(kv_refs) :]
+        q_buf, g_buf, f_buf, dots, dots_out = refs[:5]
+        kv_out = refs[5] if kv else None
+
+        def read(which, part):
+            buf = (q_buf, g_buf, f_buf)[which]
+            return pltpu.make_async_copy(
+                sources[which].at[pl.ds(first + part * step, step)],
+                buf.at[pl.ds(part * step, step)],
+                in_sems.at[which, part],
+            )
+
+        def write(which, part, h):
+            buf = (q_buf, g_buf)[which]
+            pltpu.make_async_copy(
+                buf.at[pl.ds(part * step, step), :, pl.ds(h * HD, HD)],
+                out_ref.at[h, pl.ds(which * count + part * step, step)],
+                out_sems.at[which],
+            ).start()
+
+        for part in range(parts):
+            for which in (1, 2, 0):
+                read(which, part).start()
+        if kv:
+            for which in range(2):
+                codes, scales = kv_refs[2 * which], kv_refs[2 * which + 1]
+                factor = scales[...].astype(jnp.float32)
+                for h in range(heads):
+                    rows = codes[:, :, h * HD : (h + 1) * HD].astype(jnp.float32)
+                    rows = rows * factor[:, :, h : h + 1]
+                    kv_out[h, which * blocks : (which + 1) * blocks] = rows.astype(jnp.bfloat16)
+            kv_copy = pltpu.make_async_copy(
+                kv_out, out_ref.at[:, pl.ds(2 * count + 1, 2 * blocks)], out_sems.at[3]
+            )
+            kv_copy.start()
+        lane = lax.broadcasted_iota(jnp.int32, (step * toks, HD), 1)
+        place = lax.broadcasted_iota(jnp.int32, (step * toks, HD), 0) // toks
+        for part in range(parts):
+            rows_at = slice(part * step, (part + 1) * step)
+            chosen = lane == place + part * step
+            read(1, part).wait()
+            read(2, part).wait()
+            for h in range(heads):
+                write(1, part, h)
+            read(0, part).wait()
+            for h in range(heads):
+                write(0, part, h)
+            for h in range(heads):
+                cut = slice(h * HD, (h + 1) * HD)
+                product = g_buf[rows_at, :, cut].astype(jnp.float32)
+                product *= f_buf[rows_at, :, cut].astype(jnp.float32)
+                total = jnp.sum(product.reshape(step * toks, HD), axis=-1, keepdims=True)
+                rows = jnp.where(chosen, total, 0.0).reshape(step, toks, HD)
+                value = jnp.sum(rows, axis=0)
+                dots[h] = value if part == 0 else dots[h] + value
         for h in range(heads):
-            pltpu.make_async_copy(
-                q_ref.at[:, :, pl.ds(h * HD, HD)], out_ref.at[h, pl.ds(at * step, step)], sems.at[0]
-            ).start()
-            pltpu.make_async_copy(
-                g_ref.at[:, :, pl.ds(h * HD, HD)],
-                out_ref.at[h, pl.ds(count + at * step, step)],
-                sems.at[1],
-            ).start()
-        lane = lax.broadcasted_iota(jnp.int32, (step * toks, HD), 1)
-        place = lax.broadcasted_iota(jnp.int32, (step * toks, HD), 0) // toks + at * step
-        chosen = lane == place
-        for h in range(heads):
-            cut = slice(h * HD, (h + 1) * HD)
-            product = g_ref[:, :, cut].astype(jnp.float32) * f_ref[:, :, cut].astype(jnp.float32)
-            total = jnp.sum(product.reshape(step * toks, HD), axis=-1, keepdims=True)
-            rows_of = jnp.where(chosen, total, 0.0)
-            dots[h] += jnp.sum(rows_of.reshape(step, toks, HD), axis=0)
-
-        @pl.when(at == steps - 1)
-        def _():
-            for h in range(heads):
-                value = dots[h]
-                high = value.astype(jnp.bfloat16).astype(jnp.float32)
-                middle = (value - high).astype(jnp.bfloat16).astype(jnp.float32)
-                low = (value - high - middle).astype(jnp.bfloat16).astype(jnp.float32)
-                spread = high + pltpu.roll(middle, PIECE, 1) + pltpu.roll(low, 2 * PIECE, 1)
-                dots_out[h, 0] = spread.astype(jnp.bfloat16)
-            copies = [
-                pltpu.make_async_copy(dots_out, out_ref.at[:, pl.ds(2 * count, 1)], sems.at[2])
-            ]
-            if kv:
-                copies.append(
-                    pltpu.make_async_copy(
-                        kv_out, out_ref.at[:, pl.ds(2 * count + 1, 2 * blocks)], sems.at[3]
-                    )
-                )
-            for copy in copies:
-                copy.start()
-            for copy in copies:
-                copy.wait()
-
-        pltpu.make_async_copy(q_ref, q_ref, sems.at[0]).wait()
-        pltpu.make_async_copy(g_ref, g_ref, sems.at[1]).wait()
-
-    rows = pl.BlockSpec((step, toks, width), lambda i: (start + i, 0, 0))
-    in_specs = [rows] * 3
+            value = dots[h]
+            high = value.astype(jnp.bfloat16).astype(jnp.float32)
+            middle = (value - high).astype(jnp.bfloat16).astype(jnp.float32)
+            low = (value - high - middle).astype(jnp.bfloat16).astype(jnp.float32)
+            spread = high + pltpu.roll(middle, PIECE, 1) + pltpu.roll(low, 2 * PIECE, 1)
+            dots_out[h, 0] = spread.astype(jnp.bfloat16)
+        dots_copy = pltpu.make_async_copy(
+            dots_out, out_ref.at[:, pl.ds(2 * count, 1)], out_sems.at[2]
+        )
+        dots_copy.start()
+        if kv:
+            kv_copy.wait()
+        pltpu.make_async_copy(g_buf, g_buf, out_sems.at[1]).wait()
+        pltpu.make_async_copy(q_buf, q_buf, out_sems.at[0]).wait()
+        dots_copy.wait()
+
+    in_specs = [pl.BlockSpec(memory_space=pl.ANY)] * 3
     args = [query, out_grad, forward_out]
-    scratch = [
-        pltpu.VMEM((heads, toks, HD), jnp.float32),
-        pltpu.VMEM((heads, 1, toks, HD), jnp.bfloat16),
-    ]
+    scratch = [pltpu.VMEM((count, toks, width), jnp.bfloat16)] * 3
+    scratch.append(pltpu.VMEM((heads, toks, HD), jnp.float32))
+    scratch.append(pltpu.VMEM((heads, 1, toks, HD), jnp.bfloat16))
     if kv:
         in_specs += [pl.BlockSpec(x.shape, lambda i: (0, 0, 0)) for x in kv]
         args += list(kv)
         scratch.append(pltpu.VMEM((heads, 2 * blocks, toks, HD), jnp.bfloat16))
-    scratch.append(pltpu.SemaphoreType.DMA((4,)))
+    scratch += [pltpu.SemaphoreType.DMA((3, parts)), pltpu.SemaphoreType.DMA((4,))]
     return pl.pallas_call(
         body,
-        grid=(steps,),
+        grid=(1,),
         in_specs=in_specs,
         out_specs=pl.BlockSpec(memory_space=pl.ANY),
         out_shape=jax.ShapeDtypeStruct((heads, slots, toks, HD), jnp.bfloat16),
@@ -201,11 +208,14 @@
                 )
 
         def grads_of(c, slot):
+            value_part = nn(probs[slot][...].reshape(2 * length, length), grads[slot][...])
+            key_part = nn(score_grads[slot][...].reshape(2 * length, length), queries[slot][...])
             query_t = None
             for j in range(2):
                 b = place(c, j)
-                value_acc[b] += nn(probs[slot][j], grads[slot][...])
-                key_acc[b] += nn(score_grads[slot][j], queries[slot][...])
+                rows = slice(j * length, (j + 1) * length)
+                value_acc[b] += value_part[rows]
+                key_acc[b] += key_part[rows]
                 part = nn(keys_t[b], score_grads[slot][j])
                 query_t = part if query_t is None else query_t + part
             out_ref[:, c] = (query_t * SCALE).T.astype(jnp.bfloat16).reshape(srcs, toks, HD)
@@ -245,18 +255,20 @@
     scratch += [pltpu.VMEM((2, length, length), jnp.float32)] * (2 * SLOTS)
     scratch += [pltpu.VMEM((2, length, length), jnp.bfloat16)] * (2 * SLOTS)
     scratch += [pltpu.VMEM((length, HD), jnp.bfloat16)] * (2 * SLOTS)
-    in_specs = [HELD if last else whole(message.shape), HELD, HELD]
-    args = [held(message) if last else message, held(kv_own), held(kv_other)]
+    in_specs = [whole(x.shape) for x in (message, kv_own, kv_other)]
+    args = [message, kv_own, kv_other]
+    if last:
+        in_specs[0], args[0] = HELD, held(message)
     if last:
         part = (2, blocks, length, HD)
         out_shape = (dq, pltpu.VMEM(part, jnp.float32), pltpu.VMEM(part, jnp.bfloat16))
         out_specs = [dq_spec, HELD, HELD]
         scratch += [pltpu.VMEM((total, length, HD), jnp.float32)] * 2
-        in_specs.append(HELD)
-        args.append(held(sums))
+        in_specs.append(whole(acc))
+        args.append(sums)
     else:
-        out_shape = (dq, pltpu.VMEM(acc, jnp.float32))
-        out_specs = [dq_spec, HELD]
+        out_shape = (dq, jax.ShapeDtypeStruct(acc, jnp.float32))
+        out_specs = [dq_spec, whole(acc)]
     flops = 2 * 5 * count * length * 2 * length * HD
     return pl.pallas_call(
         body,
@@ -351,10 +363,10 @@
     mine = lax.dynamic_slice_in_dim(pairing, group * count, count, 0)
     pairs = ((mine + blocks * group) % (2 * blocks)).reshape(-1)
     codes = (key_codes, key_scale, value_codes, value_scale)
-    send0 = pack(query, out_grad, forward_out, 0, large, large, codes)
+    send0 = pack(query, out_grad, forward_out, 0, large, 2, codes)
     got0 = to_heads(send0)
     later, pairs = lax.optimization_barrier((forward_out, pairs))
-    send1 = pack(query, out_grad, later, large, small, small)
+    send1 = pack(query, out_grad, later, large, small, 1)
     got1 = to_heads(send1)
     kv_own = got0[:, 2 * large + 1 :]
     kv_other = lax.ppermute(kv_own, "grp", swap)

time: 183 us -> 181 us (0.989)
  local copies, waits for them, and re-layouts: 7.39 us -> 4.23 us
    unnamed x12 -> x8, local copies, waits for them, and re-layouts: 5.61 us -> 2.44 us
  transfers between devices with their start and end apart: 6 -> 6, of which waited for: 4 -> 4; matrix products, arithmetic and copies ran while one was open for 1% -> 1% of each run, Pallas kernels for 18% -> 19%
where the time goes in v5:
time: 181 us
  waiting for transfers between devices  97.2 us (54%)
  Pallas kernels  40.2 us (22%)
  starting transfers between devices  38.1 us (21%)
  local copies, waits for them, and re-layouts  4.23 us (2%)
    all_to_all x4, waiting for transfers between devices, to_heads(): lax.all_to_all(message, 'head', split_axis=0, concat_axis=0, tiled=True)  59.2 us
    all_to_all x4, starting transfers between devices, to_heads(): lax.all_to_all(message, 'head', split_axis=0, concat_axis=0, tiled=True)  37.3 us
    pallas_call x2, Pallas kernels, attend(): pl.pallas_call(body, grid_spec=pltpu.PrefetchScalarGridSpec(num_scalar_pr...  27.7 us
    ppermute x1, waiting for transfers between devices, on_device(): kv_other = lax.ppermute(kv_own, 'grp', swap)  23.4 us
    ppermute x1, waiting for transfers between devices, on_device(): theirs = lax.ppermute(other_sum, 'grp', swap)  14.7 us
    pallas_call x2, Pallas kernels, pack(): pl.pallas_call(body, grid=(1,), in_specs=in_specs, out_specs=pl.BlockSpec...  8.36 us
  transfers between devices with their start and end apart: 6, of which 4 were waited for; matrix products, arithmetic and copies ran while one was open for 1% of the time, Pallas kernels for 19%

profile of v5, /device:TPU:1, one launch (start us, length us, event | category | flops | bytes accessed | tf_op | source)
XLA Modules:
  0.0 180.5 jit_solution(7729935928820135919)
XLA Ops:
  0.6 5.2 %shard_map.104 = bf16[64,53,4,128]{3,2,1,0:T(4,128)(2,1)} custom-call(bf16[36,4,8192]{2,1,0:T(4,128)(2,1)} %refs_0_.3, bf16[36,4,8192]{2,1,0:T(4,128)(2,1)} %refs_1_.3, bf16[36,4,8192]{2,1,0:T(4,128)(2,1)} %refs_2_.2, bf16[2,4,8192]{2,1,0:T(4,128)(2,1)} %refs_3_.1, bf16[2,4,64]{2,1,0:T(4,128)(2,1)} %refs_4_.1, bf16[2,4,8192]{2,1,0:T(4,128)(2,1)} %refs_5_.1, ...), custom_call_target="tpu_custom_call" | custom-call | tf_op jit(solution)/shard_map/pallas_call | solution.py:121
  5.8 0.0 copy-start.2
  5.8 12.3 %all-to-all-start.1 = ((bf16[64,53,4,128]{3,2,1,0:T(4,128)(2,1)}), bf16[64,53,4,128]{3,2,1,0:T(4,128)(2,1)S(1)}, u32[]{:S(2)}, u32[]{:S(2)}) async-start(bf16[64,53,4,128]{3,2,1,0:T(4,128)(2,1)} %shard_map.104), calls=%async_computation.1 | async-start | bytes 6946816 | tf_op jit(solution)/shard_map/all_to_all | solution.py:351
  18.2 0.1 and_select_fusion
  18.2 0.1 copy.14
  18.3 0.6 reshape.9.pair_ref
  19.0 3.2 %shard_map.103 = bf16[64,25,4,128]{3,2,1,0:T(4,128)(2,1)} custom-call(bf16[36,4,8192]{2,1,0:T(4,128)(2,1)} %refs_0_.3, bf16[36,4,8192]{2,1,0:T(4,128)(2,1)} %refs_1_.3, bf16[36,4,8192]{2,1,0:T(4,128)(2,1)} %refs_2_.2), custom_call_target="tpu_custom_call" | custom-call | tf_op jit(solution)/shard_map/pallas_call | solution.py:121
  22.2 41.6 %all-to-all-done.1.m_ref = bf16[64,53,4,128]{3,2,1,0:T(4,128)(2,1)S(1)} async-done(((bf16[64,53,4,128]{3,2,1,0:T(4,128)(2,1)}), bf16[64,53,4,128]{3,2,1,0:T(4,128)(2,1)S(1)}, u32[]{:S(2)}, u32[]{:S(2)}) %all-to-all-start.1) | async-done | bytes 3473440 | tf_op jit(solution)/shard_map/all_to_all | solution.py:351
  63.7 1.7 copy-done
  65.4 4.8 %all-to-all-start = ((bf16[64,25,4,128]{3,2,1,0:T(4,128)(2,1)}), bf16[64,25,4,128]{3,2,1,0:T(4,128)(2,1)S(1)}, u32[]{:S(2)}, u32[]{:S(2)}) async-start(bf16[64,25,4,128]{3,2,1,0:T(4,128)(2,1)} %shard_map.103), calls=%async_computation | async-start | bytes 3276800 | tf_op jit(solution)/shard_map/all_to_all | solution.py:351
  70.3 1.1 slice.4.own_ref
  71.3 0.8 collective-permute-start
  72.2 23.4 %collective-permute-done.other_ref = bf16[64,4,4,128]{3,2,1,0:T(4,128)(2,1)S(1)} collective-permute-done((bf16[64,4,4,128]{3,2,1,0:T(4,128)(2,1)S(1)}, bf16[64,4,4,128]{3,2,1,0:T(4,128)(2,1)S(1)}, u32[]{:S(2)}, u32[]{:S(2)}) %collective-permute-start) | collective-permute-done | bytes 262176 | tf_op jit(solution)/shard_map/ppermute | solution.py:372
  95.5 0.7 copy-done.3
  96.2 17.6 %shard_map.105 = (bf16[64,24,4,128]{3,2,1,0:T(4,128)(2,1)}, f32[2,4,256,128]{3,2,1,0:T(8,128)}) custom-call(s32[72]{0:T(128)} %reshape.9.pair_ref, bf16[64,53,4,128]{3,2,1,0:T(4,128)(2,1)} %copy-done, bf16[64,4,4,128]{3,2,1,0:T(4,128)(2,1)} %copy-done.1, bf16[64,4,4,128]{3,2,1,0:T(4,128)(2,1)} %copy-done.3), custom_call_target="tpu_custom_call" | custom-call | flops 4026531840 | bytes 6291456 | tf_op jit(solution)/shard_map/pallas_call | solution.py:273
  113.8 10.9 %all-to-all-start.3 = ((bf16[64,24,4,128]{3,2,1,0:T(4,128)(2,1)}), bf16[64,24,4,128]{3,2,1,0:T(4,128)(2,1)S(1)}, u32[]{:S(2)}, u32[]{:S(2)}) async-start(bf16[64,24,4,128]{3,2,1,0:T(4,128)(2,1)} %get-tuple-element.16), calls=%async_computation.3 | async-start | bytes 3145728 | tf_op jit(solution)/shard_map/all_to_all | solution.py:351
  124.6 10.1 %shard_map.106 = (bf16[64,16,4,128]{3,2,1,0:T(4,128)(2,1)}, f32[2,2,256,128]{3,2,1,0:T(8,128)S(1)}, bf16[2,2,256,128]{3,2,1,0:T(8,128)(2,1)S(1)}) custom-call(s32[72]{0:T(128)} %reshape.9.pair_ref, bf16[64,25,4,128]{3,2,1,0:T(4,128)(2,1)S(1)} %all-to-all-done.m_ref, bf16[64,4,4,128]{3,2,1,0:T(4,128)(2,1)} %copy-done.1, bf16[64,4,4,128]{3,2,1,0:T(4,128)(2,1)} %copy-done.3, ...), custom_call_target="tpu_custom_call" | custom-call | flops 2013265920 | bytes 6291456 | tf_op jit(solution)/shard_map/pallas_call | solution.py:273
  134.8 14.7 %collective-permute-done.1.other_ref = bf16[2,2,256,128]{3,2,1,0:T(8,128)(2,1)S(1)} collective-permute-done((bf16[2,2,256,128]{3,2,1,0:T(8,128)(2,1)S(1)}, bf16[2,2,256,128]{3,2,1,0:T(8,128)(2,1)S(1)}, u32[]{:S(2)}, u32[]{:S(2)}) %collective-permute-start.1) | collective-permute-done | bytes 262176 | tf_op jit(solution)/shard_map/ppermute | solution.py:378
  149.4 0.8 combine.1
  150.2 0.0 all-to-all-done.3.m_ref
  150.2 9.3 %all-to-all-start.2 = ((bf16[64,16,4,128]{3,2,1,0:T(4,128)(2,1)}), bf16[64,16,4,128]{3,2,1,0:T(4,128)(2,1)S(1)}, u32[]{:S(2)}, u32[]{:S(2)}) async-start(bf16[64,16,4,128]{3,2,1,0:T(4,128)(2,1)} %combine.1), calls=%async_computation.2 | async-start | bytes 2097152 | tf_op jit(solution)/shard_map/all_to_all | solution.py:351
  159.5 1.9 %shard_map.107.refs_0_ = bf16[36,4,8192]{2,1,0:T(4,128)(2,1)} custom-call(bf16[64,24,4,128]{3,2,1,0:T(4,128)(2,1)S(1)} %all-to-all-done.3.m_ref), custom_call_target="tpu_custom_call" | custom-call | tf_op jit(solution)/shard_map/pallas_call | solution.py:339
  161.5 17.6 %all-to-all-done.2.m_ref = bf16[64,16,4,128]{3,2,1,0:T(4,128)(2,1)S(1)} async-done(((bf16[64,16,4,128]{3,2,1,0:T(4,128)(2,1)}), bf16[64,16,4,128]{3,2,1,0:T(4,128)(2,1)S(1)}, u32[]{:S(2)}, u32[]{:S(2)}) %all-to-all-start.2) | async-done | bytes 1048608 | tf_op jit(solution)/shard_map/all_to_all | solution.py:351
  179.1 1.4 shard_map.108
  (7 shorter events, 0.0 us)
Async XLA Ops:
  5.8 12.3 %copy-start.2 = (s32[72,2]{0,1:T(2,128)S(1)}, s32[72,2]{0,1:T(2,128)}, u32[]{:S(2)}) copy-start(s32[72,2]{0,1:T(2,128)} %param.15) | copy-start | bytes 1732
  5.8 57.9 %all-to-all-start.1 = ((bf16[64,53,4,128]{3,2,1,0:T(4,128)(2,1)}), bf16[64,53,4,128]{3,2,1,0:T(4,128)(2,1)S(1)}, u32[]{:S(2)}, u32[]{:S(2)}) async-start(bf16[64,53,4,128]{3,2,1,0:T(4,128)(2,1)} %shard_map.104), calls=%async_computation.1 | async-start | bytes 6946816 | tf_op jit(solution)/shard_map/all_to_all | solution.py:351
  63.7 1.7 copy-start
  65.4 48.3 %all-to-all-start = ((bf16[64,25,4,128]{3,2,1,0:T(4,128)(2,1)}), bf16[64,25,4,128]{3,2,1,0:T(4,128)(2,1)S(1)}, u32[]{:S(2)}, u32[]{:S(2)}) async-start(bf16[64,25,4,128]{3,2,1,0:T(4,128)(2,1)} %shard_map.103), calls=%async_computation | async-start | bytes 3276800 | tf_op jit(solution)/shard_map/all_to_all | solution.py:351
  71.3 24.2 %copy-start.1 = (bf16[64,4,4,128]{3,2,1,0:T(4,128)(2,1)}, bf16[64,4,4,128]{3,2,1,0:T(4,128)(2,1)S(1)}, u32[]{:S(2)}) copy-start(bf16[64,4,4,128]{3,2,1,0:T(4,128)(2,1)S(1)} %slice.4.own_ref) | copy-start | bytes 786436
  71.3 24.2 %collective-permute-start = (bf16[64,4,4,128]{3,2,1,0:T(4,128)(2,1)S(1)}, bf16[64,4,4,128]{3,2,1,0:T(4,128)(2,1)S(1)}, u32[]{:S(2)}, u32[]{:S(2)}) collective-permute-start(bf16[64,4,4,128]{3,2,1,0:T(4,128)(2,1)S(1)} %slice.4.own_ref), channel_id=1, source_target_pairs={{0,64},{64,0},{1,65},{65,1},{2,66},{66,2},{3,67},{67,3},{4,68},{68... | collective-permute-start | bytes 786440 | tf_op jit(solution)/shard_map/ppermute | solution.py:372
  95.5 0.7 copy-start.3
  113.8 36.4 %all-to-all-start.3 = ((bf16[64,24,4,128]{3,2,1,0:T(4,128)(2,1)}), bf16[64,24,4,128]{3,2,1,0:T(4,128)(2,1)S(1)}, u32[]{:S(2)}, u32[]{:S(2)}) async-start(bf16[64,24,4,128]{3,2,1,0:T(4,128)(2,1)} %get-tuple-element.16), calls=%async_computation.3 | async-start | bytes 3145728 | tf_op jit(solution)/shard_map/all_to_all | solution.py:351
  134.8 14.7 %collective-permute-start.1 = (bf16[2,2,256,128]{3,2,1,0:T(8,128)(2,1)S(1)}, bf16[2,2,256,128]{3,2,1,0:T(8,128)(2,1)S(1)}, u32[]{:S(2)}, u32[]{:S(2)}) collective-permute-start(bf16[2,2,256,128]{3,2,1,0:T(8,128)(2,1)S(1)} %get-tuple-element.15), channel_id=1, source_target_pairs={{0,64},{64,0},{1,65},{65,1},{2,66},{66,2},{3,67},{67,3},{4,68},{68... | collective-permute-start | bytes 786440 | tf_op jit(solution)/shard_map/ppermute | solution.py:378
  150.2 28.9 %all-to-all-start.2 = ((bf16[64,16,4,128]{3,2,1,0:T(4,128)(2,1)}), bf16[64,16,4,128]{3,2,1,0:T(4,128)(2,1)S(1)}, u32[]{:S(2)}, u32[]{:S(2)}) async-start(bf16[64,16,4,128]{3,2,1,0:T(4,128)(2,1)} %combine.1), calls=%async_computation.2 | async-start | bytes 2097152 | tf_op jit(solution)/shard_map/all_to_all | solution.py:351

commit v6 on v5

v6 whole, which is shorter than its diff:
```python
import jax
import jax.numpy as jnp
from jax import lax
from jax.experimental import pallas as pl
from jax.experimental.pallas import tpu as pltpu
from jax.sharding import PartitionSpec as P

HD = 128
SCALE = HD ** (-0.5)
LOG2E = 1.4426950408889634
EXP_SCALE = SCALE * LOG2E
SLOTS = 3
PIECE = 32


HELD = pl.BlockSpec(memory_space=pltpu.VMEM)


def held(x):
    return pltpu.with_memory_space_constraint(x, pltpu.VMEM)


def params(mib=56):
    return pltpu.CompilerParams(vmem_limit_bytes=mib << 20)


def pack(query, out_grad, forward_out, first, count, parts, kv=None):
    _, toks, width = query.shape
    heads = width // HD
    blocks = kv[0].shape[0] if kv else 0
    step = count // parts
    ahead = 2 * blocks
    slots = ahead + 2 * step + 1

    def body(*refs):
        sources = refs[:3]
        kv_refs = refs[3 : 3 + (4 if kv else 0)]
        out_ref = refs[3 + len(kv_refs)]
        *refs, in_sems, out_sems = refs[4 + len(kv_refs) :]
        q_buf, g_buf, f_buf, dots, dots_out = refs[:5]
        kv_out = refs[5] if kv else None

        def read(which, part):
            buf = (q_buf, g_buf, f_buf)[which]
            return pltpu.make_async_copy(
                sources[which].at[pl.ds(first + part * step, step)],
                buf.at[pl.ds(part * step, step)],
                in_sems.at[which, part],
            )

        def write(which, part, h):
            buf = (q_buf, g_buf)[which]
            pltpu.make_async_copy(
                buf.at[pl.ds(part * step, step), :, pl.ds(h * HD, HD)],
                out_ref.at[part * heads + h, pl.ds(ahead + which * step, step)],
                out_sems.at[which],
            ).start()

        for part in range(parts):
            for which in (1, 2, 0):
                read(which, part).start()
        if kv:
            for which in range(2):
                codes, scales = kv_refs[2 * which], kv_refs[2 * which + 1]
                factor = scales[...].astype(jnp.float32)
                for h in range(heads):
                    rows = codes[:, :, h * HD : (h + 1) * HD].astype(jnp.float32)
                    rows = rows * factor[:, :, h : h + 1]
                    kv_out[h, which * blocks : (which + 1) * blocks] = rows.astype(jnp.bfloat16)
            kv_copies = [
                pltpu.make_async_copy(
                    kv_out,
                    out_ref.at[pl.ds(part * heads, heads), pl.ds(0, ahead)],
                    out_sems.at[3 + part],
                )
                for part in range(parts)
            ]
            for copy in kv_copies:
                copy.start()
        lane = lax.broadcasted_iota(jnp.int32, (step * toks, HD), 1)
        place = lax.broadcasted_iota(jnp.int32, (step * toks, HD), 0) // toks
        chosen = lane == place
        for part in range(parts):
            rows_at = slice(part * step, (part + 1) * step)
            read(1, part).wait()
            read(2, part).wait()
            for h in range(heads):
                write(1, part, h)
            read(0, part).wait()
            for h in range(heads):
                write(0, part, h)
            for h in range(heads):
                cut = slice(h * HD, (h + 1) * HD)
                product = g_buf[rows_at, :, cut].astype(jnp.float32)
                product *= f_buf[rows_at, :, cut].astype(jnp.float32)
                total = jnp.sum(product.reshape(step * toks, HD), axis=-1, keepdims=True)
                rows = jnp.where(chosen, total, 0.0).reshape(step, toks, HD)
                dots[part * heads + h] = jnp.sum(rows, axis=0)
        for h in range(parts * heads):
            value = dots[h]
            high = value.astype(jnp.bfloat16).astype(jnp.float32)
            middle = (value - high).astype(jnp.bfloat16).astype(jnp.float32)
            low = (value - high - middle).astype(jnp.bfloat16).astype(jnp.float32)
            spread = high + pltpu.roll(middle, PIECE, 1) + pltpu.roll(low, 2 * PIECE, 1)
            dots_out[h, 0] = spread.astype(jnp.bfloat16)
        dots_copy = pltpu.make_async_copy(
            dots_out, out_ref.at[:, pl.ds(ahead + 2 * step, 1)], out_sems.at[2]
        )
        dots_copy.start()
        if kv:
            for copy in kv_copies:
                copy.wait()
        pltpu.make_async_copy(g_buf, g_buf, out_sems.at[1]).wait()
        pltpu.make_async_copy(q_buf, q_buf, out_sems.at[0]).wait()
        dots_copy.wait()

    in_specs = [pl.BlockSpec(memory_space=pl.ANY)] * 3
    args = [query, out_grad, forward_out]
    scratch = [pltpu.VMEM((count, toks, width), jnp.bfloat16)] * 3
    scratch.append(pltpu.VMEM((parts * heads, toks, HD), jnp.float32))
    scratch.append(pltpu.VMEM((parts * heads, 1, toks, HD), jnp.bfloat16))
    if kv:
        in_specs += [pl.BlockSpec(x.shape, lambda i: (0, 0, 0)) for x in kv]
        args += list(kv)
        scratch.append(pltpu.VMEM((heads, 2 * blocks, toks, HD), jnp.bfloat16))
    scratch += [pltpu.SemaphoreType.DMA((3, parts)), pltpu.SemaphoreType.DMA((3 + parts,))]
    return pl.pallas_call(
        body,
        name=f"pack{first}",
        grid=(1,),
        in_specs=in_specs,
        out_specs=pl.BlockSpec(memory_space=pl.ANY),
        out_shape=jax.ShapeDtypeStruct((parts * heads, slots, toks, HD), jnp.bfloat16),
        scratch_shapes=scratch,
        compiler_params=params(),
    )(*args)


def nt(a, b):
    return lax.dot_general(a, b, (((1,), (1,)), ((), ())), preferred_element_type=jnp.float32)


def nn(a, b):
    return jnp.dot(a, b, preferred_element_type=jnp.float32)


def attend(pairs, message, source, first, per, count, groups, blocks, sums=None):
    devices, slots, toks, _ = message.shape
    srcs = devices // groups
    length = srcs * toks
    total = groups * blocks
    steps = groups * count
    last = sums is not None
    ahead = slots - 2 * count - 1
    extra = 2 * blocks if last else 0

    def body(pair_ref, group_ref, m_ref, kv_ref, *refs):
        if last:
            sum_ref, out_ref = refs[:2]
            refs, (key_acc, value_acc) = refs[2:-2], refs[-2:]
        else:
            out_ref, sum_out = refs[:2]
            refs = refs[2:]
            key_acc, value_acc = sum_out.at[0], sum_out.at[1]
        keys, keys_t, values, dots = refs[:4]
        scores, prob_grads, probs, score_grads, queries, grads = (
            refs[4 + SLOTS * at : 4 + SLOTS * (at + 1)] for at in range(6)
        )
        for b in range(total):
            rows, at = slice(b // blocks * srcs, (b // blocks + 1) * srcs), b % blocks
            key = kv_ref[rows, at].reshape(length, HD)
            keys[b] = key
            keys_t[b] = key.astype(jnp.float32).T.astype(jnp.bfloat16)
            values[b] = kv_ref[rows, blocks + at].reshape(length, HD)
        row = lax.broadcasted_iota(jnp.int32, (PIECE, HD), 0)
        lane = lax.broadcasted_iota(jnp.int32, (PIECE, HD), 1)
        picks = jnp.where((lane % PIECE == row) & (lane < 3 * PIECE), 1.0, 0.0).astype(jnp.bfloat16)
        for g in range(groups):
            tile = m_ref[g * srcs : (g + 1) * srcs, ahead + 2 * count].reshape(length, HD)
            dots[g * PIECE : (g + 1) * PIECE] = nt(picks, tile)
        if last:
            key_acc[...] = sum_ref[0]
            value_acc[...] = sum_ref[1]
        else:
            sum_out[...] = jnp.zeros_like(sum_out)

        def where(c):
            group = lax.div(c, jnp.int32(count))
            return group, c - group * count

        def place(c, j):
            group, at = where(c)
            block = group * per + first + group_ref[0] * count + at
            return pair_ref[2 * block + j]

        def scores_of(c, slot):
            group, at = where(c)
            rows = pl.ds(group * srcs, srcs)
            query = m_ref[rows, ahead + at].reshape(length, HD)
            grad = m_ref[rows, ahead + count + at].reshape(length, HD)
            queries[slot][...] = query
            grads[slot][...] = grad
            for j in range(2):
                scores[slot][j] = nt(keys[place(c, j)], query)
                prob_grads[slot][j] = nt(values[place(c, j)], grad)

        def probs_of(c, slot):
            score, prob_grad = scores[slot], prob_grads[slot]
            cuts = [(j, slice(r, r + 32)) for j in range(2) for r in range(0, length, 32)]
            high = None
            for j, rows in cuts:
                part = jnp.max(score[j, rows].reshape(32 // 8, 8, length), axis=0)
                high = part if high is None else jnp.maximum(high, part)
            high = jnp.max(high, axis=0, keepdims=True) * EXP_SCALE
            norm = None
            for j, rows in cuts:
                weight = jnp.exp2(score[j, rows] * EXP_SCALE - high)
                score[j, rows] = weight
                part = jnp.sum(weight.reshape(32 // 8, 8, length), axis=0)
                norm = part if norm is None else norm + part
            inverse = 1.0 / jnp.sum(norm, axis=0, keepdims=True)
            group, at = where(c)
            dot_row = dots[pl.ds(group * PIECE + at, 1), :]
            for j, rows in cuts:
                prob = score[j, rows] * inverse
                probs[slot][j, rows] = prob.astype(jnp.bfloat16)
                score_grads[slot][j, rows] = (prob * (prob_grad[j, rows] - dot_row)).astype(
                    jnp.bfloat16
                )

        def grads_of(c, slot):
            value_part = nn(probs[slot][...].reshape(2 * length, length), grads[slot][...])
            key_part = nn(score_grads[slot][...].reshape(2 * length, length), queries[slot][...])
            query_t = None
            for j in range(2):
                b = place(c, j)
                rows = slice(j * length, (j + 1) * length)
                value_acc[b] += value_part[rows]
                key_acc[b] += key_part[rows]
                part = nn(keys_t[b], score_grads[slot][j])
                query_t = part if query_t is None else query_t + part
            group, at = where(c)
            rows = (query_t * SCALE).T.astype(jnp.bfloat16)
            out_ref[pl.ds(group * srcs, srcs), at] = rows.reshape(srcs, toks, HD)

        for ref in (probs[-1], score_grads[-1], queries[-1], grads[-1]):
            ref[...] = jnp.zeros_like(ref)
        scores_of(jnp.int32(0), 0)

        def several(i, _):
            for k in range(SLOTS):
                c = i * SLOTS + k
                grads_of(jnp.maximum(c - 1, 0), (k - 1) % SLOTS)
                scores_of(jnp.minimum(c + 1, steps - 1), (k + 1) % SLOTS)
                probs_of(c, k)
            return 0

        lax.fori_loop(0, steps // SLOTS, several, 0)
        grads_of(jnp.int32(steps - 1), SLOTS - 1)
        if last:
            for b in range(total):
                rows, at = slice(b // blocks * srcs, (b // blocks + 1) * srcs), count + b % blocks
                key_rows = (key_acc[b] * SCALE).astype(jnp.bfloat16)
                out_ref[rows, at] = key_rows.reshape(srcs, toks, HD)
                value_rows = value_acc[b].astype(jnp.bfloat16)
                out_ref[rows, at + blocks] = value_rows.reshape(srcs, toks, HD)

    def whole(shape):
        return pl.BlockSpec(shape, lambda i, p, g: (0,) * len(shape))

    dq = jax.ShapeDtypeStruct((devices, count + extra, toks, HD), jnp.bfloat16)
    acc = (2, total, length, HD)
    scratch = [
        pltpu.VMEM((total, length, HD), jnp.bfloat16),
        pltpu.VMEM((total, HD, length), jnp.bfloat16),
        pltpu.VMEM((total, length, HD), jnp.bfloat16),
        pltpu.VMEM((groups * PIECE, length), jnp.float32),
    ]
    scratch += [pltpu.VMEM((2, length, length), jnp.float32)] * (2 * SLOTS)
    scratch += [pltpu.VMEM((2, length, length), jnp.bfloat16)] * (2 * SLOTS)
    scratch += [pltpu.VMEM((length, HD), jnp.bfloat16)] * (2 * SLOTS)
    in_specs = [whole(message.shape), whole((devices, 2 * blocks, toks, HD))]
    args = [message, source]
    if last:
        in_specs[0], args[0] = HELD, held(message)
        in_specs.append(whole(acc))
        args.append(sums)
        out_shape, out_specs = dq, whole(dq.shape)
        scratch += [pltpu.VMEM((total, length, HD), jnp.float32)] * 2
    else:
        out_shape = (dq, jax.ShapeDtypeStruct(acc, jnp.float32))
        out_specs = [whole(dq.shape), whole(acc)]
    flops = 2 * 5 * steps * length * 2 * length * HD
    return pl.pallas_call(
        body,
        name=f"attend{first}",
        grid_spec=pltpu.PrefetchScalarGridSpec(
            num_scalar_prefetch=2,
            grid=(1,),
            in_specs=in_specs,
            out_specs=out_specs,
            scratch_shapes=scratch,
        ),
        out_shape=out_shape,
        compiler_params=params(),
        cost_estimate=pl.CostEstimate(
            flops=flops, transcendentals=2 * steps * length * length, bytes_accessed=6 << 20
        ),
    )(*pairs, *args)


def unpack(message, total, first, count, step, groups, into=None, blocks=0):
    devices, _, toks, _ = message.shape
    heads = devices // groups
    width = heads * HD
    start = first // step
    per = count // step

    def body(m_ref, *refs):
        out_ref, *sums = refs if into is None else refs[1:]
        part = lax.div(pl.program_id(0), jnp.int32(per))
        at = (pl.program_id(0) - part * per) * step
        for h in range(heads):
            out_ref[:, :, h * HD : (h + 1) * HD] = m_ref[part * heads + h, pl.ds(at, step)]
        if blocks:

            @pl.when(pl.program_id(0) == 0)
            def _():
                for which, out in enumerate(sums):
                    behind = slice(count + which * blocks, count + (which + 1) * blocks)
                    for h in range(heads):
                        value = m_ref[h, behind].astype(jnp.float32)
                        for g in range(1, groups):
                            value += m_ref[g * heads + h, behind].astype(jnp.float32)
                        out[:, :, h * HD : (h + 1) * HD] = value.astype(jnp.bfloat16)

    in_specs = [HELD]
    args = [held(message)]
    out_shape = [jax.ShapeDtypeStruct((total, toks, width), message.dtype)]
    out_specs = [pl.BlockSpec((step, toks, width), lambda i: (start + i, 0, 0))]
    if blocks:
        out_shape += [jax.ShapeDtypeStruct((blocks, toks, width), message.dtype)] * 2
        out_specs += [pl.BlockSpec((blocks, toks, width), lambda i: (0, 0, 0))] * 2
    aliases = {}
    if into is not None:
        in_specs.append(pl.BlockSpec(memory_space=pl.ANY))
        args.append(into)
        aliases = {1: 0}
    return pl.pallas_call(
        body,
        name=f"unpack{first}",
        grid=(groups * per,),
        in_specs=in_specs,
        out_specs=out_specs,
        out_shape=out_shape,
        input_output_aliases=aliases,
        compiler_params=params(),
    )(*args)


def exchange(message):
    return lax.all_to_all(message, ("grp", "head"), split_axis=0, concat_axis=0, tiled=True)


def on_device(
    query, out_grad, forward_out, key_codes, key_scale, value_codes, value_scale, pairing
):
    per = query.shape[0]
    blocks = key_codes.shape[0]
    groups = lax.axis_size("grp")
    large = per * 2 // 3
    small = per - large
    pairs = pairing.reshape(-1)
    group = lax.axis_index("grp").reshape(1)
    codes = (key_codes, key_scale, value_codes, value_scale)
    got0 = exchange(pack(query, out_grad, forward_out, 0, large, groups, codes))
    later, pairs, group = lax.optimization_barrier((forward_out, pairs, group))
    got1 = exchange(pack(query, out_grad, later, large, small, groups))
    pairs = (pairs, group)
    first, second = large // groups, small // groups
    grads0, sums = attend(pairs, got0, got0, 0, per, first, groups, blocks)
    back0 = exchange(grads0)
    grads1 = attend(pairs, got1, got0, large, per, second, groups, blocks, sums)
    back1 = exchange(grads1)
    (rows,) = unpack(back0, per, 0, first, 6, groups)
    return unpack(back1, per, large, second, 6, groups, into=rows, blocks=blocks)


def solution(mesh):
    spec = P("grp", "head", None)
    return jax.shard_map(
        on_device,
        mesh=mesh,
        in_specs=(spec,) * 7 + (P(),),
        out_specs=(spec,) * 3,
        check_vma=False,
    )
```

time: 181 us -> 156 us (0.86)
  starting transfers between devices: 38.1 us -> 27.4 us
  waiting for transfers between devices: 97.2 us -> 86.7 us
  local copies, waits for them, and re-layouts: 4.23 us -> 0.81 us
    ppermute x2 -> x0, waiting for transfers between devices: 38 us -> none  [the longest x1 23.4 us: on_device(): kv_other = lax.ppermute(kv_own, 'grp', swap)]
    all_to_all x4, waiting for transfers between devices: 59.2 us -> 86.7 us  [exchange(): lax.all_to_all(message, ('grp', 'head'), split_axis=0, concat_axis=0, til...]
    all_to_all x4, starting transfers between devices: 37.3 us -> 27.4 us  [exchange(): lax.all_to_all(message, ('grp', 'head'), split_axis=0, concat_axis=0, til...]
    unnamed x8 -> x3, local copies, waits for them, and re-layouts: 2.44 us -> 0.1 us
    pallas_call x7 -> x6, Pallas kernels: 40.2 us -> 39.9 us  [the longest x2 28.3 us: attend(): pl.pallas_call(body, name=f'attend{first}', grid_spec=pltpu.PrefetchScala...]
  transfers between devices with their start and end apart: 6 -> 4, of which waited for: 4 -> 4; matrix products, arithmetic and copies ran while one was open for 1% -> 1% of each run, Pallas kernels for 19% -> 21%
where the time goes in v6:
time: 156 us
  waiting for transfers between devices  86.7 us (56%)
  Pallas kernels  39.9 us (26%)
  starting transfers between devices  27.4 us (18%)
    all_to_all x4, waiting for transfers between devices, exchange(): lax.all_to_all(message, ('grp', 'head'), split_axis=0, concat_axis=0, til...  86.7 us
    pallas_call x2, Pallas kernels, attend(): pl.pallas_call(body, name=f'attend{first}', grid_spec=pltpu.PrefetchScala...  28.3 us
    all_to_all x4, starting transfers between devices, exchange(): lax.all_to_all(message, ('grp', 'head'), split_axis=0, concat_axis=0, til...  27.4 us
    pallas_call x2, Pallas kernels, pack(): pl.pallas_call(body, name=f'pack{first}', grid=(1,), in_specs=in_specs, o...  8.39 us
    pallas_call x2, Pallas kernels, unpack(): pl.pallas_call(body, name=f'unpack{first}', grid=(groups * per,), in_spec...  3.21 us
  transfers between devices with their start and end apart: 4, of which 4 were waited for; matrix products, arithmetic and copies ran while one was open for 1% of the time, Pallas kernels for 21%

profile of v6, /device:TPU:1, one launch (start us, length us, event | category | flops | bytes accessed | tf_op | source)
XLA Modules:
  0.0 155.5 jit_solution(8725066651584542138)
XLA Ops:
  0.6 5.4 %pack0.1 = bf16[128,29,4,128]{3,2,1,0:T(4,128)(2,1)} custom-call(bf16[36,4,8192]{2,1,0:T(4,128)(2,1)} %refs_0_.3, bf16[36,4,8192]{2,1,0:T(4,128)(2,1)} %refs_1_.3, bf16[36,4,8192]{2,1,0:T(4,128)(2,1)} %refs_2_.2, bf16[2,4,8192]{2,1,0:T(4,128)(2,1)} %refs_3_.1, bf16[2,4,64]{2,1,0:T(4,128)(2,1)} %refs_4_.1, bf16[2,4,8192]{2,1,0:T(4,128)(2,1)} %refs_5_.1, ...), custom_call_target="tpu_custom_call" | custom-call | tf_op jit(solution)/shard_map/pack0/pallas_call | solution.py:127
  6.0 0.0 copy-start
  6.0 11.9 %all-to-all-start.1 = ((bf16[128,29,4,128]{3,2,1,0:T(4,128)(2,1)}), bf16[128,29,4,128]{3,2,1,0:T(4,128)(2,1)}, u32[]{:S(2)}, u32[]{:S(2)}) async-start(bf16[128,29,4,128]{3,2,1,0:T(4,128)(2,1)} %pack0.1), calls=%async_computation.1 | async-start | bytes 7602176 | tf_op jit(solution)/shard_map/all_to_all | solution.py:362
  17.9 0.0 copy-done
  17.9 0.1 copy.12
  18.0 0.7 reshape.12.pair_ref
  18.7 3.0 %pack24.1 = bf16[128,13,4,128]{3,2,1,0:T(4,128)(2,1)} custom-call(bf16[36,4,8192]{2,1,0:T(4,128)(2,1)} %refs_0_.3, bf16[36,4,8192]{2,1,0:T(4,128)(2,1)} %refs_1_.3, bf16[36,4,8192]{2,1,0:T(4,128)(2,1)} %refs_2_.2), custom_call_target="tpu_custom_call" | custom-call | tf_op jit(solution)/shard_map/pack24/pallas_call | solution.py:127
  21.8 44.4 %all-to-all-done.1.m_ref.kv_ref = bf16[128,29,4,128]{3,2,1,0:T(4,128)(2,1)} async-done(((bf16[128,29,4,128]{3,2,1,0:T(4,128)(2,1)}), bf16[128,29,4,128]{3,2,1,0:T(4,128)(2,1)}, u32[]{:S(2)}, u32[]{:S(2)}) %all-to-all-start.1) | async-done | bytes 3801120 | tf_op jit(solution)/shard_map/all_to_all | solution.py:362
  66.2 6.0 %all-to-all-start = ((bf16[128,13,4,128]{3,2,1,0:T(4,128)(2,1)}), bf16[128,13,4,128]{3,2,1,0:T(4,128)(2,1)S(1)}, u32[]{:S(2)}, u32[]{:S(2)}) async-start(bf16[128,13,4,128]{3,2,1,0:T(4,128)(2,1)} %pack24.1), calls=%async_computation | async-start | bytes 3407872 | tf_op jit(solution)/shard_map/all_to_all | solution.py:362
  72.1 17.8 %attend0.1 = (bf16[128,12,4,128]{3,2,1,0:T(4,128)(2,1)}, f32[2,4,256,128]{3,2,1,0:T(8,128)}) custom-call(s32[144]{0:T(256)} %reshape.12.pair_ref, s32[1]{0:T(128)} %bitcast.group_ref, bf16[128,29,4,128]{3,2,1,0:T(4,128)(2,1)} %all-to-all-done.1.m_ref.kv_ref, bf16[128,29,4,128]{3,2,1,0:T(4,128)(2,1)} %all-to-all-done.1.m_ref.kv_ref), custom_call_target="tpu_custom_call" | custom-call | flops 4026531840 | bytes 6291456 | tf_op jit(solution)/shard_map/attend0/pallas_call | solution.py:294
  89.9 8.2 %all-to-all-done.m_ref = bf16[128,13,4,128]{3,2,1,0:T(4,128)(2,1)S(1)} async-done(((bf16[128,13,4,128]{3,2,1,0:T(4,128)(2,1)}), bf16[128,13,4,128]{3,2,1,0:T(4,128)(2,1)S(1)}, u32[]{:S(2)}, u32[]{:S(2)}) %all-to-all-start) | async-done | bytes 1703968 | tf_op jit(solution)/shard_map/all_to_all | solution.py:362
  98.1 4.8 %all-to-all-start.3 = ((bf16[128,12,4,128]{3,2,1,0:T(4,128)(2,1)}), bf16[128,12,4,128]{3,2,1,0:T(4,128)(2,1)S(1)}, u32[]{:S(2)}, u32[]{:S(2)}) async-start(bf16[128,12,4,128]{3,2,1,0:T(4,128)(2,1)} %get-tuple-element.12), calls=%async_computation.3 | async-start | bytes 3145728 | tf_op jit(solution)/shard_map/all_to_all | solution.py:362
  102.9 10.5 %attend24.1 = bf16[128,10,4,128]{3,2,1,0:T(4,128)(2,1)} custom-call(s32[144]{0:T(256)} %reshape.12.pair_ref, s32[1]{0:T(128)} %bitcast.group_ref, bf16[128,13,4,128]{3,2,1,0:T(4,128)(2,1)S(1)} %all-to-all-done.m_ref, bf16[128,29,4,128]{3,2,1,0:T(4,128)(2,1)} %all-to-all-done.1.m_ref.kv_ref, f32[2,4,256,128]{3,2,1,0:T(8,128)} %get-tuple-element.11.refs_0_), custom_call_target="tpu_custom_call" | custom-call | flops 2013265920 | bytes 6291456 | tf_op jit(solution)/shard_map/attend24/pallas_call | solution.py:294
  113.4 14.2 %all-to-all-done.3.m_ref = bf16[128,12,4,128]{3,2,1,0:T(4,128)(2,1)S(1)} async-done(((bf16[128,12,4,128]{3,2,1,0:T(4,128)(2,1)}), bf16[128,12,4,128]{3,2,1,0:T(4,128)(2,1)S(1)}, u32[]{:S(2)}, u32[]{:S(2)}) %all-to-all-start.3) | async-done | bytes 1572896 | tf_op jit(solution)/shard_map/all_to_all | solution.py:362
  127.6 4.8 %all-to-all-start.2 = ((bf16[128,10,4,128]{3,2,1,0:T(4,128)(2,1)}), bf16[128,10,4,128]{3,2,1,0:T(4,128)(2,1)S(1)}, u32[]{:S(2)}, u32[]{:S(2)}) async-start(bf16[128,10,4,128]{3,2,1,0:T(4,128)(2,1)} %attend24.1), calls=%async_computation.2 | async-start | bytes 2621440 | tf_op jit(solution)/shard_map/all_to_all | solution.py:362
  132.4 1.9 %unpack0.1.refs_0_ = bf16[36,4,8192]{2,1,0:T(4,128)(2,1)} custom-call(bf16[128,12,4,128]{3,2,1,0:T(4,128)(2,1)S(1)} %all-to-all-done.3.m_ref), custom_call_target="tpu_custom_call" | custom-call | tf_op jit(solution)/shard_map/unpack0/pallas_call | solution.py:349
  134.3 19.9 %all-to-all-done.2.m_ref = bf16[128,10,4,128]{3,2,1,0:T(4,128)(2,1)S(1)} async-done(((bf16[128,10,4,128]{3,2,1,0:T(4,128)(2,1)}), bf16[128,10,4,128]{3,2,1,0:T(4,128)(2,1)S(1)}, u32[]{:S(2)}, u32[]{:S(2)}) %all-to-all-start.2) | async-done | bytes 1310752 | tf_op jit(solution)/shard_map/all_to_all | solution.py:362
  154.2 1.3 unpack24.1
Async XLA Ops:
  6.0 11.9 %copy-start = (s32[72,2]{0,1:T(2,128)S(1)}, s32[72,2]{0,1:T(2,128)}, u32[]{:S(2)}) copy-start(s32[72,2]{0,1:T(2,128)} %param.15) | copy-start | bytes 1732
  6.0 60.2 %all-to-all-start.1 = ((bf16[128,29,4,128]{3,2,1,0:T(4,128)(2,1)}), bf16[128,29,4,128]{3,2,1,0:T(4,128)(2,1)}, u32[]{:S(2)}, u32[]{:S(2)}) async-start(bf16[128,29,4,128]{3,2,1,0:T(4,128)(2,1)} %pack0.1), calls=%async_computation.1 | async-start | bytes 7602176 | tf_op jit(solution)/shard_map/all_to_all | solution.py:362
  66.2 31.9 %all-to-all-start = ((bf16[128,13,4,128]{3,2,1,0:T(4,128)(2,1)}), bf16[128,13,4,128]{3,2,1,0:T(4,128)(2,1)S(1)}, u32[]{:S(2)}, u32[]{:S(2)}) async-start(bf16[128,13,4,128]{3,2,1,0:T(4,128)(2,1)} %pack24.1), calls=%async_computation | async-start | bytes 3407872 | tf_op jit(solution)/shard_map/all_to_all | solution.py:362
  98.1 29.5 %all-to-all-start.3 = ((bf16[128,12,4,128]{3,2,1,0:T(4,128)(2,1)}), bf16[128,12,4,128]{3,2,1,0:T(4,128)(2,1)S(1)}, u32[]{:S(2)}, u32[]{:S(2)}) async-start(bf16[128,12,4,128]{3,2,1,0:T(4,128)(2,1)} %get-tuple-element.12), calls=%async_computation.3 | async-start | bytes 3145728 | tf_op jit(solution)/shard_map/all_to_all | solution.py:362
  127.6 26.7 %all-to-all-start.2 = ((bf16[128,10,4,128]{3,2,1,0:T(4,128)(2,1)}), bf16[128,10,4,128]{3,2,1,0:T(4,128)(2,1)S(1)}, u32[]{:S(2)}, u32[]{:S(2)}) async-start(bf16[128,10,4,128]{3,2,1,0:T(4,128)(2,1)} %attend24.1), calls=%async_computation.2 | async-start | bytes 2621440 | tf_op jit(solution)/shard_map/all_to_all | solution.py:362

commit v7 on v6

--- a/solution.py
+++ b/solution.py
@@ -24,42 +24,63 @@
     return pltpu.CompilerParams(vmem_limit_bytes=mib << 20)
 
 
-def pack(query, out_grad, forward_out, first, count, parts, kv=None):
-    _, toks, width = query.shape
+def pack(query, out_grad, first, count, parts, forward_out=None, kv=()):
+    total, toks, width = query.shape
     heads = width // HD
-    blocks = kv[0].shape[0] if kv else 0
+    ahead = 2 * kv[0].shape[0] if kv else 0
+    blocks = ahead // 2
     step = count // parts
-    ahead = 2 * blocks
-    slots = ahead + 2 * step + 1
+    rest = (total - first - count) // parts
+    slots = ahead + 2 * step + (1 if kv else 0)
 
     def body(*refs):
-        sources = refs[:3]
-        kv_refs = refs[3 : 3 + (4 if kv else 0)]
-        out_ref = refs[3 + len(kv_refs)]
-        *refs, in_sems, out_sems = refs[4 + len(kv_refs) :]
-        q_buf, g_buf, f_buf, dots, dots_out = refs[:5]
-        kv_out = refs[5] if kv else None
+        sources = refs[: 3 if kv else 2]
+        kv_refs = refs[len(sources) : len(sources) + len(kv)]
+        out_ref = refs[len(sources) + len(kv)]
+        *refs, in_sems, out_sems = refs[len(sources) + len(kv) + 1 :]
+        bufs = refs[: len(sources)]
+        if kv:
+            more, (dots, dots_out, kv_out) = refs[3:5], refs[5:]
 
         def read(which, part):
-            buf = (q_buf, g_buf, f_buf)[which]
             return pltpu.make_async_copy(
                 sources[which].at[pl.ds(first + part * step, step)],
-                buf.at[pl.ds(part * step, step)],
+                bufs[which].at[pl.ds(part * step, step)],
                 in_sems.at[which, part],
             )
 
+        def read_more(which):
+            return pltpu.make_async_copy(
+                sources[which].at[pl.ds(first + count, rest * parts)],
+                more[which - 1],
+                in_sems.at[2 + which, 0],
+            )
+
         def write(which, part, h):
-            buf = (q_buf, g_buf)[which]
             pltpu.make_async_copy(
-                buf.at[pl.ds(part * step, step), :, pl.ds(h * HD, HD)],
+                bufs[which].at[pl.ds(part * step, step), :, pl.ds(h * HD, HD)],
                 out_ref.at[part * heads + h, pl.ds(ahead + which * step, step)],
                 out_sems.at[which],
             ).start()
 
+        def row_dots(part, grad, other, rows, size, offset):
+            lane = lax.broadcasted_iota(jnp.int32, (size * toks, HD), 1)
+            chosen = lane == lax.broadcasted_iota(jnp.int32, (size * toks, HD), 0) // toks + offset
+            for h in range(heads):
+                cut = slice(h * HD, (h + 1) * HD)
+                product = grad[rows, :, cut].astype(jnp.float32)
+                product *= other[rows, :, cut].astype(jnp.float32)
+                sums = jnp.sum(product.reshape(size * toks, HD), axis=-1, keepdims=True)
+                value = jnp.sum(jnp.where(chosen, sums, 0.0).reshape(size, toks, HD), axis=0)
+                at = part * heads + h
+                dots[at] = value if offset == 0 else dots[at] + value
+
         for part in range(parts):
-            for which in (1, 2, 0):
+            for which in (1, 2, 0) if kv else (1, 0):
                 read(which, part).start()
         if kv:
+            read_more(1).start()
+            read_more(2).start()
             for which in range(2):
                 codes, scales = kv_refs[2 * which], kv_refs[2 * which + 1]
                 factor = scales[...].astype(jnp.float32)
@@ -77,53 +98,48 @@
             ]
             for copy in kv_copies:
                 copy.start()
-        lane = lax.broadcasted_iota(jnp.int32, (step * toks, HD), 1)
-        place = lax.broadcasted_iota(jnp.int32, (step * toks, HD), 0) // toks
-        chosen = lane == place
         for part in range(parts):
-            rows_at = slice(part * step, (part + 1) * step)
-            read(1, part).wait()
-            read(2, part).wait()
-            for h in range(heads):
-                write(1, part, h)
-            read(0, part).wait()
-            for h in range(heads):
-                write(0, part, h)
-            for h in range(heads):
-                cut = slice(h * HD, (h + 1) * HD)
-                product = g_buf[rows_at, :, cut].astype(jnp.float32)
-                product *= f_buf[rows_at, :, cut].astype(jnp.float32)
-                total = jnp.sum(product.reshape(step * toks, HD), axis=-1, keepdims=True)
-                rows = jnp.where(chosen, total, 0.0).reshape(step, toks, HD)
-                dots[part * heads + h] = jnp.sum(rows, axis=0)
-        for h in range(parts * heads):
-            value = dots[h]
-            high = value.astype(jnp.bfloat16).astype(jnp.float32)
-            middle = (value - high).astype(jnp.bfloat16).astype(jnp.float32)
-            low = (value - high - middle).astype(jnp.bfloat16).astype(jnp.float32)
-            spread = high + pltpu.roll(middle, PIECE, 1) + pltpu.roll(low, 2 * PIECE, 1)
-            dots_out[h, 0] = spread.astype(jnp.bfloat16)
-        dots_copy = pltpu.make_async_copy(
-            dots_out, out_ref.at[:, pl.ds(ahead + 2 * step, 1)], out_sems.at[2]
-        )
-        dots_copy.start()
+            for which in (1, 2, 0) if kv else (1, 0):
+                read(which, part).wait()
+            for which in (1, 0):
+                for h in range(heads):
+                    write(which, part, h)
+            if kv:
+                row_dots(part, bufs[1], bufs[2], slice(part * step, (part + 1) * step), step, 0)
         if kv:
+            read_more(1).wait()
+            read_more(2).wait()
+            for part in range(parts):
+                row_dots(part, *more, slice(part * rest, (part + 1) * rest), rest, step)
+            for h in range(parts * heads):
+                value = dots[h]
+                high = value.astype(jnp.bfloat16).astype(jnp.float32)
+                middle = (value - high).astype(jnp.bfloat16).astype(jnp.float32)
+                low = (value - high - middle).astype(jnp.bfloat16).astype(jnp.float32)
+                spread = high + pltpu.roll(middle, PIECE, 1) + pltpu.roll(low, 2 * PIECE, 1)
+                dots_out[h, 0] = spread.astype(jnp.bfloat16)
+            dots_copy = pltpu.make_async_copy(
+                dots_out, out_ref.at[:, pl.ds(ahead + 2 * step, 1)], out_sems.at[2]
+            )
+            dots_copy.start()
             for copy in kv_copies:
                 copy.wait()
-        pltpu.make_async_copy(g_buf, g_buf, out_sems.at[1]).wait()
-        pltpu.make_async_copy(q_buf, q_buf, out_sems.at[0]).wait()
-        dots_copy.wait()
-
-    in_specs = [pl.BlockSpec(memory_space=pl.ANY)] * 3
-    args = [query, out_grad, forward_out]
-    scratch = [pltpu.VMEM((count, toks, width), jnp.bfloat16)] * 3
-    scratch.append(pltpu.VMEM((parts * heads, toks, HD), jnp.float32))
-    scratch.append(pltpu.VMEM((parts * heads, 1, toks, HD), jnp.bfloat16))
+        for which in (1, 0):
+            pltpu.make_async_copy(bufs[which], bufs[which], out_sems.at[which]).wait()
+        if kv:
+            dots_copy.wait()
+
+    args = [query, out_grad] + ([forward_out] if kv else [])
+    in_specs = [pl.BlockSpec(memory_space=pl.ANY)] * len(args)
+    scratch = [pltpu.VMEM((count, toks, width), jnp.bfloat16)] * len(args)
     if kv:
         in_specs += [pl.BlockSpec(x.shape, lambda i: (0, 0, 0)) for x in kv]
         args += list(kv)
-        scratch.append(pltpu.VMEM((heads, 2 * blocks, toks, HD), jnp.bfloat16))
-    scratch += [pltpu.SemaphoreType.DMA((3, parts)), pltpu.SemaphoreType.DMA((3 + parts,))]
+        scratch += [pltpu.VMEM((rest * parts, toks, width), jnp.bfloat16)] * 2
+        scratch.append(pltpu.VMEM((parts * heads, toks, HD), jnp.float32))
+        scratch.append(pltpu.VMEM((parts * heads, 1, toks, HD), jnp.bfloat16))
+        scratch.append(pltpu.VMEM((heads, ahead, toks, HD), jnp.bfloat16))
+    scratch += [pltpu.SemaphoreType.DMA((5, parts)), pltpu.SemaphoreType.DMA((3 + parts,))]
     return pl.pallas_call(
         body,
         name=f"pack{first}",
@@ -151,10 +167,12 @@
     total = groups * blocks
     steps = groups * count
     last = sums is not None
-    ahead = slots - 2 * count - 1
+    ahead = 0 if last else 2 * blocks
+    behind = source.shape[1] - 1
+    before = first // groups
     extra = 2 * blocks if last else 0
 
-    def body(pair_ref, group_ref, m_ref, kv_ref, *refs):
+    def body(pair_ref, group_ref, m_ref, kv_ref, dots_ref, *refs):
         if last:
             sum_ref, out_ref = refs[:2]
             refs, (key_acc, value_acc) = refs[2:-2], refs[-2:]
@@ -176,7 +194,7 @@
         lane = lax.broadcasted_iota(jnp.int32, (PIECE, HD), 1)
         picks = jnp.where((lane % PIECE == row) & (lane < 3 * PIECE), 1.0, 0.0).astype(jnp.bfloat16)
         for g in range(groups):
-            tile = m_ref[g * srcs : (g + 1) * srcs, ahead + 2 * count].reshape(length, HD)
+            tile = dots_ref[g * srcs : (g + 1) * srcs, 0].reshape(length, HD)
             dots[g * PIECE : (g + 1) * PIECE] = nt(picks, tile)
         if last:
             key_acc[...] = sum_ref[0]
@@ -220,7 +238,7 @@
                 norm = part if norm is None else norm + part
             inverse = 1.0 / jnp.sum(norm, axis=0, keepdims=True)
             group, at = where(c)
-            dot_row = dots[pl.ds(group * PIECE + at, 1), :]
+            dot_row = dots[pl.ds(group * PIECE + before + at, 1), :]
             for j, rows in cuts:
                 prob = score[j, rows] * inverse
                 probs[slot][j, rows] = prob.astype(jnp.bfloat16)
@@ -279,8 +297,9 @@
     scratch += [pltpu.VMEM((2, length, length), jnp.float32)] * (2 * SLOTS)
     scratch += [pltpu.VMEM((2, length, length), jnp.bfloat16)] * (2 * SLOTS)
     scratch += [pltpu.VMEM((length, HD), jnp.bfloat16)] * (2 * SLOTS)
-    in_specs = [whole(message.shape), whole((devices, 2 * blocks, toks, HD))]
-    args = [message, source]
+    dots_spec = pl.BlockSpec((devices, 1, toks, HD), lambda i, p, g: (0, behind, 0, 0))
+    in_specs = [whole(message.shape), whole((devices, 2 * blocks, toks, HD)), dots_spec]
+    args = [message, source, source]
     if last:
         in_specs[0], args[0] = HELD, held(message)
         in_specs.append(whole(acc))
@@ -373,9 +392,9 @@
     pairs = pairing.reshape(-1)
     group = lax.axis_index("grp").reshape(1)
     codes = (key_codes, key_scale, value_codes, value_scale)
-    got0 = exchange(pack(query, out_grad, forward_out, 0, large, groups, codes))
-    later, pairs, group = lax.optimization_barrier((forward_out, pairs, group))
-    got1 = exchange(pack(query, out_grad, later, large, small, groups))
+    got0 = exchange(pack(query, out_grad, 0, large, groups, forward_out, codes))
+    later, pairs, group = lax.optimization_barrier((out_grad, pairs, group))
+    got1 = exchange(pack(query, later, large, small, groups))
     pairs = (pairs, group)
     first, second = large // groups, small // groups
     grads0, sums = attend(pairs, got0, got0, 0, per, first, groups, blocks)

time: 156 us -> 156 us (level)
  no operation moved by 1% of the time
where the time goes in v7:
time: 156 us; the launch traced here: 155 us
  waiting for transfers between devices  85.5 us (55%)
  Pallas kernels  40.7 us (26%)
  starting transfers between devices  27.4 us (18%)
    all_to_all x4, waiting for transfers between devices, exchange(): lax.all_to_all(message, ('grp', 'head'), split_axis=0, concat_axis=0, til...  85.5 us
    pallas_call x2, Pallas kernels, attend(): pl.pallas_call(body, name=f'attend{first}', grid_spec=pltpu.PrefetchScala...  28.4 us
    all_to_all x4, starting transfers between devices, exchange(): lax.all_to_all(message, ('grp', 'head'), split_axis=0, concat_axis=0, til...  27.4 us
    pallas_call x2, Pallas kernels, pack(): pl.pallas_call(body, name=f'pack{first}', grid=(1,), in_specs=in_specs, o...  9.1 us
    pallas_call x2, Pallas kernels, unpack(): pl.pallas_call(body, name=f'unpack{first}', grid=(groups * per,), in_spec...  3.21 us
  transfers between devices with their start and end apart: 4, of which 4 were waited for; matrix products, arithmetic and copies ran while one was open for 1% of the time, Pallas kernels for 21%

profile of v7, /device:TPU:1, one launch (start us, length us, event | category | flops | bytes accessed | tf_op | source)
XLA Modules:
  0.0 155.1 jit_solution(10750421489762604413)
XLA Ops:
  0.6 6.3 %pack0.1 = bf16[128,29,4,128]{3,2,1,0:T(4,128)(2,1)} custom-call(bf16[36,4,8192]{2,1,0:T(4,128)(2,1)} %refs_0_.3, bf16[36,4,8192]{2,1,0:T(4,128)(2,1)} %refs_1_.2, bf16[36,4,8192]{2,1,0:T(4,128)(2,1)} %refs_2_.1, bf16[2,4,8192]{2,1,0:T(4,128)(2,1)} %refs_3_.1, bf16[2,4,64]{2,1,0:T(4,128)(2,1)} %refs_4_.1, bf16[2,4,8192]{2,1,0:T(4,128)(2,1)} %refs_5_.1, ...), custom_call_target="tpu_custom_call" | custom-call | tf_op jit(solution)/shard_map/pack0/pallas_call | solution.py:143
  7.0 0.0 copy-start
  7.0 11.9 %all-to-all-start.1 = ((bf16[128,29,4,128]{3,2,1,0:T(4,128)(2,1)}), bf16[128,29,4,128]{3,2,1,0:T(4,128)(2,1)}, u32[]{:S(2)}, u32[]{:S(2)}) async-start(bf16[128,29,4,128]{3,2,1,0:T(4,128)(2,1)} %pack0.1), calls=%async_computation.1 | async-start | bytes 7602176 | tf_op jit(solution)/shard_map/all_to_all | solution.py:381
  18.9 0.0 copy-done
  18.9 0.1 copy.12
  19.0 0.7 reshape.12.pair_ref
  19.7 2.8 %pack24.1 = bf16[128,12,4,128]{3,2,1,0:T(4,128)(2,1)} custom-call(bf16[36,4,8192]{2,1,0:T(4,128)(2,1)} %refs_0_.3, bf16[36,4,8192]{2,1,0:T(4,128)(2,1)} %refs_1_.2), custom_call_target="tpu_custom_call" | custom-call | tf_op jit(solution)/shard_map/pack24/pallas_call | solution.py:143
  22.5 44.7 %all-to-all-done.1.m_ref.kv_ref.dots_ref = bf16[128,29,4,128]{3,2,1,0:T(4,128)(2,1)} async-done(((bf16[128,29,4,128]{3,2,1,0:T(4,128)(2,1)}), bf16[128,29,4,128]{3,2,1,0:T(4,128)(2,1)}, u32[]{:S(2)}, u32[]{:S(2)}) %all-to-all-start.1) | async-done | bytes 3801120 | tf_op jit(solution)/shard_map/all_to_all | solution.py:381
  67.1 6.0 %all-to-all-start = ((bf16[128,12,4,128]{3,2,1,0:T(4,128)(2,1)}), bf16[128,12,4,128]{3,2,1,0:T(4,128)(2,1)S(1)}, u32[]{:S(2)}, u32[]{:S(2)}) async-start(bf16[128,12,4,128]{3,2,1,0:T(4,128)(2,1)} %pack24.1), calls=%async_computation | async-start | bytes 3145728 | tf_op jit(solution)/shard_map/all_to_all | solution.py:381
  73.1 17.8 %attend0.1 = (bf16[128,12,4,128]{3,2,1,0:T(4,128)(2,1)}, f32[2,4,256,128]{3,2,1,0:T(8,128)}) custom-call(s32[144]{0:T(256)} %reshape.12.pair_ref, s32[1]{0:T(128)} %bitcast.group_ref, bf16[128,29,4,128]{3,2,1,0:T(4,128)(2,1)} %all-to-all-done.1.m_ref.kv_ref.dots_ref, bf16[128,29,4,128]{3,2,1,0:T(4,128)(2,1)} %all-to-all-done.1.m_ref.kv_ref.dots_ref, ...), custom_call_target="tpu_custom_call" | custom-call | flops 4026531840 | bytes 6291456 | tf_op jit(solution)/shard_map/attend0/pallas_call | solution.py:313
  90.9 6.7 %all-to-all-done.m_ref = bf16[128,12,4,128]{3,2,1,0:T(4,128)(2,1)S(1)} async-done(((bf16[128,12,4,128]{3,2,1,0:T(4,128)(2,1)}), bf16[128,12,4,128]{3,2,1,0:T(4,128)(2,1)S(1)}, u32[]{:S(2)}, u32[]{:S(2)}) %all-to-all-start) | async-done | bytes 1572896 | tf_op jit(solution)/shard_map/all_to_all | solution.py:381
  97.7 4.8 %all-to-all-start.3 = ((bf16[128,12,4,128]{3,2,1,0:T(4,128)(2,1)}), bf16[128,12,4,128]{3,2,1,0:T(4,128)(2,1)S(1)}, u32[]{:S(2)}, u32[]{:S(2)}) async-start(bf16[128,12,4,128]{3,2,1,0:T(4,128)(2,1)} %get-tuple-element.12), calls=%async_computation.3 | async-start | bytes 3145728 | tf_op jit(solution)/shard_map/all_to_all | solution.py:381
  102.5 10.6 %attend24.1 = bf16[128,10,4,128]{3,2,1,0:T(4,128)(2,1)} custom-call(s32[144]{0:T(256)} %reshape.12.pair_ref, s32[1]{0:T(128)} %bitcast.group_ref, bf16[128,12,4,128]{3,2,1,0:T(4,128)(2,1)S(1)} %all-to-all-done.m_ref, bf16[128,29,4,128]{3,2,1,0:T(4,128)(2,1)} %all-to-all-done.1.m_ref.kv_ref.dots_ref, ...), custom_call_target="tpu_custom_call" | custom-call | flops 2013265920 | bytes 6291456 | tf_op jit(solution)/shard_map/attend24/pallas_call | solution.py:313
  113.0 14.1 %all-to-all-done.3.m_ref = bf16[128,12,4,128]{3,2,1,0:T(4,128)(2,1)S(1)} async-done(((bf16[128,12,4,128]{3,2,1,0:T(4,128)(2,1)}), bf16[128,12,4,128]{3,2,1,0:T(4,128)(2,1)S(1)}, u32[]{:S(2)}, u32[]{:S(2)}) %all-to-all-start.3) | async-done | bytes 1572896 | tf_op jit(solution)/shard_map/all_to_all | solution.py:381
  127.1 4.8 %all-to-all-start.2 = ((bf16[128,10,4,128]{3,2,1,0:T(4,128)(2,1)}), bf16[128,10,4,128]{3,2,1,0:T(4,128)(2,1)S(1)}, u32[]{:S(2)}, u32[]{:S(2)}) async-start(bf16[128,10,4,128]{3,2,1,0:T(4,128)(2,1)} %attend24.1), calls=%async_computation.2 | async-start | bytes 2621440 | tf_op jit(solution)/shard_map/all_to_all | solution.py:381
  131.9 1.9 %unpack0.1.refs_0_ = bf16[36,4,8192]{2,1,0:T(4,128)(2,1)} custom-call(bf16[128,12,4,128]{3,2,1,0:T(4,128)(2,1)S(1)} %all-to-all-done.3.m_ref), custom_call_target="tpu_custom_call" | custom-call | tf_op jit(solution)/shard_map/unpack0/pallas_call | solution.py:368
  133.9 19.9 %all-to-all-done.2.m_ref = bf16[128,10,4,128]{3,2,1,0:T(4,128)(2,1)S(1)} async-done(((bf16[128,10,4,128]{3,2,1,0:T(4,128)(2,1)}), bf16[128,10,4,128]{3,2,1,0:T(4,128)(2,1)S(1)}, u32[]{:S(2)}, u32[]{:S(2)}) %all-to-all-start.2) | async-done | bytes 1310752 | tf_op jit(solution)/shard_map/all_to_all | solution.py:381
  153.8 1.3 unpack24.1
Async XLA Ops:
  7.0 11.9 %copy-start = (s32[72,2]{0,1:T(2,128)S(1)}, s32[72,2]{0,1:T(2,128)}, u32[]{:S(2)}) copy-start(s32[72,2]{0,1:T(2,128)} %param.15) | copy-start | bytes 1732
  7.0 60.2 %all-to-all-start.1 = ((bf16[128,29,4,128]{3,2,1,0:T(4,128)(2,1)}), bf16[128,29,4,128]{3,2,1,0:T(4,128)(2,1)}, u32[]{:S(2)}, u32[]{:S(2)}) async-start(bf16[128,29,4,128]{3,2,1,0:T(4,128)(2,1)} %pack0.1), calls=%async_computation.1 | async-start | bytes 7602176 | tf_op jit(solution)/shard_map/all_to_all | solution.py:381
  67.1 30.5 %all-to-all-start = ((bf16[128,12,4,128]{3,2,1,0:T(4,128)(2,1)}), bf16[128,12,4,128]{3,2,1,0:T(4,128)(2,1)S(1)}, u32[]{:S(2)}, u32[]{:S(2)}) async-start(bf16[128,12,4,128]{3,2,1,0:T(4,128)(2,1)} %pack24.1), calls=%async_computation | async-start | bytes 3145728 | tf_op jit(solution)/shard_map/all_to_all | solution.py:381
  97.7 29.5 %all-to-all-start.3 = ((bf16[128,12,4,128]{3,2,1,0:T(4,128)(2,1)}), bf16[128,12,4,128]{3,2,1,0:T(4,128)(2,1)S(1)}, u32[]{:S(2)}, u32[]{:S(2)}) async-start(bf16[128,12,4,128]{3,2,1,0:T(4,128)(2,1)} %get-tuple-element.12), calls=%async_computation.3 | async-start | bytes 3145728 | tf_op jit(solution)/shard_map/all_to_all | solution.py:381
  127.1 26.7 %all-to-all-start.2 = ((bf16[128,10,4,128]{3,2,1,0:T(4,128)(2,1)}), bf16[128,10,4,128]{3,2,1,0:T(4,128)(2,1)S(1)}, u32[]{:S(2)}, u32[]{:S(2)}) async-start(bf16[128,10,4,128]{3,2,1,0:T(4,128)(2,1)} %attend24.1), calls=%async_computation.2 | async-start | bytes 2621440 | tf_op jit(solution)/shard_map/all_to_all | solution.py:381
